TPU v7x, 128 devices: a whole 4x4x4 slice. The times are simulated.
128 devices in a mesh: tm: 16 (over x_hi, z, core), space: 8 (over x_lo, y).
Axes of the slice: x: 4 (x_hi: 2, x_lo: 2; x = x_hi * 2 + x_lo), y: 4, z: 4, core: 2. Of those that a mesh axis runs over, the one named last changes fastest.
Arguments:
- velocity: float32 [256, 3, 48, 2304], P('tm', None, 'space'), may hold values from -2.4 to 2.4
- period: float32 [1], replicated, may hold values from 40 to 80
- wavenumber: int32 [1], replicated, may hold values from 1 to 23
Outputs:
- new_field: float32 [256, 3, 48, 2304], P('tm', None, 'space')
- residual: float32 [256, 3, 48, 2304], P('tm', None, 'space')
- period_grad: float32 [1], replicated
All inputs are finite; a program needn't handle non-finite values.
Results may differ from a plain program's by a relative error of at most 0.0003.
Values sent between devices are 32-bit elements; how exact they have to be, the bound alone decides.
No kernel may reach another device: no remote copies, remote signals or barrier semaphores. Data moves between devices by JAX's collectives and lax.ppermute only.
A program may use at most 128 MiB of HBM per device.

v0:
```python
import functools
import math

import jax
import jax.numpy as jnp
from jax import lax
from jax.sharding import Mesh
from jax.sharding import PartitionSpec as P

NY = 48
NZ = 48
TM = ("tm_0", "tm_1", "tm_2")
SPACE = ("space_0", "space_1")
TM_SPACE = ("tm_0", "tm_1", "tm_2", "space_0", "space_1")


weights = (0.8, -0.2, 4.0 / 105.0, -1.0 / 280.0)
viscosity = 0.02
step_size = 0.15


def padded_2(array, sides, width):
    for axis, dim in sides:
        count, length = (lax.axis_size(axis), array.shape[dim])
        up = [(i, (i + 1) % count) for i in range(count)]
        down = [(j, i) for i, j in up]
        last = lax.slice_in_dim(array, length - width, length, axis=dim)
        leading = lax.slice_in_dim(array, 0, width, axis=dim)
        before = lax.ppermute(last, axis, up)
        after = lax.ppermute(leading, axis, down)
        array = jnp.concatenate([before, array, after], axis=dim)
    return array


def over_axes(array, axes):
    return functools.reduce(lax.psum, axes, array)


def rate_in_time(values, inverse_step):
    out_levels = values.shape[0] - 8
    summed = jnp.zeros((out_levels,) + values.shape[1:], jnp.float32)
    for offset, weight in enumerate(weights, 1):
        summed = summed + weight * (
            values[4 + offset : 4 + offset + out_levels]
            - values[4 - offset : 4 - offset + out_levels]
        )
    return summed * inverse_step


def along_first(values, spacing):
    return (values[:, :, 2:] - values[:, :, :-2]) / (2.0 * spacing)


def next_y(values):
    return jnp.roll(values, -NZ, 3)


def prev_y(values):
    return jnp.roll(values, NZ, 3)


def column_index():
    return lax.broadcasted_iota(jnp.int32, (1, 1, 1, NY * NZ), 3) % NZ


def next_z(values):
    return jnp.where(column_index() == NZ - 1, jnp.roll(values, NZ - 1, 3), jnp.roll(values, -1, 3))


def prev_z(values):
    return jnp.where(column_index() == 0, jnp.roll(values, 1 - NZ, 3), jnp.roll(values, 1, 3))


def along_y(values, spacing):
    return (next_y(values) - prev_y(values)) / (2.0 * spacing)


def along_z(values, spacing):
    return (next_z(values) - prev_z(values)) / (2.0 * spacing)


def laplace(padded, spacings):
    center = padded[:, :, 1:-1]
    result = (padded[:, :, 2:] + padded[:, :, :-2] - 2.0 * center) / spacings[0] ** 2
    result = result + (next_y(center) + prev_y(center) - 2.0 * center) / spacings[1] ** 2
    result = result + (next_z(center) + prev_z(center) - 2.0 * center) / spacings[2] ** 2
    return result


def forcing_term(wavenumber):
    row_index = jnp.arange(NY, dtype=jnp.float32)
    profile = jnp.sin(wavenumber[0].astype(jnp.float32) * (2.0 * math.pi / NY) * row_index)
    profile = jnp.repeat(profile, NZ)
    return jnp.stack([profile, 0.0 * profile, 0.0 * profile]).reshape(1, 3, 1, NY * NZ)


def residual_parts(flow_levels, flow_slabs, inverse_step, spacings, forcing):
    level_rate = rate_in_time(flow_levels, inverse_step)
    center = flow_slabs[:, :, 1:-1]
    gradients = (
        along_first(flow_slabs, spacings[0]),
        along_y(center, spacings[1]),
        along_z(center, spacings[2]),
    )
    advect = (
        center[:, 0:1] * gradients[0]
        + center[:, 1:2] * gradients[1]
        + center[:, 2:3] * gradients[2]
    )
    residue = level_rate + advect - viscosity * laplace(flow_slabs, spacings) - forcing
    return (residue, level_rate, gradients)


def descent_direction(residue_levels, residue_slabs, flow_near, gradients, inverse_step, spacings):
    residue_center = residue_slabs[:, :, 1:-1]
    flow_center = flow_near[:, :, 1:-1]
    result = -rate_in_time(residue_levels, inverse_step)
    result = result - along_first(flow_near[:, 0:1] * residue_slabs, spacings[0])
    result = result - along_y(flow_center[:, 1:2] * residue_center, spacings[1])
    result = result - along_z(flow_center[:, 2:3] * residue_center, spacings[2])
    result = result + jnp.stack(
        [jnp.sum(residue_center * gradient, axis=1) for gradient in gradients], axis=1
    )
    result = result - viscosity * laplace(residue_slabs, spacings)
    return result


def on_device(velocity, period, wavenumber):
    slab_cells = velocity.shape[2]
    total_levels = velocity.shape[0] * lax.axis_size(TM)
    grid_first = slab_cells * lax.axis_size(SPACE)
    inverse_step = total_levels / period[0]
    spacings = (2.0 * math.pi / grid_first, 2.0 * math.pi / NY, 2.0 * math.pi / NZ)
    forcing = forcing_term(wavenumber)
    flow_levels = padded_2(velocity, ((TM, 0),), 4)
    flow_slabs = padded_2(velocity, ((SPACE, 2),), 1)
    residue, level_rate, gradients = residual_parts(
        flow_levels, flow_slabs, inverse_step, spacings, forcing
    )
    residue_levels = padded_2(residue, ((TM, 0),), 4)
    residue_slabs = padded_2(residue, ((SPACE, 2),), 1)
    orbit_totals = (
        over_axes(jnp.sum(residue * level_rate), TM_SPACE),
        over_axes(jnp.sum(level_rate * level_rate), TM_SPACE),
    )
    descent = descent_direction(
        residue_levels, residue_slabs, flow_slabs, gradients, inverse_step, spacings
    )
    descent_total = over_axes(jnp.sum(descent * level_rate), TM_SPACE)
    totals = (orbit_totals[0], orbit_totals[1], descent_total)
    shift_weight = totals[2] / totals[1]
    updated = velocity - step_size * (descent - shift_weight * level_rate)
    cell_count = 3.0 * total_levels * grid_first * NY * NZ
    period_grad = (-totals[0] / (period[0] * cell_count)).reshape(1)
    return (updated, residue, period_grad)


def solution(mesh):
    split = Mesh(
        mesh.devices.reshape(2, 4, 2, 2, 4), ("tm_0", "tm_1", "tm_2", "space_0", "space_1")
    )
    in_specs = (P(TM, None, SPACE, None), P(), P())
    out_specs = (P(TM, None, SPACE, None), P(TM, None, SPACE, None), P())
    return jax.shard_map(
        on_device, mesh=split, in_specs=in_specs, out_specs=out_specs, check_vma=False
    )
```

profile of v0, /device:TPU:40, one launch (start us, length us, event | category | flops | bytes accessed | tf_op | source)
XLA Modules:
  0.0 218.4 jit_solution(8474762105391625208)
XLA Ops:
  0.6 3.5 %copy.71 = f32[16,3,6,2304]{3,2,1,0:T(8,128)S(1)} copy(f32[16,3,6,2304]{3,0,2,1:T(8,128)} %param.3) | data formatting | bytes 5308416 | tf_op args[0]
  5.5 1.7 collective-permute-start
  10.4 4.0 %fusion.70 = (f32[16,3,6,2256]{3,2,1,0:T(8,128)}, f32[16,3,6,2256]{3,2,1,0:T(8,128)}) fusion(f32[16,3,6,2304]{3,2,1,0:T(8,128)S(1)} %copy.71), kind=kLoop, calls=%fused_computation.128 | loop fusion | bytes 10395648 | tf_op jit(solution)/shard_map/jit(_roll_static)/slice | solution.py:55
  14.4 4.0 %fusion.73 = (f32[16,3,6,2257]{3,2,1,0:T(8,128)}, f32[16,3,6,2257]{3,2,1,0:T(8,128)}) fusion(f32[16,3,6,2304]{3,2,1,0:T(8,128)S(1)} %copy.71), kind=kLoop, calls=%fused_computation.131 | loop fusion | bytes 10400256 | tf_op jit(solution)/shard_map/jit(_roll_static)/slice | solution.py:67
  18.4 4.1 %fusion.74 = (f32[16,3,6,2303]{3,2,1,0:T(8,128)}, f32[16,3,6,2303]{3,2,1,0:T(8,128)}) fusion(f32[16,3,6,2304]{3,2,1,0:T(8,128)S(1)} %copy.71), kind=kLoop, calls=%fused_computation.132 | loop fusion | bytes 10612224 | tf_op jit(solution)/shard_map/jit(_roll_static)/slice | solution.py:67
  29.4 2.8 %copy.46 = f32[16,6,2304]{2,1,0:T(8,128)} copy(f32[16,6,2304]{2,0,1:T(8,128)} %get-tuple-element.78) | data formatting | bytes 1769472 | tf_op jit(solution)/shard_map/mul | solution.py:106
  44.2 2.2 %copy.44 = f32[16,3,1,2304]{3,2,1,0:T(1,128)} copy(f32[16,3,1,2304]{3,0,2,1:T(8,128)} %collective-permute-done.3) | data formatting | bytes 884736 | tf_op jit(solution)/shard_map/ppermute | solution.py:29
  49.3 1.9 constant_dynamic-update-slice_fusion
  51.3 20.0 %multiply_reduce_fusion.5 = (f32[16,6,2304]{2,1,0:T(8,128)}, f32[16,6,2304]{2,1,0:T(8,128)}, f32[16,6,2304]{2,1,0:T(8,128)}, f32[16,3,6,2304]{3,2,1,0:T(8,128)S(1)}, f32[16,3,6,2304]{3,2,1,0:T(8,128)}) fusion(f32[16,3,1,2304]{3,2,1,0:T(1,128)S(1)} %copy.43, f32[16,3,6,2304]{3,2,1,0:T(8,128)S(1)} %copy.71, f32[16,3,1,2304]{3,2,1,0:T(1,128)} %copy.44, ...), kind=kLoop, calls=%fused_computation.86 | loop fusion | flops 33841152 | bytes 51346948 | tf_op jit(solution)/shard_map/reduce_sum | solution.py:122
  73.6 4.1 %fusion.60 = (f32[16,3,6,2303]{3,2,1,0:T(8,128)}, f32[16,3,6,2303]{3,2,1,0:T(8,128)}) fusion(f32[16,3,6,2304]{3,2,1,0:T(8,128)S(1)} %get-tuple-element.40), kind=kLoop, calls=%fused_computation.118 | loop fusion | bytes 10612224 | tf_op jit(solution)/shard_map/jit(_roll_static)/slice | solution.py:67
  78.6 3.9 %fusion.56 = (f32[16,3,6,2256]{3,2,1,0:T(8,128)}, f32[16,3,6,2256]{3,2,1,0:T(8,128)}) fusion(f32[16,3,6,2304]{3,2,1,0:T(8,128)S(1)} %get-tuple-element.39), kind=kLoop, calls=%fused_computation.114 | loop fusion | bytes 10395648 | tf_op jit(solution)/shard_map/jit(_roll_static)/slice | solution.py:55
  83.3 4.1 %fusion.63 = (f32[16,3,6,2256]{3,2,1,0:T(8,128)}, f32[16,3,6,2256]{3,2,1,0:T(8,128)}) fusion(f32[16,3,6,2304]{3,2,1,0:T(8,128)S(1)} %get-tuple-element.31), kind=kLoop, calls=%fused_computation.121 | loop fusion | bytes 10395648 | tf_op jit(solution)/shard_map/jit(_roll_static)/slice | solution.py:55
  87.4 4.0 %fusion.66 = (f32[16,3,6,2257]{3,2,1,0:T(8,128)}, f32[16,3,6,2257]{3,2,1,0:T(8,128)}) fusion(f32[16,3,6,2304]{3,2,1,0:T(8,128)S(1)} %get-tuple-element.31), kind=kLoop, calls=%fused_computation.124 | loop fusion | bytes 10400256 | tf_op jit(solution)/shard_map/jit(_roll_static)/slice | solution.py:67
  91.3 4.0 %fusion.67 = (f32[16,3,6,2303]{3,2,1,0:T(8,128)}, f32[16,3,6,2303]{3,2,1,0:T(8,128)}) fusion(f32[16,3,6,2304]{3,2,1,0:T(8,128)S(1)} %get-tuple-element.31), kind=kLoop, calls=%fused_computation.125 | loop fusion | bytes 10612224 | tf_op jit(solution)/shard_map/jit(_roll_static)/slice | solution.py:67
  96.3 2.3 %copy.73 = f32[16,3,6,2304]{3,0,2,1:T(8,128)} copy(f32[16,3,6,2304]{3,2,1,0:T(8,128)S(1)} %get-tuple-element.31) | data formatting | bytes 5308416
  103.5 7.9 %collective-permute-done.6 = f32[16,3,1,2304]{3,0,2,1:T(8,128)S(1)} collective-permute-done((f32[16,3,1,2304]{3,0,2,1:T(8,128)S(1)}, f32[16,3,1,2304]{3,0,2,1:T(8,128)S(1)}, u32[]{:S(2)}, u32[]{:S(2)}) %collective-permute-start.6) | collective-permute-done | bytes 442400 | tf_op jit(solution)/shard_map/ppermute | solution.py:29
  117.1 44.7 %multiply_reduce_fusion = (f32[]{:T(128)}, f32[]{:T(128)}, f32[]{:T(128)}, f32[16,3,6,2304]{3,2,1,0:T(8,128)}) fusion(f32[16,3,6,2304]{3,2,1,0:T(8,128)S(1)} %get-tuple-element.31, f32[16,3,6,2304]{3,2,1,0:T(8,128)S(1)} %copy-done.4, f32[16,3,6,2303]{3,2,1,0:T(8,128)} %get-tuple-element.60, f32[16,3,6,1]{3,2,1,0:T(8,128)} %get-tuple-element.62, ...), kind=kLoop, calls=%fused_computation.80 | loop fusion | flops 45121536 | bytes 49992208 | tf_op jit(solution)/shard_map/reduce_sum | solution.py:143
  161.8 7.1 %all-reduce.4 = (f32[]{:T(128)}, f32[]{:T(128)}, f32[]{:T(128)}) all-reduce(f32[]{:T(128)} %get-tuple-element.11, f32[]{:T(128)} %get-tuple-element.10, f32[]{:T(128)} %get-tuple-element.9), channel_id=1, replica_groups=mesh['tm_0'=2,'tm_1'=4,'tm_2'=2,'space_0'=2,'space_1'=4] {'tm_0'}, use_global_device_ids=true, to_apply=%region_4.5 | all-reduce | flops 3 | bytes 24 | tf_op jit(solution)/shard_map/psum | solution.py:36
  168.9 13.9 %all-reduce.1 = (f32[]{:T(128)}, f32[]{:T(128)}, f32[]{:T(128)}) all-reduce(f32[]{:T(128)} %get-tuple-element.27, f32[]{:T(128)} %get-tuple-element.28, f32[]{:T(128)} %get-tuple-element.29), channel_id=1, replica_groups=mesh['tm_0'=2,'tm_1'=4,'tm_2'=2,'space_0'=2,'space_1'=4] {'tm_1'}, use_global_device_ids=true, to_apply=%region_5.6 | all-reduce | flops 3 | bytes 24 | tf_op jit(solution)/shard_map/psum | solution.py:36
  182.7 3.1 %all-reduce.3 = (f32[]{:T(128)}, f32[]{:T(128)}, f32[]{:T(128)}) all-reduce(f32[]{:T(128)} %get-tuple-element.18, f32[]{:T(128)} %get-tuple-element.19, f32[]{:T(128)} %get-tuple-element.20), channel_id=1, replica_groups=mesh['tm_0'=2,'tm_1'=4,'tm_2'=2,'space_0'=2,'space_1'=4] {'tm_2'}, use_global_device_ids=true, to_apply=%region_6.7 | all-reduce | flops 3 | bytes 24 | tf_op jit(solution)/shard_map/psum | solution.py:36
  185.8 5.6 %all-reduce.2 = (f32[]{:T(128)}, f32[]{:T(128)}, f32[]{:T(128)}) all-reduce(f32[]{:T(128)} %get-tuple-element.24, f32[]{:T(128)} %get-tuple-element.25, f32[]{:T(128)} %get-tuple-element.26), channel_id=1, replica_groups=mesh['tm_0'=2,'tm_1'=4,'tm_2'=2,'space_0'=2,'space_1'=4] {'space_0'}, use_global_device_ids=true, to_apply=%region_7.8 | all-reduce | flops 3 | bytes 24 | tf_op jit(solution)/shard_map/psum | solution.py:36
  191.4 16.0 %all-reduce = (f32[]{:T(128)}, f32[]{:T(128)}, f32[]{:T(128)}) all-reduce(f32[]{:T(128)} %get-tuple-element.21, f32[]{:T(128)} %get-tuple-element.22, f32[]{:T(128)} %get-tuple-element.23), channel_id=1, replica_groups=mesh['tm_0'=2,'tm_1'=4,'tm_2'=2,'space_0'=2,'space_1'=4] {'space_1'}, use_global_device_ids=true, to_apply=%region_8.9 | all-reduce | flops 3 | bytes 24 | tf_op jit(solution)/shard_map/psum | solution.py:36
  208.8 5.1 %multiply_subtract_fusion.2 = f32[16,3,6,2304]{3,2,1,0:T(8,128)S(1)} fusion(f32[16,3,6,2304]{3,2,1,0:T(8,128)} %get-tuple-element.30, f32[16,3,6,2304]{3,2,1,0:T(8,128)} %get-tuple-element.32, f32[]{:T(128)S(6)} %div.62, f32[16,3,6,2304]{3,0,2,1:T(8,128)S(1)} %copy-done.2), kind=kLoop, calls=%fused_computation.81 | loop fusion | flops 2654208 | bytes 10616836 | tf_op jit(solution)/shard_map/sub | solution.py:152
  213.9 2.3 %copy.72 = f32[16,3,6,2304]{3,0,2,1:T(8,128)} copy(f32[16,3,6,2304]{3,2,1,0:T(8,128)S(1)} %multiply_subtract_fusion.2) | data formatting | bytes 5308416
  (81 shorter events, 40.4 us)
Async XLA Ops:
  0.6 6.6 %copy-start = (f32[16,3,6,2304]{3,0,2,1:T(8,128)S(1)}, f32[16,3,6,2304]{3,0,2,1:T(8,128)}, u32[]{:S(2)}) copy-start(f32[16,3,6,2304]{3,0,2,1:T(8,128)} %param.3) | copy-start | bytes 7962628
  5.5 41.0 %collective-permute-start.1 = (f32[4,3,6,2304]{3,2,1,0:T(8,128)}, f32[4,3,6,2304]{3,2,1,0:T(8,128)}, u32[]{:S(2)}, u32[]{:S(2)}) collective-permute-start(f32[4,3,6,2304]{3,2,1,0:T(8,128)} %get-tuple-element.64), channel_id=1, source_target_pairs={{0,8},{8,16},{16,24},{24,32},{32,40},{40,48},{48,56},{56,64},{64,7... | collective-permute-start | bytes 1990664 | tf_op jit(solution)/shard_map/ppermute | solution.py:29
  5.5 43.8 %collective-permute-start = (f32[4,3,6,2304]{3,2,1,0:T(8,128)}, f32[4,3,6,2304]{3,2,1,0:T(8,128)}, u32[]{:S(2)}, u32[]{:S(2)}) collective-permute-start(f32[4,3,6,2304]{3,2,1,0:T(8,128)} %get-tuple-element.63), channel_id=1, source_target_pairs={{8,0},{16,8},{24,16},{32,24},{40,32},{48,40},{56,48},{64,56},{72,6... | collective-permute-start | bytes 1990664 | tf_op jit(solution)/shard_map/ppermute | solution.py:30
  8.2 31.7 %collective-permute-start.2 = (f32[16,3,1,2304]{3,0,2,1:T(8,128)}, f32[16,3,1,2304]{3,0,2,1:T(8,128)}, u32[]{:S(2)}, u32[]{:S(2)}) collective-permute-start(f32[16,3,1,2304]{3,0,2,1:T(8,128)} %get-tuple-element.85), channel_id=1, source_target_pairs={{1,0},{2,1},{3,2},{4,3},{5,4},{6,5},{7,6},{0,7},{9,8},{10,9},{11,1... | collective-permute-start | bytes 1327112 | tf_op jit(solution)/shard_map/ppermute | solution.py:30
  8.7 31.3 %collective-permute-start.3 = (f32[16,3,1,2304]{3,0,2,1:T(8,128)}, f32[16,3,1,2304]{3,0,2,1:T(8,128)}, u32[]{:S(2)}, u32[]{:S(2)}) collective-permute-start(f32[16,3,1,2304]{3,0,2,1:T(8,128)} %get-tuple-element.84), channel_id=1, source_target_pairs={{0,1},{1,2},{2,3},{3,4},{4,5},{5,6},{6,7},{7,0},{8,9},{9,10},{10,1... | collective-permute-start | bytes 1327112 | tf_op jit(solution)/shard_map/ppermute | solution.py:29
  28.5 4.4 %copy-start.10 = (f32[16,6,2304]{2,0,1:T(8,128)S(1)}, f32[16,6,2304]{2,0,1:T(8,128)}, u32[]{:S(2)}) copy-start(f32[16,6,2304]{2,0,1:T(8,128)} %get-tuple-element.82) | copy-start | bytes 2654212
  28.5 6.0 %copy-start.9 = (f32[16,6,2304]{2,0,1:T(8,128)S(1)}, f32[16,6,2304]{2,0,1:T(8,128)}, u32[]{:S(2)}) copy-start(f32[16,6,2304]{2,0,1:T(8,128)} %get-tuple-element.83) | copy-start | bytes 2654212
  28.5 7.5 %copy-start.12 = (f32[16,6,2304]{2,0,1:T(8,128)S(1)}, f32[16,6,2304]{2,0,1:T(8,128)}, u32[]{:S(2)}) copy-start(f32[16,6,2304]{2,0,1:T(8,128)} %get-tuple-element.77) | copy-start | bytes 2654212
  32.2 5.4 %copy-start.11 = (f32[16,6,2304]{2,0,1:T(8,128)S(1)}, f32[16,6,2304]{2,0,1:T(8,128)}, u32[]{:S(2)}) copy-start(f32[16,6,2304]{2,0,1:T(8,128)} %get-tuple-element.79) | copy-start | bytes 2654212
  34.4 5.5 %copy-start.1 = (f32[16,3,6,2304]{3,0,2,1:T(8,128)S(1)}, f32[16,3,6,2304]{3,0,2,1:T(8,128)}, u32[]{:S(2)}) copy-start(f32[16,3,6,2304]{3,0,2,1:T(8,128)} %param.3) | copy-start | bytes 7962628
  49.3 2.0 copy-start.3
  51.3 20.7 %copy-start.6 = (f32[16,6,2304]{2,1,0:T(8,128)S(1)}, f32[16,6,2304]{2,1,0:T(8,128)}, u32[]{:S(2)}) copy-start(f32[16,6,2304]{2,1,0:T(8,128)} %copy.67) | copy-start | bytes 2654212
  51.3 20.7 %copy-start.7 = (f32[16,6,2304]{2,1,0:T(8,128)S(1)}, f32[16,6,2304]{2,1,0:T(8,128)}, u32[]{:S(2)}) copy-start(f32[16,6,2304]{2,1,0:T(8,128)} %copy.68) | copy-start | bytes 2654212
  98.6 15.4 %copy-start.5 = (f32[16,8,2304]{2,1,0:T(8,128)S(1)}, f32[16,8,2304]{2,1,0:T(8,128)}, u32[]{:S(2)}) copy-start(f32[16,8,2304]{2,1,0:T(8,128)} %copy.62) | copy-start | bytes 3538948
  98.6 12.8 %collective-permute-start.6 = (f32[16,3,1,2304]{3,0,2,1:T(8,128)S(1)}, f32[16,3,1,2304]{3,0,2,1:T(8,128)S(1)}, u32[]{:S(2)}, u32[]{:S(2)}) collective-permute-start(f32[16,3,1,2304]{3,0,2,1:T(8,128)S(1)} %copy.63), channel_id=1, source_target_pairs={{0,1},{1,2},{2,3},{3,4},{4,5},{5,6},{6,7},{7,0},{8,9},{9,10},{10,1... | collective-permute-start | bytes 1327112 | tf_op jit(solution)/shard_map/ppermute | solution.py:29
  100.3 13.2 %collective-permute-start.7 = (f32[16,3,1,2304]{3,0,2,1:T(8,128)S(1)}, f32[16,3,1,2304]{3,0,2,1:T(8,128)S(1)}, u32[]{:S(2)}, u32[]{:S(2)}) collective-permute-start(f32[16,3,1,2304]{3,0,2,1:T(8,128)S(1)} %copy.64), channel_id=1, source_target_pairs={{1,0},{2,1},{3,2},{4,3},{5,4},{6,5},{7,6},{0,7},{9,8},{10,9},{11,1... | collective-permute-start | bytes 1327112 | tf_op jit(solution)/shard_map/ppermute | solution.py:30
  101.2 14.0 %collective-permute-start.4 = (f32[4,3,6,2304]{3,2,1,0:T(8,128)S(1)}, f32[4,3,6,2304]{3,2,1,0:T(8,128)S(1)}, u32[]{:S(2)}, u32[]{:S(2)}) collective-permute-start(f32[4,3,6,2304]{3,2,1,0:T(8,128)S(1)} %get-tuple-element.33), channel_id=1, source_target_pairs={{8,0},{16,8},{24,16},{32,24},{40,32},{48,40},{56,48},{64,56},{72,6... | collective-permute-start | bytes 1990664 | tf_op jit(solution)/shard_map/ppermute | solution.py:30
  101.4 14.8 %collective-permute-start.5 = (f32[4,3,6,2304]{3,2,1,0:T(8,128)S(1)}, f32[4,3,6,2304]{3,2,1,0:T(8,128)S(1)}, u32[]{:S(2)}, u32[]{:S(2)}) collective-permute-start(f32[4,3,6,2304]{3,2,1,0:T(8,128)S(1)} %get-tuple-element.34), channel_id=1, source_target_pairs={{0,8},{8,16},{16,24},{24,32},{32,40},{40,48},{48,56},{56,64},{64,7... | collective-permute-start | bytes 1990664 | tf_op jit(solution)/shard_map/ppermute | solution.py:29
  114.0 3.1 %copy-start.4 = (f32[16,3,6,2304]{3,2,1,0:T(8,128)S(1)}, f32[16,3,6,2304]{3,2,1,0:T(8,128)}, u32[]{:S(2)}) copy-start(f32[16,3,6,2304]{3,2,1,0:T(8,128)} %get-tuple-element.32) | copy-start | bytes 7962628
  114.0 3.1 %copy-start.8 = (f32[16,6,2304]{2,1,0:T(8,128)S(1)}, f32[16,6,2304]{2,1,0:T(8,128)}, u32[]{:S(2)}) copy-start(f32[16,6,2304]{2,1,0:T(8,128)} %get-tuple-element.12) | copy-start | bytes 2654212
  115.2 1.0 copy-start.13
  116.2 0.9 copy-start.14
  117.1 91.7 %copy-start.2 = (f32[16,3,6,2304]{3,0,2,1:T(8,128)S(1)}, f32[16,3,6,2304]{3,0,2,1:T(8,128)}, u32[]{:S(2)}) copy-start(f32[16,3,6,2304]{3,0,2,1:T(8,128)} %param.3) | copy-start | bytes 7962628
where the time goes:
time: 222 us; the launch traced here: 218 us
  other arithmetic  75.5 us (34%)
  local copies, waits for them, and re-layouts  73.7 us (33%)
  blocking collectives  45.7 us (21%)
  waiting for transfers between devices  10.5 us (5%)
  starting transfers between devices  7.2 us (3%)
  between operations  5.91 us (3%)
    psum x5, blocking collectives, over_axes(): return functools.reduce(lax.psum, axes, array)  45.7 us
    reduce_sum x1, other arithmetic, on_device(): jnp.sum(residue * level_rate)  44.7 us
    reduce_sum x1, other arithmetic, descent_direction(): jnp.sum(residue_center * gradient, axis=1)  20 us
    slice x6, local copies, waits for them, and re-layouts, next_z(): jnp.roll(values, -1, 3)  14.5 us
    slice x6, local copies, waits for them, and re-layouts, next_y(): return jnp.roll(values, -NZ, 3)  14.4 us
    unnamed x35, local copies, waits for them, and re-layouts  12 us
    slice x6, local copies, waits for them, and re-layouts, next_z(): jnp.roll(values, NZ - 1, 3)  10.8 us
    ppermute x4, waiting for transfers between devices, padded_2(): before = lax.ppermute(last, axis, up)  8.86 us
  transfers between devices with their start and end apart: 8, of which 3 were waited for; matrix products, arithmetic and copies ran while one was open for 19% of the time, Pallas kernels for 0%

commit v1 on v0

v1 whole, which is shorter than its diff:
```python
import math

import jax
import jax.numpy as jnp
from jax import lax
from jax.experimental import pallas as pl
from jax.experimental.pallas import tpu as pltpu
from jax.sharding import Mesh
from jax.sharding import PartitionSpec as P

NY = 48
NZ = 48
NC = NY * NZ
LANES = 128
NJ = NC // LANES
TM = ("tm_0", "tm_1", "tm_2")
SPACE = ("space_0", "space_1")
ALL = TM + SPACE

weights = (0.8, -0.2, 4.0 / 105.0, -1.0 / 280.0)
viscosity = 0.02
step_size = 0.15

ROWS = 32
OWN = 8


def cols(j):
    return pl.ds(j * LANES, LANES)


def roll(x, shift):
    return pltpu.roll(x, shift % LANES, x.ndim - 1)


class Shifts:
    def __init__(self, shape):
        self.lane = lax.broadcasted_iota(jnp.int32, shape, len(shape) - 1)

    def y_next(self, here, after):
        return roll(jnp.where(self.lane < NZ, after, here), -NZ)

    def y_prev(self, before, here):
        return roll(jnp.where(self.lane >= LANES - NZ, before, here), NZ)

    def column(self, j, value):
        base = (j * LANES) % NZ
        mask = None
        for lane in range(LANES):
            if (base + lane) % NZ == value:
                one = self.lane == lane
                mask = one if mask is None else jnp.logical_or(mask, one)
        return mask

    def z_next(self, j, before, here, after):
        base = (j * LANES) % NZ
        straight = here if (base + LANES) % NZ == 0 else jnp.where(self.lane == 0, after, here)
        first = (NZ - 1 - base) % NZ
        wrap = here if first >= NZ - 1 else jnp.where(self.lane >= LANES - (NZ - 1), before, here)
        return jnp.where(self.column(j, NZ - 1), roll(wrap, NZ - 1), roll(straight, -1))

    def z_prev(self, j, before, here, after):
        base = (j * LANES) % NZ
        straight = here if base == 0 else jnp.where(self.lane == LANES - 1, before, here)
        last = LANES - 1 - (base + LANES - 1) % NZ
        wrap = here if last + NZ - 1 < LANES else jnp.where(self.lane < NZ - 1, after, here)
        return jnp.where(self.column(j, 0), roll(wrap, -(NZ - 1)), roll(straight, 1))


def rate(ref, c, x, j, levels, scaled):
    total = None
    for m in range(1, 5):
        ahead = ref[c, x, j, pl.ds(OWN + m, levels), :]
        behind = ref[c, x, j, pl.ds(OWN - m, levels), :]
        term = scaled[m - 1] * (ahead - behind)
        total = term if total is None else total + term
    return total


def fill(scratch, own, low, high, left, right):
    slabs, levels = own.shape[1], own.shape[2]

    def slab(x, carry):
        for c in range(3):
            for j in range(NJ):
                scratch[c, x + 1, j, pl.ds(OWN, levels), :] = own[c, x, :, cols(j)]
                scratch[c, x + 1, j, pl.ds(OWN - 4, 4), :] = low[c, x, :, cols(j)]
                scratch[c, x + 1, j, pl.ds(OWN + levels, 4), :] = high[c, x, :, cols(j)]
        return carry

    lax.fori_loop(0, slabs, slab, 0)
    for c in range(3):
        for j in range(NJ):
            scratch[c, 0, j, pl.ds(OWN, levels), :] = left[c, :, cols(j)]
            scratch[c, slabs + 1, j, pl.ds(OWN, levels), :] = right[c, :, cols(j)]


def residual_kernel(spacing, scale, own, low, high, left, right, forcing, res, rt, grad, scratch):
    levels = own.shape[2]
    x = pl.program_id(0)

    @pl.when(x == 0)
    def _():
        fill(scratch, own, low, high, left, right)

    scaled = [w * scale[0] for w in weights]
    alpha = 1.0 / (2.0 * spacing)
    beta = viscosity / spacing**2
    sh = Shifts((levels, LANES))

    def at(c, dx, j):
        return scratch[c, x + 1 + dx, j % NJ, pl.ds(OWN, levels), :]

    for j in range(NJ):
        vel = [alpha * at(a, 0, j) for a in range(3)]
        for c in range(3):
            here, before, after = at(c, 0, j), at(c, 0, j - 1), at(c, 0, j + 1)
            pairs = (
                (at(c, 1, j), at(c, -1, j)),
                (sh.y_next(here, after), sh.y_prev(before, here)),
                (sh.z_next(j, before, here, after), sh.z_prev(j, before, here, after)),
            )
            q = rate(scratch, c, x + 1, j, levels, scaled)
            total = q + (6.0 * beta) * here
            near = None
            for a, (nxt, prv) in enumerate(pairs):
                diff = nxt - prv
                grad[a * 3 + c, 0, :, cols(j)] = diff
                total = total + vel[a] * diff
                both = nxt + prv
                near = both if near is None else near + both
            total = total - beta * near
            if c == 0:
                total = total - forcing[:, cols(j)]
            res[c, 0, :, cols(j)] = total
            rt[c, 0, :, cols(j)] = q


def descent_kernel(spacing, scale, own, rt, grad, left0, right0, res, low, high, left, right, base, sums, scratch, flow, acc):
    levels = own.shape[2]
    slabs = own.shape[1]
    x = pl.program_id(0)
    alpha = 1.0 / (2.0 * spacing)
    beta = viscosity / spacing**2

    @pl.when(x == 0)
    def _():
        fill(scratch, res, low, high, left, right)
        flow[0] = alpha * left0[...]
        flow[slabs + 1] = alpha * right0[...]

        def slab(i, carry):
            flow[i + 1] = alpha * own[0, i]
            return carry

        lax.fori_loop(0, slabs, slab, 0)
        acc[...] = jnp.zeros_like(acc)

    scaled = [w * scale[0] for w in weights]
    sh = Shifts((levels, LANES))

    def at(c, dx, j):
        return scratch[c, x + 1 + dx, j % NJ, pl.ds(OWN, levels), :]

    s1 = s2 = s3 = None
    for c in range(3):
        cache = {}

        def products(j):
            j = j % NJ
            if j not in cache:
                value = at(c, 0, j)
                y = (alpha * own[1, x, :, cols(j)]) * value
                z = (alpha * own[2, x, :, cols(j)]) * value
                s = beta * value
                cache[j] = (y + s, y - s, z + s, z - s)
            return cache[j]

        for j in range(NJ):
            here = at(c, 0, j)
            (yp0, ym0, zp0, zm0) = products(j - 1)
            (yp1, ym1, zp1, zm1) = products(j)
            (yp2, ym2, zp2, zm2) = products(j + 1)
            total = (6.0 * beta) * here - rate(scratch, c, x + 1, j, levels, scaled)
            nxt, prv = at(c, 1, j), at(c, -1, j)
            total = total - (flow[x + 2, :, cols(j)] + beta) * nxt
            total = total + (flow[x, :, cols(j)] - beta) * prv
            total = total - sh.y_next(yp1, yp2) + sh.y_prev(ym0, ym1)
            total = total - sh.z_next(j, zp0, zp1, zp2) + sh.z_prev(j, zm0, zm1, zm2)
            dots = None
            for k in range(3):
                term = at(k, 0, j) * grad[c * 3 + k, 0, :, cols(j)]
                dots = term if dots is None else dots + term
            total = total + alpha * dots
            q = rt[c, 0, :, cols(j)]
            t1, t2, t3 = here * q, q * q, total * q
            s1 = t1 if s1 is None else s1 + t1
            s2 = t2 if s2 is None else s2 + t2
            s3 = t3 if s3 is None else s3 + t3
            base[c, 0, :, cols(j)] = own[c, x, :, cols(j)] - step_size * total
    acc[0] += s1
    acc[1] += s2
    acc[2] += s3

    @pl.when(x == slabs - 1)
    def _():
        lane = lax.broadcasted_iota(jnp.int32, (1, LANES), 1)
        row = jnp.zeros((1, LANES), jnp.float32)
        for k in range(3):
            row = jnp.where(lane == k, jnp.sum(acc[k]), row)
        sums[...] = jnp.broadcast_to(row[None], sums.shape)


def update_kernel(cells, period, gathered, base, rt, out, pgrad):
    row = jnp.sum(gathered[...], axis=0)
    s1, s2, s3 = row[0, 0], row[0, 1], row[0, 2]
    weight = jnp.full((1, LANES), step_size * s3, jnp.float32) / jnp.full((1, LANES), s2, jnp.float32)
    weight = weight[0, 0]
    out[...] = base[...] + weight * rt[...]

    @pl.when(pl.program_id(0) == 0)
    def _():
        pgrad[...] = jnp.full((1, LANES), -s1, jnp.float32) / jnp.full((1, LANES), period[0] * cells, jnp.float32)


def halo(array, axis, dim, width):
    count, length = lax.axis_size(axis), array.shape[dim]
    up = [(i, (i + 1) % count) for i in range(count)]
    down = [(j, i) for i, j in up]
    last = lax.slice_in_dim(array, length - width, length, axis=dim)
    first = lax.slice_in_dim(array, 0, width, axis=dim)
    return lax.ppermute(last, axis, up), lax.ppermute(first, axis, down)


def halos(array):
    low, high = halo(array, TM, 2, 4)
    left, right = halo(array, SPACE, 1, 1)
    return low, high, left[:, 0], right[:, 0]


def on_device(velocity, period, wavenumber):
    levels, _, slabs, _ = velocity.shape
    devices = lax.axis_size(ALL)
    total_levels = levels * lax.axis_size(TM)
    grid_first = slabs * lax.axis_size(SPACE)
    spacing = 2.0 * math.pi / NY
    u = jnp.transpose(velocity, (1, 2, 0, 3))
    scale = total_levels / period
    row_index = jnp.arange(NY, dtype=jnp.float32)
    profile = jnp.sin(wavenumber[0].astype(jnp.float32) * (2.0 * math.pi / NY) * row_index)
    forcing = jnp.repeat(profile, NZ).reshape(1, NC)

    vmem = pl.BlockSpec(memory_space=pltpu.VMEM)
    smem = pl.BlockSpec(memory_space=pltpu.SMEM)
    slab3 = pl.BlockSpec((3, 1, levels, NC), lambda i: (0, i, 0, 0))
    slab9 = pl.BlockSpec((9, 1, levels, NC), lambda i: (0, i, 0, 0))
    field = jax.ShapeDtypeStruct((3, slabs, levels, NC), jnp.float32)
    padded = pltpu.VMEM((3, slabs + 2, NJ, ROWS, LANES), jnp.float32)

    low, high, left, right = halos(u)
    res, rt, grad = pl.pallas_call(
        lambda *refs: residual_kernel(spacing, *refs),
        grid=(slabs,),
        in_specs=[smem] + [vmem] * 6,
        out_specs=[slab3, slab3, slab9],
        out_shape=[field, field, jax.ShapeDtypeStruct((9, slabs, levels, NC), jnp.float32)],
        scratch_shapes=[padded],
        name="residual",
    )(scale, u, low, high, left, right, forcing)

    rlow, rhigh, rleft, rright = halos(res)
    base, sums = pl.pallas_call(
        lambda *refs: descent_kernel(spacing, *refs),
        grid=(slabs,),
        in_specs=[smem, vmem, slab3, slab9] + [vmem] * 7,
        out_specs=[slab3, pl.BlockSpec((devices, 1, LANES), lambda i: (0, 0, 0))],
        out_shape=[field, jax.ShapeDtypeStruct((devices, 1, LANES), jnp.float32)],
        scratch_shapes=[
            padded,
            pltpu.VMEM((slabs + 2, levels, NC), jnp.float32),
            pltpu.VMEM((3, levels, LANES), jnp.float32),
        ],
        name="descent",
    )(scale, u, rt, grad, left[0], right[0], res, rlow, rhigh, rleft, rright)

    gathered = lax.all_to_all(sums, ALL, 0, 0)
    cells = 3.0 * total_levels * grid_first * NY * NZ
    updated, pgrad = pl.pallas_call(
        lambda *refs: update_kernel(cells, *refs),
        grid=(slabs,),
        in_specs=[smem, vmem, slab3, slab3],
        out_specs=[slab3, pl.BlockSpec((1, LANES), lambda i: (0, 0))],
        out_shape=[field, jax.ShapeDtypeStruct((1, LANES), jnp.float32)],
        name="update",
    )(period, gathered, base, rt)
    back = (2, 0, 1, 3)
    return jnp.transpose(updated, back), jnp.transpose(res, back), pgrad[0, :1]


def solution(mesh):
    split = Mesh(mesh.devices.reshape(2, 4, 2, 2, 4), ALL)
    in_specs = (P(TM, None, SPACE, None), P(), P())
    out_specs = (P(TM, None, SPACE, None), P(TM, None, SPACE, None), P())
    return jax.shard_map(on_device, mesh=split, in_specs=in_specs, out_specs=out_specs, check_vma=False)
```

time: 222 us -> 102 us (0.46)
  the two profiles are of different devices: /device:TPU:40 before, /device:TPU:1 now
where the time goes in v1:
time: 102 us
  Pallas kernels  29.2 us (29%)
  blocking collectives  25.3 us (25%)
  starting transfers between devices  21.3 us (21%)
  local copies, waits for them, and re-layouts  13.6 us (13%)
  waiting for transfers between devices  10.4 us (10%)
  between operations  2.02 us (2%)
    all_to_all x1, blocking collectives, on_device(): gathered = lax.all_to_all(sums, ALL, 0, 0)  25.3 us
    ppermute x8, starting transfers between devices, halo(): return (lax.ppermute(last, axis, up), lax.ppermute(first, axis, down))  21.3 us
    pallas_call x1, Pallas kernels, on_device(): pl.pallas_call(lambda *refs: descent_kernel(spacing, *refs), grid=(slabs,...  12.7 us
    ppermute x8, waiting for transfers between devices, halo(): return (lax.ppermute(last, axis, up), lax.ppermute(first, axis, down))  10.4 us
    pallas_call x1, Pallas kernels, on_device(): pl.pallas_call(lambda *refs: residual_kernel(spacing, *refs), grid=(slabs...  10.1 us
    slice x4, local copies, waits for them, and re-layouts, halo(): first = lax.slice_in_dim(array, 0, width, axis=dim)  7.23 us
    pallas_call x1, Pallas kernels, on_device(): pl.pallas_call(lambda *refs: update_kernel(cells, *refs), grid=(slabs,),...  6.36 us
  transfers between devices with their start and end apart: 8, of which 5 were waited for; matrix products, arithmetic and copies ran while one was open for 6% of the time, Pallas kernels for 0%

profile of v1, /device:TPU:1, one launch (start us, length us, event | category | flops | bytes accessed | tf_op | source)
XLA Modules:
  0.0 101.9 jit_solution(144964191018986054)
XLA Ops:
  0.6 2.1 %fusion.2 = (f32[3,1,16,2304]{3,2,1,0:T(8,128)}, f32[3,1,16,2304]{3,2,1,0:T(8,128)}) fusion(f32[3,6,16,2304]{3,2,1,0:T(8,128)} %bitcast.14), kind=kLoop, calls=%fused_computation.5 | loop fusion | bytes 1769472 | tf_op jit(solution)/shard_map/slice | solution.py:231
  2.7 4.5 %collective-permute-start.3 = (f32[3,1,16,2304]{3,2,1,0:T(8,128)}, f32[3,1,16,2304]{3,2,1,0:T(8,128)S(1)}, u32[]{:S(2)}, u32[]{:S(2)}) collective-permute-start(f32[3,1,16,2304]{3,2,1,0:T(8,128)} %get-tuple-element.21), channel_id=1, source_target_pairs={{1,0},{2,1},{3,2},{4,3},{5,4},{6,5},{7,6},{0,7},{9,8},{10,9},{11,1... | collective-permute-start | bytes 1327112 | tf_op jit(solution)/shard_map/ppermute | solution.py:232
  7.2 2.0 %fusion.3 = (f32[3,6,4,2304]{3,2,1,0:T(4,128)S(1)}, f32[3,6,4,2304]{3,2,1,0:T(4,128)S(1)}) fusion(f32[3,6,16,2304]{3,2,1,0:T(8,128)} %bitcast.15), kind=kLoop, calls=%fused_computation.6 | loop fusion | bytes 2654208 | tf_op jit(solution)/shard_map/slice | solution.py:231
  9.2 1.0 %collective-permute-start.1 = (f32[3,6,4,2304]{3,2,1,0:T(4,128)S(1)}, f32[3,6,4,2304]{3,2,1,0:T(4,128)S(1)}, u32[]{:S(2)}, u32[]{:S(2)}) collective-permute-start(f32[3,6,4,2304]{3,2,1,0:T(4,128)S(1)} %get-tuple-element.23), channel_id=1, source_target_pairs={{8,0},{16,8},{24,16},{32,24},{40,32},{48,40},{56,48},{64,56},{72,6... | collective-permute-start | bytes 1990664 | tf_op jit(solution)/shard_map/ppermute | solution.py:232
  10.2 1.6 %collective-permute-start = (f32[3,6,4,2304]{3,2,1,0:T(4,128)S(1)}, f32[3,6,4,2304]{3,2,1,0:T(4,128)S(1)}, u32[]{:S(2)}, u32[]{:S(2)}) collective-permute-start(f32[3,6,4,2304]{3,2,1,0:T(4,128)S(1)} %get-tuple-element.24), channel_id=1, source_target_pairs={{0,8},{8,16},{16,24},{24,32},{32,40},{40,48},{48,56},{56,64},{64,7... | collective-permute-start | bytes 1990664 | tf_op jit(solution)/shard_map/ppermute | solution.py:232
  13.2 0.7 broadcast_in_dim.3
  13.8 1.4 %reshape_reshape.3.refs_6_ = f32[1,2304]{1,0:T(1,128)} reshape(f32[48,48]{1,0:T(8,128)} %broadcast_in_dim.3) | data formatting | bytes 18432 | tf_op jit(solution)/shard_map/reshape;reshape | solution.py:251
  15.3 1.1 %collective-permute-done.3 = f32[3,1,16,2304]{3,2,1,0:T(8,128)S(1)} collective-permute-done((f32[3,1,16,2304]{3,2,1,0:T(8,128)}, f32[3,1,16,2304]{3,2,1,0:T(8,128)S(1)}, u32[]{:S(2)}, u32[]{:S(2)}) %collective-permute-start.3) | collective-permute-done | bytes 442400 | tf_op jit(solution)/shard_map/ppermute | solution.py:232
  16.4 0.7 slice_bitcast_fusion.refs_5_
  17.1 3.2 %collective-permute-done.2 = f32[3,1,16,2304]{3,2,1,0:T(8,128)S(1)} collective-permute-done((f32[3,1,16,2304]{3,2,1,0:T(8,128)}, f32[3,1,16,2304]{3,2,1,0:T(8,128)S(1)}, u32[]{:S(2)}, u32[]{:S(2)}) %collective-permute-start.2) | collective-permute-done | bytes 442400 | tf_op jit(solution)/shard_map/ppermute | solution.py:232
  20.4 0.7 copy-done
  21.1 0.2 copy-done.4
  21.3 0.2 copy-done.5
  21.5 10.1 %residual.1 = (f32[3,6,16,2304]{3,2,1,0:T(8,128)}, f32[3,6,16,2304]{3,2,1,0:T(8,128)}, f32[9,6,16,2304]{3,2,1,0:T(8,128)}) custom-call(f32[1]{0:T(128)S(6)} %div.3.refs_0_, f32[3,6,16,2304]{3,2,1,0:T(8,128)} %bitcast.16, f32[3,6,4,2304]{3,2,1,0:T(4,128)} %copy-done.5, f32[3,6,4,2304]{3,2,1,0:T(4,128)} %copy-done.4, f32[3,16,2304]{2,1,0:T(8,128)} %bitcast.19, ...), custom_call_target="tpu_custom_call" | custom-call | tf_op jit(solution)/shard_map/residual/pallas_call | solution.py:261
  31.6 1.2 %fusion = (f32[3,1,16,2304]{3,2,0,1:T(8,128)S(1)}, f32[3,1,16,2304]{3,2,0,1:T(8,128)S(1)}) fusion(f32[3,6,16,2304]{3,2,1,0:T(8,128)} %get-tuple-element.12.refs_6_), kind=kLoop, calls=%fused_computation.3 | loop fusion | bytes 1769472 | tf_op jit(solution)/shard_map/slice | solution.py:231
  32.8 2.0 %fusion.1 = (f32[3,6,4,2304]{3,2,1,0:T(4,128)S(1)}, f32[3,6,4,2304]{3,2,1,0:T(4,128)S(1)}) fusion(f32[3,6,16,2304]{3,2,1,0:T(8,128)} %get-tuple-element.12.refs_6_), kind=kLoop, calls=%fused_computation.4 | loop fusion | bytes 2654208 | tf_op jit(solution)/shard_map/slice | solution.py:231
  34.8 3.5 %collective-permute-start.7 = (f32[3,1,16,2304]{3,2,0,1:T(8,128)S(1)}, f32[3,1,16,2304]{3,2,0,1:T(8,128)S(1)}, u32[]{:S(2)}, u32[]{:S(2)}) collective-permute-start(f32[3,1,16,2304]{3,2,0,1:T(8,128)S(1)} %get-tuple-element.17), channel_id=1, source_target_pairs={{1,0},{2,1},{3,2},{4,3},{5,4},{6,5},{7,6},{0,7},{9,8},{10,9},{11,1... | collective-permute-start | bytes 1327112 | tf_op jit(solution)/shard_map/ppermute | solution.py:232
  38.3 10.7 %collective-permute-start.5 = (f32[3,6,4,2304]{3,2,1,0:T(4,128)S(1)}, f32[3,6,4,2304]{3,2,1,0:T(4,128)S(1)}, u32[]{:S(2)}, u32[]{:S(2)}) collective-permute-start(f32[3,6,4,2304]{3,2,1,0:T(4,128)S(1)} %get-tuple-element.19), channel_id=1, source_target_pairs={{8,0},{16,8},{24,16},{32,24},{40,32},{48,40},{56,48},{64,56},{72,6... | collective-permute-start | bytes 1990664 | tf_op jit(solution)/shard_map/ppermute | solution.py:232
  49.0 1.6 %slice_bitcast_fusion.1.refs_4_ = f32[16,2304]{1,0:T(8,128)} fusion(f32[3,1,16,2304]{3,2,1,0:T(8,128)} %copy-done), kind=kLoop, calls=%fused_computation.1 | loop fusion | bytes 294912 | tf_op jit(solution)/shard_map/squeeze | solution.py:284
  50.8 5.9 %collective-permute-done.4.refs_7_ = f32[3,6,4,2304]{3,2,1,0:T(4,128)S(1)} collective-permute-done((f32[3,6,4,2304]{3,2,1,0:T(4,128)S(1)}, f32[3,6,4,2304]{3,2,1,0:T(4,128)S(1)}, u32[]{:S(2)}, u32[]{:S(2)}) %collective-permute-start.4) | collective-permute-done | bytes 663584 | tf_op jit(solution)/shard_map/ppermute | solution.py:232
  56.6 0.8 copy-done.3
  57.5 12.7 %descent.1 = (f32[3,6,16,2304]{3,2,1,0:T(8,128)}, f32[128,1,128]{2,1,0:T(1,128)}) custom-call(f32[1]{0:T(128)S(6)} %div.3.refs_0_, f32[3,6,16,2304]{3,2,1,0:T(8,128)} %bitcast.17, f32[3,6,16,2304]{3,2,1,0:T(8,128)} %get-tuple-element.10.refs_2_.refs_3_, f32[9,6,16,2304]{3,2,1,0:T(8,128)} %get-tuple-element.11.refs_3_, ...), custom_call_target="tpu_custom_call" | custom-call | tf_op jit(solution)/shard_map/descent/pallas_call | solution.py:272
  70.2 25.3 %all_to_all.5.refs_1_ = f32[128,1,128]{2,1,0:T(1,128)} all-to-all(f32[128,1,128]{2,1,0:T(1,128)} %get-tuple-element.13), channel_id=1, replica_groups=mesh['tm_0'=2,'tm_1'=4,'tm_2'=2,'space_0'=2,'space_1'=4] {'tm_0','tm_1',..., dimensions={0} | all-to-all | bytes 131072 | tf_op jit(solution)/shard_map/all_to_all | solution.py:286
  95.5 6.4 %update.1 = (f32[3,6,16,2304]{3,2,1,0:T(8,128)}, f32[1,128]{1,0:T(1,128)}) custom-call(f32[1]{0:T(128)S(6)} %copy.10.refs_0_, f32[128,1,128]{2,1,0:T(1,128)} %all_to_all.5.refs_1_, f32[3,6,16,2304]{3,2,1,0:T(8,128)} %get-tuple-element.14.refs_2_, f32[3,6,16,2304]{3,2,1,0:T(8,128)} %get-tuple-element.10.refs_2_.refs_3_), custom_call_target="tpu_custom_call" | custom-call | tf_op jit(solution)/shard_map/update/pallas_call | solution.py:288
  (21 shorter events, 0.3 us)
Async XLA Ops:
  2.7 13.6 %collective-permute-start.3 = (f32[3,1,16,2304]{3,2,1,0:T(8,128)}, f32[3,1,16,2304]{3,2,1,0:T(8,128)S(1)}, u32[]{:S(2)}, u32[]{:S(2)}) collective-permute-start(f32[3,1,16,2304]{3,2,1,0:T(8,128)} %get-tuple-element.21), channel_id=1, source_target_pairs={{1,0},{2,1},{3,2},{4,3},{5,4},{6,5},{7,6},{0,7},{9,8},{10,9},{11,1... | collective-permute-start | bytes 1327112 | tf_op jit(solution)/shard_map/ppermute | solution.py:232
  7.2 13.1 %collective-permute-start.2 = (f32[3,1,16,2304]{3,2,1,0:T(8,128)}, f32[3,1,16,2304]{3,2,1,0:T(8,128)S(1)}, u32[]{:S(2)}, u32[]{:S(2)}) collective-permute-start(f32[3,1,16,2304]{3,2,1,0:T(8,128)} %get-tuple-element.22), channel_id=1, source_target_pairs={{0,1},{1,2},{2,3},{3,4},{4,5},{5,6},{6,7},{7,0},{8,9},{9,10},{10,1... | collective-permute-start | bytes 1327112 | tf_op jit(solution)/shard_map/ppermute | solution.py:232
  9.2 11.2 %collective-permute-start.1 = (f32[3,6,4,2304]{3,2,1,0:T(4,128)S(1)}, f32[3,6,4,2304]{3,2,1,0:T(4,128)S(1)}, u32[]{:S(2)}, u32[]{:S(2)}) collective-permute-start(f32[3,6,4,2304]{3,2,1,0:T(4,128)S(1)} %get-tuple-element.23), channel_id=1, source_target_pairs={{8,0},{16,8},{24,16},{32,24},{40,32},{48,40},{56,48},{64,56},{72,6... | collective-permute-start | bytes 1990664 | tf_op jit(solution)/shard_map/ppermute | solution.py:232
  10.2 10.2 %collective-permute-start = (f32[3,6,4,2304]{3,2,1,0:T(4,128)S(1)}, f32[3,6,4,2304]{3,2,1,0:T(4,128)S(1)}, u32[]{:S(2)}, u32[]{:S(2)}) collective-permute-start(f32[3,6,4,2304]{3,2,1,0:T(4,128)S(1)} %get-tuple-element.24), channel_id=1, source_target_pairs={{0,8},{8,16},{16,24},{24,32},{32,40},{40,48},{48,56},{56,64},{64,7... | collective-permute-start | bytes 1990664 | tf_op jit(solution)/shard_map/ppermute | solution.py:232
  16.4 4.0 %copy-start.1 = (f32[3,1,16,2304]{3,2,1,0:T(8,128)}, f32[3,1,16,2304]{3,2,1,0:T(8,128)S(1)}, u32[]{:S(2)}) copy-start(f32[3,1,16,2304]{3,2,1,0:T(8,128)S(1)} %collective-permute-done.3) | copy-start | bytes 1327108
  20.3 0.8 copy-start
  20.4 0.9 copy-start.4
  20.4 1.1 %copy-start.5 = (f32[3,6,4,2304]{3,2,1,0:T(4,128)}, f32[3,6,4,2304]{3,2,1,0:T(4,128)S(1)}, u32[]{:S(2)}) copy-start(f32[3,6,4,2304]{3,2,1,0:T(4,128)S(1)} %collective-permute-done.refs_2_) | copy-start | bytes 1990660
  34.8 15.8 %collective-permute-start.7 = (f32[3,1,16,2304]{3,2,0,1:T(8,128)S(1)}, f32[3,1,16,2304]{3,2,0,1:T(8,128)S(1)}, u32[]{:S(2)}, u32[]{:S(2)}) collective-permute-start(f32[3,1,16,2304]{3,2,0,1:T(8,128)S(1)} %get-tuple-element.17), channel_id=1, source_target_pairs={{1,0},{2,1},{3,2},{4,3},{5,4},{6,5},{7,6},{0,7},{9,8},{10,9},{11,1... | collective-permute-start | bytes 1327112 | tf_op jit(solution)/shard_map/ppermute | solution.py:232
  38.3 12.3 %collective-permute-start.6 = (f32[3,1,16,2304]{3,2,0,1:T(8,128)S(1)}, f32[3,1,16,2304]{3,2,0,1:T(8,128)S(1)}, u32[]{:S(2)}, u32[]{:S(2)}) collective-permute-start(f32[3,1,16,2304]{3,2,0,1:T(8,128)S(1)} %get-tuple-element.18), channel_id=1, source_target_pairs={{0,1},{1,2},{2,3},{3,4},{4,5},{5,6},{6,7},{7,0},{8,9},{9,10},{10,1... | collective-permute-start | bytes 1327112 | tf_op jit(solution)/shard_map/ppermute | solution.py:232
  38.3 12.4 %collective-permute-start.5 = (f32[3,6,4,2304]{3,2,1,0:T(4,128)S(1)}, f32[3,6,4,2304]{3,2,1,0:T(4,128)S(1)}, u32[]{:S(2)}, u32[]{:S(2)}) collective-permute-start(f32[3,6,4,2304]{3,2,1,0:T(4,128)S(1)} %get-tuple-element.19), channel_id=1, source_target_pairs={{8,0},{16,8},{24,16},{32,24},{40,32},{48,40},{56,48},{64,56},{72,6... | collective-permute-start | bytes 1990664 | tf_op jit(solution)/shard_map/ppermute | solution.py:232
  49.0 7.6 %collective-permute-start.4 = (f32[3,6,4,2304]{3,2,1,0:T(4,128)S(1)}, f32[3,6,4,2304]{3,2,1,0:T(4,128)S(1)}, u32[]{:S(2)}, u32[]{:S(2)}) collective-permute-start(f32[3,6,4,2304]{3,2,1,0:T(4,128)S(1)} %get-tuple-element.20), channel_id=1, source_target_pairs={{0,8},{8,16},{16,24},{24,32},{32,40},{40,48},{48,56},{56,64},{64,7... | collective-permute-start | bytes 1990664 | tf_op jit(solution)/shard_map/ppermute | solution.py:232
  50.6 6.0 %copy-start.6 = (f32[3,1,16,2304]{3,2,0,1:T(8,128)}, f32[3,1,16,2304]{3,2,0,1:T(8,128)S(1)}, u32[]{:S(2)}) copy-start(f32[3,1,16,2304]{3,2,0,1:T(8,128)S(1)} %collective-permute-done.7) | copy-start | bytes 1327108
  50.6 6.0 %copy-start.7 = (f32[3,1,16,2304]{3,2,0,1:T(8,128)}, f32[3,1,16,2304]{3,2,0,1:T(8,128)S(1)}, u32[]{:S(2)}) copy-start(f32[3,1,16,2304]{3,2,0,1:T(8,128)S(1)} %collective-permute-done.6) | copy-start | bytes 1327108
  50.7 5.9 %copy-start.2 = (f32[3,6,4,2304]{3,2,1,0:T(4,128)}, f32[3,6,4,2304]{3,2,1,0:T(4,128)S(1)}, u32[]{:S(2)}) copy-start(f32[3,6,4,2304]{3,2,1,0:T(4,128)S(1)} %collective-permute-done.5.refs_8_) | copy-start | bytes 1990660
  56.6 0.8 copy-start.3

commit v2 on v1

--- a/solution.py
+++ b/solution.py
@@ -77,31 +77,73 @@
     return total
 
 
-def fill(scratch, own, low, high, left, right):
+def fill(scratch, own):
     slabs, levels = own.shape[1], own.shape[2]
+    zero = jnp.zeros((levels, LANES), jnp.float32)
+    edge = jnp.zeros((4, LANES), jnp.float32)
 
     def slab(x, carry):
         for c in range(3):
             for j in range(NJ):
                 scratch[c, x + 1, j, pl.ds(OWN, levels), :] = own[c, x, :, cols(j)]
-                scratch[c, x + 1, j, pl.ds(OWN - 4, 4), :] = low[c, x, :, cols(j)]
-                scratch[c, x + 1, j, pl.ds(OWN + levels, 4), :] = high[c, x, :, cols(j)]
+                scratch[c, x + 1, j, pl.ds(OWN - 4, 4), :] = edge
+                scratch[c, x + 1, j, pl.ds(OWN + levels, 4), :] = edge
         return carry
 
     lax.fori_loop(0, slabs, slab, 0)
     for c in range(3):
         for j in range(NJ):
-            scratch[c, 0, j, pl.ds(OWN, levels), :] = left[c, :, cols(j)]
-            scratch[c, slabs + 1, j, pl.ds(OWN, levels), :] = right[c, :, cols(j)]
-
-
-def residual_kernel(spacing, scale, own, low, high, left, right, forcing, res, rt, grad, scratch):
+            scratch[c, 0, j, pl.ds(OWN, levels), :] = zero
+            scratch[c, slabs + 1, j, pl.ds(OWN, levels), :] = zero
+
+
+class Borders:
+    def __init__(self, scaled):
+        row = lax.broadcasted_iota(jnp.int32, (8, LANES), 0)
+        zero = jnp.zeros((8, LANES), jnp.float32)
+        self.low = [jnp.where(row < m, zero - scaled[m - 1], zero) for m in range(1, 5)]
+        self.high = [jnp.where(row >= 8 - m, zero + scaled[m - 1], zero) for m in range(1, 5)]
+        self.pad = jnp.zeros((4, LANES), jnp.float32)
+
+    def from_low(self, four):
+        eight = jnp.concatenate([four, self.pad], axis=0)
+        total = self.low[3] * eight
+        for m in range(1, 4):
+            total = total + self.low[m - 1] * pltpu.roll(eight, m + 4, 0)
+        return total
+
+    def from_high(self, four):
+        eight = jnp.concatenate([four, self.pad], axis=0)
+        total = None
+        for m in range(1, 5):
+            term = self.high[m - 1] * pltpu.roll(eight, 8 - m, 0)
+            total = term if total is None else total + term
+        return total
+
+
+def pack_kernel(own, first, last, down, up):
     levels = own.shape[2]
     x = pl.program_id(0)
-
-    @pl.when(x == 0)
-    def _():
-        fill(scratch, own, low, high, left, right)
+    for c in range(3):
+        first[c, 0] = own[c, 0, pl.ds(0, 4), :]
+        last[c, 0] = own[c, 0, pl.ds(levels - 4, 4), :]
+
+    @pl.when(x == 0)
+    def _():
+        down[...] = own[:, 0]
+
+    @pl.when(x == pl.num_programs(0) - 1)
+    def _():
+        up[...] = own[:, 0]
+
+
+def residual_kernel(spacing, scale, own, forcing, res, rt, grad, scratch):
+    levels = own.shape[2]
+    x = pl.program_id(0)
+
+    @pl.when(x == 0)
+    def _():
+        fill(scratch, own)
 
     scaled = [w * scale[0] for w in weights]
     alpha = 1.0 / (2.0 * spacing)
@@ -136,18 +178,54 @@
             rt[c, 0, :, cols(j)] = q
 
 
-def descent_kernel(spacing, scale, own, rt, grad, left0, right0, res, low, high, left, right, base, sums, scratch, flow, acc):
-    levels = own.shape[2]
-    slabs = own.shape[1]
+def joined_kernel(spacing, scale, part, flow, low, high, left, right, res, first, last, down, up):
+    levels = part.shape[2]
+    half = levels - 8
     x = pl.program_id(0)
     alpha = 1.0 / (2.0 * spacing)
     beta = viscosity / spacing**2
-
-    @pl.when(x == 0)
-    def _():
-        fill(scratch, res, low, high, left, right)
-        flow[0] = alpha * left0[...]
-        flow[slabs + 1] = alpha * right0[...]
+    border = Borders([w * scale[0] for w in weights])
+    for c in range(3):
+        for j in range(NJ):
+            res[c, 0, pl.ds(0, 8), cols(j)] = part[c, 0, pl.ds(0, 8), cols(j)] + border.from_low(low[c, 0, :, cols(j)])
+            res[c, 0, pl.ds(half, 8), cols(j)] = part[c, 0, pl.ds(half, 8), cols(j)] + border.from_high(high[c, 0, :, cols(j)])
+
+    @pl.when(x == 0)
+    def _():
+        for c in range(3):
+            for j in range(NJ):
+                plus = alpha * flow[0, 0, :, cols(j)] + beta
+                value = res[c, 0, :, cols(j)] - plus * left[c, :, cols(j)]
+                res[c, 0, :, cols(j)] = value
+                down[c, :, cols(j)] = plus * value
+
+    @pl.when(x == pl.num_programs(0) - 1)
+    def _():
+        for c in range(3):
+            for j in range(NJ):
+                minus = alpha * flow[0, 0, :, cols(j)] - beta
+                value = res[c, 0, :, cols(j)] + minus * right[c, :, cols(j)]
+                res[c, 0, :, cols(j)] = value
+                up[c, :, cols(j)] = minus * value
+
+    for c in range(3):
+        first[c, 0] = res[c, 0, pl.ds(0, 4), :]
+        last[c, 0] = res[c, 0, pl.ds(levels - 4, 4), :]
+
+
+def descent_kernel(spacing, scale, own, res, left, right, part, grad, low, high, base, rt, sums, scratch, flow, acc):
+    levels = own.shape[2]
+    slabs = own.shape[1]
+    half = levels - 8
+    x = pl.program_id(0)
+    alpha = 1.0 / (2.0 * spacing)
+    beta = viscosity / spacing**2
+
+    @pl.when(x == 0)
+    def _():
+        fill(scratch, res)
+        flow[0] = jnp.zeros_like(flow[0])
+        flow[slabs + 1] = jnp.zeros_like(flow[0])
 
         def slab(i, carry):
             flow[i + 1] = alpha * own[0, i]
@@ -157,7 +235,15 @@
         acc[...] = jnp.zeros_like(acc)
 
     scaled = [w * scale[0] for w in weights]
+    border = Borders(scaled)
+    for c in range(3):
+        for j in range(NJ):
+            rt[c, 0, pl.ds(0, 8), cols(j)] = part[c, 0, pl.ds(0, 8), cols(j)] + border.from_low(low[c, 0, :, cols(j)])
+            rt[c, 0, pl.ds(half, 8), cols(j)] = part[c, 0, pl.ds(half, 8), cols(j)] + border.from_high(high[c, 0, :, cols(j)])
+
     sh = Shifts((levels, LANES))
+    is_first = jnp.where(x == 0, 1.0, 0.0).astype(jnp.float32)
+    is_last = jnp.where(x == slabs - 1, 1.0, 0.0).astype(jnp.float32)
 
     def at(c, dx, j):
         return scratch[c, x + 1 + dx, j % NJ, pl.ds(OWN, levels), :]
@@ -189,7 +275,10 @@
             total = total - sh.z_next(j, zp0, zp1, zp2) + sh.z_prev(j, zm0, zm1, zm2)
             dots = None
             for k in range(3):
-                term = at(k, 0, j) * grad[c * 3 + k, 0, :, cols(j)]
+                diff = grad[c * 3 + k, 0, :, cols(j)]
+                if c == 0:
+                    diff = diff + (is_last * right[k, :, cols(j)] - is_first * left[k, :, cols(j)])
+                term = at(k, 0, j) * diff
                 dots = term if dots is None else dots + term
             total = total + alpha * dots
             q = rt[c, 0, :, cols(j)]
@@ -204,38 +293,84 @@
 
     @pl.when(x == slabs - 1)
     def _():
+        sums[...] = acc[...]
+
+
+def closing_kernel(scale, part, rt, low, high, left, right, partial, base, sums, acc):
+    levels = part.shape[2]
+    half = levels - 8
+    x = pl.program_id(0)
+
+    @pl.when(x == 0)
+    def _():
+        acc[...] = jnp.zeros_like(acc)
+
+    border = Borders([w * scale[0] for w in weights])
+    total = jnp.zeros((8, LANES), jnp.float32)
+    for c in range(3):
+        for j in range(NJ):
+            for rows, take in (((0, 8), border.from_low(low[c, 0, :, cols(j)])), ((half, 8), border.from_high(high[c, 0, :, cols(j)]))):
+                rows = pl.ds(*rows)
+                total = total - take * rt[c, 0, rows, cols(j)]
+                base[c, 0, rows, cols(j)] = part[c, 0, rows, cols(j)] + step_size * take
+    acc[...] += total
+
+    def edge(sign, message):
+        total = jnp.zeros((levels, LANES), jnp.float32)
+        for c in range(3):
+            for j in range(NJ):
+                extra = message[c, :, cols(j)]
+                total = total + extra * rt[c, 0, :, cols(j)]
+                base[c, 0, :, cols(j)] = base[c, 0, :, cols(j)] - (sign * step_size) * extra
+        acc[...] += sign * (total[:8] + total[half:])
+
+    @pl.when(x == 0)
+    def _():
+        edge(1.0, left)
+
+    @pl.when(x == pl.num_programs(0) - 1)
+    def _():
+        edge(-1.0, right)
         lane = lax.broadcasted_iota(jnp.int32, (1, LANES), 1)
         row = jnp.zeros((1, LANES), jnp.float32)
         for k in range(3):
-            row = jnp.where(lane == k, jnp.sum(acc[k]), row)
+            value = jnp.sum(partial[k]) if k < 2 else jnp.sum(partial[k]) + jnp.sum(acc[...])
+            row = jnp.where(lane == k, value, row)
         sums[...] = jnp.broadcast_to(row[None], sums.shape)
 
 
-def update_kernel(cells, period, gathered, base, rt, out, pgrad):
-    row = jnp.sum(gathered[...], axis=0)
-    s1, s2, s3 = row[0, 0], row[0, 1], row[0, 2]
-    weight = jnp.full((1, LANES), step_size * s3, jnp.float32) / jnp.full((1, LANES), s2, jnp.float32)
-    weight = weight[0, 0]
-    out[...] = base[...] + weight * rt[...]
-
+def update_kernel(cells, period, gathered, base, rt, out, pgrad, weight):
     @pl.when(pl.program_id(0) == 0)
     def _():
+        row = jnp.sum(gathered[...], axis=0)
+        s1, s2, s3 = row[0, 0], row[0, 1], row[0, 2]
+        ratio = jnp.full((1, LANES), step_size * s3, jnp.float32) / jnp.full((1, LANES), s2, jnp.float32)
+        weight[...] = jnp.broadcast_to(ratio, weight.shape)
         pgrad[...] = jnp.full((1, LANES), -s1, jnp.float32) / jnp.full((1, LANES), period[0] * cells, jnp.float32)
 
-
-def halo(array, axis, dim, width):
-    count, length = lax.axis_size(axis), array.shape[dim]
+    factor = weight[...]
+    levels = base.shape[2]
+    for c in range(3):
+        for j in range(NJ):
+            for row in range(0, levels, 8):
+                rows = pl.ds(row, 8)
+                out[c, 0, rows, cols(j)] = base[c, 0, rows, cols(j)] + factor * rt[c, 0, rows, cols(j)]
+
+
+def ring(axis):
+    count = lax.axis_size(axis)
     up = [(i, (i + 1) % count) for i in range(count)]
-    down = [(j, i) for i, j in up]
-    last = lax.slice_in_dim(array, length - width, length, axis=dim)
-    first = lax.slice_in_dim(array, 0, width, axis=dim)
-    return lax.ppermute(last, axis, up), lax.ppermute(first, axis, down)
-
-
-def halos(array):
-    low, high = halo(array, TM, 2, 4)
-    left, right = halo(array, SPACE, 1, 1)
-    return low, high, left[:, 0], right[:, 0]
+    return up, [(j, i) for i, j in up]
+
+
+def exchange(first, last, down, up):
+    tm_up, tm_down = ring(TM)
+    space_up, space_down = ring(SPACE)
+    left = lax.ppermute(up, SPACE, space_up)
+    right = lax.ppermute(down, SPACE, space_down)
+    low = lax.ppermute(last, TM, tm_up)
+    high = lax.ppermute(first, TM, tm_down)
+    return low, high, left, right
 
 
 def on_device(velocity, period, wavenumber):
@@ -252,36 +387,78 @@
 
     vmem = pl.BlockSpec(memory_space=pltpu.VMEM)
     smem = pl.BlockSpec(memory_space=pltpu.SMEM)
+    slab1 = pl.BlockSpec((1, 1, levels, NC), lambda i: (0, i, 0, 0))
     slab3 = pl.BlockSpec((3, 1, levels, NC), lambda i: (0, i, 0, 0))
     slab9 = pl.BlockSpec((9, 1, levels, NC), lambda i: (0, i, 0, 0))
-    field = jax.ShapeDtypeStruct((3, slabs, levels, NC), jnp.float32)
+    four3 = pl.BlockSpec((3, 1, 4, NC), lambda i: (0, i, 0, 0))
+    edge3 = pl.BlockSpec((3, levels, NC), lambda i: (0, 0, 0))
+    sums3 = pl.BlockSpec((3, levels, LANES), lambda i: (0, 0, 0))
+
+    def shape(*dims):
+        return jax.ShapeDtypeStruct(dims, jnp.float32)
+
+    field = shape(3, slabs, levels, NC)
+    four = shape(3, slabs, 4, NC)
+    edge = shape(3, levels, NC)
     padded = pltpu.VMEM((3, slabs + 2, NJ, ROWS, LANES), jnp.float32)
-
-    low, high, left, right = halos(u)
-    res, rt, grad = pl.pallas_call(
+    work = pl.CostEstimate(flops=30_000_000, bytes_accessed=40_000_000, transcendentals=0)
+    little = pl.CostEstimate(flops=3_000_000, bytes_accessed=6_000_000, transcendentals=0)
+
+    first, last, down, up = pl.pallas_call(
+        pack_kernel,
+        grid=(slabs,),
+        in_specs=[slab3],
+        out_specs=[four3, four3, edge3, edge3],
+        out_shape=[four, four, edge, edge],
+        cost_estimate=little,
+        name="pack",
+    )(u)
+    low, high, left, right = exchange(first, last, down, up)
+    res_part, rt_part, grad = pl.pallas_call(
         lambda *refs: residual_kernel(spacing, *refs),
         grid=(slabs,),
-        in_specs=[smem] + [vmem] * 6,
+        in_specs=[smem, vmem, vmem],
         out_specs=[slab3, slab3, slab9],
-        out_shape=[field, field, jax.ShapeDtypeStruct((9, slabs, levels, NC), jnp.float32)],
+        out_shape=[field, field, shape(9, slabs, levels, NC)],
         scratch_shapes=[padded],
+        cost_estimate=work,
         name="residual",
-    )(scale, u, low, high, left, right, forcing)
-
-    rlow, rhigh, rleft, rright = halos(res)
-    base, sums = pl.pallas_call(
+    )(scale, u, forcing)
+
+    res, first, last, down, up = pl.pallas_call(
+        lambda *refs: joined_kernel(spacing, *refs),
+        grid=(slabs,),
+        in_specs=[smem, slab3, slab1, four3, four3, vmem, vmem],
+        out_specs=[slab3, four3, four3, edge3, edge3],
+        out_shape=[field, four, four, edge, edge],
+        cost_estimate=little,
+        name="joined",
+    )(scale, res_part, u, low, high, left, right)
+    res_low, res_high, res_left, res_right = exchange(first, last, down, up)
+    base_part, rt, partial = pl.pallas_call(
         lambda *refs: descent_kernel(spacing, *refs),
         grid=(slabs,),
-        in_specs=[smem, vmem, slab3, slab9] + [vmem] * 7,
-        out_specs=[slab3, pl.BlockSpec((devices, 1, LANES), lambda i: (0, 0, 0))],
-        out_shape=[field, jax.ShapeDtypeStruct((devices, 1, LANES), jnp.float32)],
+        in_specs=[smem, vmem, vmem, vmem, vmem, slab3, slab9, four3, four3],
+        out_specs=[slab3, slab3, sums3],
+        out_shape=[field, field, shape(3, levels, LANES)],
         scratch_shapes=[
             padded,
             pltpu.VMEM((slabs + 2, levels, NC), jnp.float32),
             pltpu.VMEM((3, levels, LANES), jnp.float32),
         ],
+        cost_estimate=work,
         name="descent",
-    )(scale, u, rt, grad, left[0], right[0], res, rlow, rhigh, rleft, rright)
+    )(scale, u, res, left, right, rt_part, grad, low, high)
+    base, sums = pl.pallas_call(
+        closing_kernel,
+        grid=(slabs,),
+        in_specs=[smem, slab3, slab3, four3, four3, vmem, vmem, vmem],
+        out_specs=[slab3, pl.BlockSpec((devices, 1, LANES), lambda i: (0, 0, 0))],
+        out_shape=[field, shape(devices, 1, LANES)],
+        scratch_shapes=[pltpu.VMEM((8, LANES), jnp.float32)],
+        cost_estimate=little,
+        name="closing",
+    )(scale, base_part, rt, res_low, res_high, res_left, res_right, partial)
 
     gathered = lax.all_to_all(sums, ALL, 0, 0)
     cells = 3.0 * total_levels * grid_first * NY * NZ
@@ -290,7 +467,9 @@
         grid=(slabs,),
         in_specs=[smem, vmem, slab3, slab3],
         out_specs=[slab3, pl.BlockSpec((1, LANES), lambda i: (0, 0))],
-        out_shape=[field, jax.ShapeDtypeStruct((1, LANES), jnp.float32)],
+        out_shape=[field, shape(1, LANES)],
+        scratch_shapes=[pltpu.VMEM((8, LANES), jnp.float32)],
+        cost_estimate=little,
         name="update",
     )(period, gathered, base, rt)
     back = (2, 0, 1, 3)

time: 102 us -> 92.7 us (0.909)
  Pallas kernels: 29.2 us -> 47.7 us
  waiting for transfers between devices: 10.4 us -> 0.02 us
  local copies, waits for them, and re-layouts: 13.6 us -> 3.34 us
  starting transfers between devices: 21.3 us -> 17.3 us
  blocking collectives: 25.3 us -> 21.5 us
    pallas_call x0 -> x3, Pallas kernels: none -> 18.9 us  [the longest x1 6.98 us: on_device(): pl.pallas_call(lambda *refs: joined_kernel(spacing, *refs), grid=(slabs,)...]
    ppermute x8, waiting for transfers between devices: 10.4 us -> 0.02 us  [the longest x2 0.01 us: exchange(): left = lax.ppermute(up, SPACE, space_up)]
    slice x4 -> x0, local copies, waits for them, and re-layouts: 7.23 us -> none  [halo(): first = lax.slice_in_dim(array, 0, width, axis=dim)]
    ppermute x8, starting transfers between devices: 21.3 us -> 17.3 us  [the longest x2 5.94 us: exchange(): right = lax.ppermute(down, SPACE, space_down)]
    all_to_all x1, blocking collectives: 25.3 us -> 21.5 us  [on_device(): gathered = lax.all_to_all(sums, ALL, 0, 0)]
    squeeze x2 -> x0, local copies, waits for them, and re-layouts: 2.29 us -> none  [the longest x1 1.59 us: on_device(): left[0]]
  transfers between devices with their start and end apart: 8 -> 8, of which waited for: 5 -> 0; matrix products, arithmetic and copies ran while one was open for 6% -> 1% of each run, Pallas kernels for 0% -> 25%
where the time goes in v2:
time: 92.7 us; the launch traced here: 91.9 us
  Pallas kernels  47.7 us (51%)
  blocking collectives  21.5 us (23%)
  starting transfers between devices  17.3 us (19%)
  local copies, waits for them, and re-layouts  3.34 us (4%)
  between operations  2.1 us (2%)
    all_to_all x1, blocking collectives, on_device(): gathered = lax.all_to_all(sums, ALL, 0, 0)  21.5 us
    pallas_call x1, Pallas kernels, on_device(): pl.pallas_call(lambda *refs: descent_kernel(spacing, *refs), grid=(slabs,...  13.5 us
    pallas_call x1, Pallas kernels, on_device(): pl.pallas_call(lambda *refs: residual_kernel(spacing, *refs), grid=(slabs...  9.47 us
    pallas_call x1, Pallas kernels, on_device(): pl.pallas_call(lambda *refs: joined_kernel(spacing, *refs), grid=(slabs,)...  6.98 us
    pallas_call x1, Pallas kernels, on_device(): pl.pallas_call(closing_kernel, grid=(slabs,), in_specs=[smem, slab3, slab...  6.87 us
    ppermute x2, starting transfers between devices, exchange(): right = lax.ppermute(down, SPACE, space_down)  5.94 us
    pallas_call x1, Pallas kernels, on_device(): pl.pallas_call(lambda *refs: update_kernel(cells, *refs), grid=(slabs,),...  5.76 us
    ppermute x2, starting transfers between devices, exchange(): low = lax.ppermute(last, TM, tm_up)  5.36 us
  transfers between devices with their start and end apart: 8, of which 0 were waited for; matrix products, arithmetic and copies ran while one was open for 1% of the time, Pallas kernels for 25%

profile of v2, /device:TPU:1, one launch (start us, length us, event | category | flops | bytes accessed | tf_op | source)
XLA Modules:
  0.0 91.9 jit_solution(2295575088644021299)
XLA Ops:
  0.6 5.1 %pack.1 = (f32[3,6,4,2304]{3,2,1,0:T(4,128)}, f32[3,6,4,2304]{3,2,1,0:T(4,128)}, f32[3,16,2304]{2,1,0:T(8,128)}, f32[3,16,2304]{2,1,0:T(8,128)}) custom-call(f32[3,6,16,2304]{3,2,1,0:T(8,128)} %bitcast.6), custom_call_target="tpu_custom_call" | custom-call | flops 3000000 | bytes 6000000 | tf_op jit(solution)/shard_map/pack/pallas_call | solution.py:407
  5.7 3.1 %collective-permute-start = (f32[3,6,4,2304]{3,2,1,0:T(4,128)}, f32[3,6,4,2304]{3,2,1,0:T(4,128)S(1)}, u32[]{:S(2)}, u32[]{:S(2)}) collective-permute-start(f32[3,6,4,2304]{3,2,1,0:T(4,128)} %get-tuple-element.23), channel_id=1, source_target_pairs={{0,8},{8,16},{16,24},{24,32},{32,40},{40,48},{48,56},{56,64},{64,7... | collective-permute-start | bytes 1990664 | tf_op jit(solution)/shard_map/ppermute | solution.py:371
  8.8 1.3 %collective-permute-start.2 = (f32[3,16,2304]{2,1,0:T(8,128)}, f32[3,16,2304]{2,1,0:T(8,128)S(1)}, u32[]{:S(2)}, u32[]{:S(2)}) collective-permute-start(f32[3,16,2304]{2,1,0:T(8,128)} %get-tuple-element.25), channel_id=1, source_target_pairs={{0,1},{1,2},{2,3},{3,4},{4,5},{5,6},{6,7},{7,0},{8,9},{9,10},{10,1... | collective-permute-start | bytes 1327112 | tf_op jit(solution)/shard_map/ppermute | solution.py:369
  10.1 2.4 %collective-permute-start.3 = (f32[3,16,2304]{2,1,0:T(8,128)}, f32[3,16,2304]{2,1,0:T(8,128)S(1)}, u32[]{:S(2)}, u32[]{:S(2)}) collective-permute-start(f32[3,16,2304]{2,1,0:T(8,128)} %get-tuple-element.26), channel_id=1, source_target_pairs={{1,0},{2,1},{3,2},{4,3},{5,4},{6,5},{7,6},{0,7},{9,8},{10,9},{11,1... | collective-permute-start | bytes 1327112 | tf_op jit(solution)/shard_map/ppermute | solution.py:370
  13.8 0.1 broadcast_in_dim.3
  13.9 0.7 reshape_reshape.3.refs_2_
  14.6 9.5 %residual.1 = (f32[3,6,16,2304]{3,2,1,0:T(8,128)}, f32[3,6,16,2304]{3,2,1,0:T(8,128)}, f32[9,6,16,2304]{3,2,1,0:T(8,128)}) custom-call(f32[1]{0:T(128)S(6)} %div.3.refs_0_.scale, f32[3,6,16,2304]{3,2,1,0:T(8,128)} %bitcast.7, f32[1,2304]{1,0:T(1,128)} %reshape_reshape.3.refs_2_), custom_call_target="tpu_custom_call" | custom-call | flops 30000000 | bytes 40000000 | tf_op jit(solution)/shard_map/residual/pallas_call | solution.py:417
  24.1 0.0 collective-permute-done.2.refs_5_.refs_3_
  24.1 0.7 copy-done.2
  24.9 0.1 copy-done.3
  25.0 0.2 copy-done
  25.2 0.2 copy-done.1
  25.4 7.0 %joined.1 = (f32[3,6,16,2304]{3,2,1,0:T(8,128)}, f32[3,6,4,2304]{3,2,1,0:T(4,128)}, f32[3,6,4,2304]{3,2,1,0:T(4,128)}, f32[3,16,2304]{2,1,0:T(8,128)}, f32[3,16,2304]{2,1,0:T(8,128)}) custom-call(f32[1]{0:T(128)S(6)} %div.3.refs_0_.scale, f32[3,6,16,2304]{3,2,1,0:T(8,128)} %get-tuple-element.22.refs_1_, f32[3,6,16,2304]{3,2,1,0:T(8,128)} %bitcast.8, ...), custom_call_target="tpu_custom_call" | custom-call | flops 3000000 | bytes 6000000 | tf_op jit(solution)/shard_map/joined/pallas_call | solution.py:428
  32.4 2.3 %collective-permute-start.4 = (f32[3,6,4,2304]{3,2,1,0:T(4,128)}, f32[3,6,4,2304]{3,2,1,0:T(4,128)S(1)}, u32[]{:S(2)}, u32[]{:S(2)}) collective-permute-start(f32[3,6,4,2304]{3,2,1,0:T(4,128)} %get-tuple-element.32), channel_id=1, source_target_pairs={{0,8},{8,16},{16,24},{24,32},{32,40},{40,48},{48,56},{56,64},{64,7... | collective-permute-start | bytes 1990664 | tf_op jit(solution)/shard_map/ppermute | solution.py:371
  34.7 4.7 %collective-permute-start.5 = (f32[3,6,4,2304]{3,2,1,0:T(4,128)}, f32[3,6,4,2304]{3,2,1,0:T(4,128)S(1)}, u32[]{:S(2)}, u32[]{:S(2)}) collective-permute-start(f32[3,6,4,2304]{3,2,1,0:T(4,128)} %get-tuple-element.33), channel_id=1, source_target_pairs={{8,0},{16,8},{24,16},{32,24},{40,32},{48,40},{56,48},{64,56},{72,6... | collective-permute-start | bytes 1990664 | tf_op jit(solution)/shard_map/ppermute | solution.py:372
  39.4 3.6 %collective-permute-start.7 = (f32[3,16,2304]{2,1,0:T(8,128)}, f32[3,16,2304]{2,1,0:T(8,128)S(1)}, u32[]{:S(2)}, u32[]{:S(2)}) collective-permute-start(f32[3,16,2304]{2,1,0:T(8,128)} %get-tuple-element.35), channel_id=1, source_target_pairs={{1,0},{2,1},{3,2},{4,3},{5,4},{6,5},{7,6},{0,7},{9,8},{10,9},{11,1... | collective-permute-start | bytes 1327112 | tf_op jit(solution)/shard_map/ppermute | solution.py:370
  42.9 13.5 %descent.1 = (f32[3,6,16,2304]{3,2,1,0:T(8,128)}, f32[3,6,16,2304]{3,2,1,0:T(8,128)}, f32[3,16,128]{2,1,0:T(8,128)}) custom-call(f32[1]{0:T(128)S(6)} %div.3.refs_0_.scale, f32[3,6,16,2304]{3,2,1,0:T(8,128)} %bitcast.9, f32[3,6,16,2304]{3,2,1,0:T(8,128)} %get-tuple-element.27.refs_2_, f32[3,16,2304]{2,1,0:T(8,128)} %copy-done.2, f32[3,16,2304]{2,1,0:T(8,128)} %copy-done.3, ...), custom_call_target="tpu_custom_call" | custom-call | flops 30000000 | bytes 40000000 | tf_op jit(solution)/shard_map/descent/pallas_call | solution.py:438
  56.5 0.7 copy-done.6
  57.2 0.2 copy-done.7
  57.4 0.2 copy-done.4
  57.6 0.2 copy-done.5
  57.8 6.9 %closing.1 = (f32[3,6,16,2304]{3,2,1,0:T(8,128)}, f32[128,1,128]{2,1,0:T(1,128)}) custom-call(f32[1]{0:T(128)S(6)} %div.3.refs_0_.scale, f32[3,6,16,2304]{3,2,1,0:T(8,128)} %get-tuple-element.30.part, f32[3,6,16,2304]{3,2,1,0:T(8,128)} %get-tuple-element.31.rt.refs_3_, f32[3,6,4,2304]{3,2,1,0:T(4,128)} %copy-done.4, f32[3,6,4,2304]{3,2,1,0:T(4,128)} %copy-done.5, ...), custom_call_target="tpu_custom_call" | custom-call | flops 3000000 | bytes 6000000 | tf_op jit(solution)/shard_map/closing/pallas_call | solution.py:452
  64.7 21.5 %all_to_all.5.refs_1_ = f32[128,1,128]{2,1,0:T(1,128)} all-to-all(f32[128,1,128]{2,1,0:T(1,128)} %get-tuple-element.37), channel_id=1, replica_groups=mesh['tm_0'=2,'tm_1'=4,'tm_2'=2,'space_0'=2,'space_1'=4] {'tm_0','tm_1',..., dimensions={0} | all-to-all | bytes 131072 | tf_op jit(solution)/shard_map/all_to_all | solution.py:463
  86.2 5.8 %update.1 = (f32[3,6,16,2304]{3,2,1,0:T(8,128)}, f32[1,128]{1,0:T(1,128)}) custom-call(f32[1]{0:T(128)S(6)} %copy.6.refs_0_, f32[128,1,128]{2,1,0:T(1,128)} %all_to_all.5.refs_1_, f32[3,6,16,2304]{3,2,1,0:T(8,128)} %get-tuple-element.38.refs_2_, f32[3,6,16,2304]{3,2,1,0:T(8,128)} %get-tuple-element.31.rt.refs_3_), custom_call_target="tpu_custom_call" | custom-call | flops 3000000 | bytes 6000000 | tf_op jit(solution)/shard_map/update/pallas_call | solution.py:465
  (18 shorter events, 0.1 us)
Async XLA Ops:
  5.7 18.4 %collective-permute-start = (f32[3,6,4,2304]{3,2,1,0:T(4,128)}, f32[3,6,4,2304]{3,2,1,0:T(4,128)S(1)}, u32[]{:S(2)}, u32[]{:S(2)}) collective-permute-start(f32[3,6,4,2304]{3,2,1,0:T(4,128)} %get-tuple-element.23), channel_id=1, source_target_pairs={{0,8},{8,16},{16,24},{24,32},{32,40},{40,48},{48,56},{56,64},{64,7... | collective-permute-start | bytes 1990664 | tf_op jit(solution)/shard_map/ppermute | solution.py:371
  8.8 15.3 %collective-permute-start.1 = (f32[3,6,4,2304]{3,2,1,0:T(4,128)}, f32[3,6,4,2304]{3,2,1,0:T(4,128)S(1)}, u32[]{:S(2)}, u32[]{:S(2)}) collective-permute-start(f32[3,6,4,2304]{3,2,1,0:T(4,128)} %get-tuple-element.24), channel_id=1, source_target_pairs={{8,0},{16,8},{24,16},{32,24},{40,32},{48,40},{56,48},{64,56},{72,6... | collective-permute-start | bytes 1990664 | tf_op jit(solution)/shard_map/ppermute | solution.py:372
  8.8 15.3 %collective-permute-start.2 = (f32[3,16,2304]{2,1,0:T(8,128)}, f32[3,16,2304]{2,1,0:T(8,128)S(1)}, u32[]{:S(2)}, u32[]{:S(2)}) collective-permute-start(f32[3,16,2304]{2,1,0:T(8,128)} %get-tuple-element.25), channel_id=1, source_target_pairs={{0,1},{1,2},{2,3},{3,4},{4,5},{5,6},{6,7},{7,0},{8,9},{9,10},{10,1... | collective-permute-start | bytes 1327112 | tf_op jit(solution)/shard_map/ppermute | solution.py:369
  10.1 14.0 %collective-permute-start.3 = (f32[3,16,2304]{2,1,0:T(8,128)}, f32[3,16,2304]{2,1,0:T(8,128)S(1)}, u32[]{:S(2)}, u32[]{:S(2)}) collective-permute-start(f32[3,16,2304]{2,1,0:T(8,128)} %get-tuple-element.26), channel_id=1, source_target_pairs={{1,0},{2,1},{3,2},{4,3},{5,4},{6,5},{7,6},{0,7},{9,8},{10,9},{11,1... | collective-permute-start | bytes 1327112 | tf_op jit(solution)/shard_map/ppermute | solution.py:370
  24.1 0.8 copy-start.2
  24.1 0.9 copy-start.3
  24.1 1.1 %copy-start = (f32[3,6,4,2304]{3,2,1,0:T(4,128)}, f32[3,6,4,2304]{3,2,1,0:T(4,128)S(1)}, u32[]{:S(2)}) copy-start(f32[3,6,4,2304]{3,2,1,0:T(4,128)S(1)} %collective-permute-done.refs_3_.refs_7_) | copy-start | bytes 1990660
  24.1 1.3 %copy-start.1 = (f32[3,6,4,2304]{3,2,1,0:T(4,128)}, f32[3,6,4,2304]{3,2,1,0:T(4,128)S(1)}, u32[]{:S(2)}) copy-start(f32[3,6,4,2304]{3,2,1,0:T(4,128)S(1)} %collective-permute-done.1.refs_4_.refs_8_) | copy-start | bytes 1990660
  32.4 24.1 %collective-permute-start.4 = (f32[3,6,4,2304]{3,2,1,0:T(4,128)}, f32[3,6,4,2304]{3,2,1,0:T(4,128)S(1)}, u32[]{:S(2)}, u32[]{:S(2)}) collective-permute-start(f32[3,6,4,2304]{3,2,1,0:T(4,128)} %get-tuple-element.32), channel_id=1, source_target_pairs={{0,8},{8,16},{16,24},{24,32},{32,40},{40,48},{48,56},{56,64},{64,7... | collective-permute-start | bytes 1990664 | tf_op jit(solution)/shard_map/ppermute | solution.py:371
  34.7 21.8 %collective-permute-start.5 = (f32[3,6,4,2304]{3,2,1,0:T(4,128)}, f32[3,6,4,2304]{3,2,1,0:T(4,128)S(1)}, u32[]{:S(2)}, u32[]{:S(2)}) collective-permute-start(f32[3,6,4,2304]{3,2,1,0:T(4,128)} %get-tuple-element.33), channel_id=1, source_target_pairs={{8,0},{16,8},{24,16},{32,24},{40,32},{48,40},{56,48},{64,56},{72,6... | collective-permute-start | bytes 1990664 | tf_op jit(solution)/shard_map/ppermute | solution.py:372
  39.4 17.1 %collective-permute-start.6 = (f32[3,16,2304]{2,1,0:T(8,128)}, f32[3,16,2304]{2,1,0:T(8,128)S(1)}, u32[]{:S(2)}, u32[]{:S(2)}) collective-permute-start(f32[3,16,2304]{2,1,0:T(8,128)} %get-tuple-element.34), channel_id=1, source_target_pairs={{0,1},{1,2},{2,3},{3,4},{4,5},{5,6},{6,7},{7,0},{8,9},{9,10},{10,1... | collective-permute-start | bytes 1327112 | tf_op jit(solution)/shard_map/ppermute | solution.py:369
  39.4 17.1 %collective-permute-start.7 = (f32[3,16,2304]{2,1,0:T(8,128)}, f32[3,16,2304]{2,1,0:T(8,128)S(1)}, u32[]{:S(2)}, u32[]{:S(2)}) collective-permute-start(f32[3,16,2304]{2,1,0:T(8,128)} %get-tuple-element.35), channel_id=1, source_target_pairs={{1,0},{2,1},{3,2},{4,3},{5,4},{6,5},{7,6},{0,7},{9,8},{10,9},{11,1... | collective-permute-start | bytes 1327112 | tf_op jit(solution)/shard_map/ppermute | solution.py:370
  56.5 0.8 copy-start.6
  56.5 0.9 copy-start.7
  56.5 1.1 %copy-start.4 = (f32[3,6,4,2304]{3,2,1,0:T(4,128)}, f32[3,6,4,2304]{3,2,1,0:T(4,128)S(1)}, u32[]{:S(2)}) copy-start(f32[3,6,4,2304]{3,2,1,0:T(4,128)S(1)} %collective-permute-done.4.low) | copy-start | bytes 1990660
  56.5 1.3 %copy-start.5 = (f32[3,6,4,2304]{3,2,1,0:T(4,128)}, f32[3,6,4,2304]{3,2,1,0:T(4,128)S(1)}, u32[]{:S(2)}) copy-start(f32[3,6,4,2304]{3,2,1,0:T(4,128)S(1)} %collective-permute-done.5.high) | copy-start | bytes 1990660

commit v3 on v2

--- a/solution.py
+++ b/solution.py
@@ -99,42 +99,51 @@
 
 class Borders:
     def __init__(self, scaled):
-        row = lax.broadcasted_iota(jnp.int32, (8, LANES), 0)
+        row = lax.broadcasted_iota(jnp.int32, (8, LANES), 0) % 4
         zero = jnp.zeros((8, LANES), jnp.float32)
         self.low = [jnp.where(row < m, zero - scaled[m - 1], zero) for m in range(1, 5)]
-        self.high = [jnp.where(row >= 8 - m, zero + scaled[m - 1], zero) for m in range(1, 5)]
-        self.pad = jnp.zeros((4, LANES), jnp.float32)
-
-    def from_low(self, four):
-        eight = jnp.concatenate([four, self.pad], axis=0)
-        total = self.low[3] * eight
+        self.high = [jnp.where(row >= 4 - m, zero + scaled[m - 1], zero) for m in range(1, 5)]
+
+    def pair(self, coefficients, sign, message, c, x, j):
+        eight = jnp.concatenate([message[c, x, :, cols(j)], message[c, x, :, cols(j + 1)]], axis=0)
+        total = coefficients[3] * eight
         for m in range(1, 4):
-            total = total + self.low[m - 1] * pltpu.roll(eight, m + 4, 0)
-        return total
-
-    def from_high(self, four):
-        eight = jnp.concatenate([four, self.pad], axis=0)
-        total = None
-        for m in range(1, 5):
-            term = self.high[m - 1] * pltpu.roll(eight, 8 - m, 0)
-            total = term if total is None else total + term
-        return total
-
-
-def pack_kernel(own, first, last, down, up):
-    levels = own.shape[2]
-    x = pl.program_id(0)
-    for c in range(3):
-        first[c, 0] = own[c, 0, pl.ds(0, 4), :]
-        last[c, 0] = own[c, 0, pl.ds(levels - 4, 4), :]
-
-    @pl.when(x == 0)
-    def _():
-        down[...] = own[:, 0]
-
-    @pl.when(x == pl.num_programs(0) - 1)
-    def _():
-        up[...] = own[:, 0]
+            total = total + coefficients[m - 1] * pltpu.roll(eight, (sign * (4 - m)) % 8, 0)
+        return total[:4], total[4:]
+
+    def from_low(self, message, c, x, j):
+        return self.pair(self.low, -1, message, c, x, j)
+
+    def from_high(self, message, c, x, j):
+        return self.pair(self.high, 1, message, c, x, j)
+
+
+def add_borders(border, ref, low, high, c, x, levels):
+    for j in range(0, NJ, 2):
+        below, above = border.from_low(low, c, x, j), border.from_high(high, c, x, j)
+        for k in range(2):
+            ref[c, x, pl.ds(0, 4), cols(j + k)] += below[k]
+            ref[c, x, pl.ds(levels - 4, 4), cols(j + k)] += above[k]
+
+
+def pack_kernel(own, first, last, down, up, first_buffer, last_buffer, sems):
+    slabs, levels = own.shape[1], own.shape[2]
+    copies = [
+        pltpu.make_async_copy(own.at[:, 0], down, sems.at[0]),
+        pltpu.make_async_copy(own.at[:, slabs - 1], up, sems.at[1]),
+    ]
+    for copy in copies:
+        copy.start()
+    first_buffer[...] = own[:, :, pl.ds(0, 4), :]
+    last_buffer[...] = own[:, :, pl.ds(levels - 4, 4), :]
+    copies += [
+        pltpu.make_async_copy(first_buffer, first, sems.at[2]),
+        pltpu.make_async_copy(last_buffer, last, sems.at[3]),
+    ]
+    for copy in copies[2:]:
+        copy.start()
+    for copy in copies:
+        copy.wait()
 
 
 def residual_kernel(spacing, scale, own, forcing, res, rt, grad, scratch):
@@ -178,45 +187,57 @@
             rt[c, 0, :, cols(j)] = q
 
 
-def joined_kernel(spacing, scale, part, flow, low, high, left, right, res, first, last, down, up):
-    levels = part.shape[2]
-    half = levels - 8
-    x = pl.program_id(0)
+def joined_kernel(spacing, scale, part, own, low, high, left, right, res, first, last, down, up, first_buffer, last_buffer, down_buffer, up_buffer, sems):
+    slabs, levels = own.shape[1], own.shape[2]
     alpha = 1.0 / (2.0 * spacing)
     beta = viscosity / spacing**2
     border = Borders([w * scale[0] for w in weights])
+
+    def slab(x):
+        for c in range(3):
+            res[c, x] = part[c, x]
+            add_borders(border, res, low, high, c, x, levels)
+
+    slab(0)
     for c in range(3):
         for j in range(NJ):
-            res[c, 0, pl.ds(0, 8), cols(j)] = part[c, 0, pl.ds(0, 8), cols(j)] + border.from_low(low[c, 0, :, cols(j)])
-            res[c, 0, pl.ds(half, 8), cols(j)] = part[c, 0, pl.ds(half, 8), cols(j)] + border.from_high(high[c, 0, :, cols(j)])
-
-    @pl.when(x == 0)
-    def _():
-        for c in range(3):
-            for j in range(NJ):
-                plus = alpha * flow[0, 0, :, cols(j)] + beta
-                value = res[c, 0, :, cols(j)] - plus * left[c, :, cols(j)]
-                res[c, 0, :, cols(j)] = value
-                down[c, :, cols(j)] = plus * value
-
-    @pl.when(x == pl.num_programs(0) - 1)
-    def _():
-        for c in range(3):
-            for j in range(NJ):
-                minus = alpha * flow[0, 0, :, cols(j)] - beta
-                value = res[c, 0, :, cols(j)] + minus * right[c, :, cols(j)]
-                res[c, 0, :, cols(j)] = value
-                up[c, :, cols(j)] = minus * value
-
+            plus = alpha * own[0, 0, :, cols(j)] + beta
+            value = res[c, 0, :, cols(j)] - plus * left[c, :, cols(j)]
+            res[c, 0, :, cols(j)] = value
+            down_buffer[c, :, cols(j)] = plus * value
+    copies = [pltpu.make_async_copy(down_buffer, down, sems.at[0])]
+    copies[0].start()
+
+    slab(slabs - 1)
     for c in range(3):
-        first[c, 0] = res[c, 0, pl.ds(0, 4), :]
-        last[c, 0] = res[c, 0, pl.ds(levels - 4, 4), :]
+        for j in range(NJ):
+            minus = alpha * own[0, slabs - 1, :, cols(j)] - beta
+            value = res[c, slabs - 1, :, cols(j)] + minus * right[c, :, cols(j)]
+            res[c, slabs - 1, :, cols(j)] = value
+            up_buffer[c, :, cols(j)] = minus * value
+    copies += [pltpu.make_async_copy(up_buffer, up, sems.at[1])]
+    copies[1].start()
+
+    def inner(x, carry):
+        slab(x)
+        return carry
+
+    lax.fori_loop(1, slabs - 1, inner, 0)
+    first_buffer[...] = res[:, :, pl.ds(0, 4), :]
+    last_buffer[...] = res[:, :, pl.ds(levels - 4, 4), :]
+    copies += [
+        pltpu.make_async_copy(first_buffer, first, sems.at[2]),
+        pltpu.make_async_copy(last_buffer, last, sems.at[3]),
+    ]
+    for copy in copies[2:]:
+        copy.start()
+    for copy in copies:
+        copy.wait()
 
 
 def descent_kernel(spacing, scale, own, res, left, right, part, grad, low, high, base, rt, sums, scratch, flow, acc):
     levels = own.shape[2]
     slabs = own.shape[1]
-    half = levels - 8
     x = pl.program_id(0)
     alpha = 1.0 / (2.0 * spacing)
     beta = viscosity / spacing**2
@@ -236,10 +257,9 @@
 
     scaled = [w * scale[0] for w in weights]
     border = Borders(scaled)
+    rt[...] = part[...]
     for c in range(3):
-        for j in range(NJ):
-            rt[c, 0, pl.ds(0, 8), cols(j)] = part[c, 0, pl.ds(0, 8), cols(j)] + border.from_low(low[c, 0, :, cols(j)])
-            rt[c, 0, pl.ds(half, 8), cols(j)] = part[c, 0, pl.ds(half, 8), cols(j)] + border.from_high(high[c, 0, :, cols(j)])
+        add_borders(border, rt, low, high, c, 0, levels)
 
     sh = Shifts((levels, LANES))
     is_first = jnp.where(x == 0, 1.0, 0.0).astype(jnp.float32)
@@ -296,65 +316,59 @@
         sums[...] = acc[...]
 
 
-def closing_kernel(scale, part, rt, low, high, left, right, partial, base, sums, acc):
-    levels = part.shape[2]
-    half = levels - 8
-    x = pl.program_id(0)
-
-    @pl.when(x == 0)
-    def _():
-        acc[...] = jnp.zeros_like(acc)
-
+def closing_kernel(scale, part, rt, low, high, left, right, partial, base, sums):
+    slabs, levels = part.shape[1], part.shape[2]
     border = Borders([w * scale[0] for w in weights])
-    total = jnp.zeros((8, LANES), jnp.float32)
-    for c in range(3):
-        for j in range(NJ):
-            for rows, take in (((0, 8), border.from_low(low[c, 0, :, cols(j)])), ((half, 8), border.from_high(high[c, 0, :, cols(j)]))):
-                rows = pl.ds(*rows)
-                total = total - take * rt[c, 0, rows, cols(j)]
-                base[c, 0, rows, cols(j)] = part[c, 0, rows, cols(j)] + step_size * take
-    acc[...] += total
-
-    def edge(sign, message):
+
+    def slab(x, total):
+        for c in range(3):
+            base[c, x] = part[c, x]
+            for j in range(0, NJ, 2):
+                below, above = border.from_low(low, c, x, j), border.from_high(high, c, x, j)
+                for k in range(2):
+                    for row, take in ((0, below[k]), (levels - 4, above[k])):
+                        rows = pl.ds(row, 4)
+                        total = total - take * rt[c, x, rows, cols(j + k)]
+                        base[c, x, rows, cols(j + k)] += step_size * take
+        return total
+
+    inner = lax.fori_loop(0, slabs, slab, jnp.zeros((4, LANES), jnp.float32))
+
+    def edge(sign, message, x):
         total = jnp.zeros((levels, LANES), jnp.float32)
         for c in range(3):
             for j in range(NJ):
                 extra = message[c, :, cols(j)]
-                total = total + extra * rt[c, 0, :, cols(j)]
-                base[c, 0, :, cols(j)] = base[c, 0, :, cols(j)] - (sign * step_size) * extra
-        acc[...] += sign * (total[:8] + total[half:])
-
-    @pl.when(x == 0)
-    def _():
-        edge(1.0, left)
-
-    @pl.when(x == pl.num_programs(0) - 1)
-    def _():
-        edge(-1.0, right)
-        lane = lax.broadcasted_iota(jnp.int32, (1, LANES), 1)
-        row = jnp.zeros((1, LANES), jnp.float32)
-        for k in range(3):
-            value = jnp.sum(partial[k]) if k < 2 else jnp.sum(partial[k]) + jnp.sum(acc[...])
-            row = jnp.where(lane == k, value, row)
-        sums[...] = jnp.broadcast_to(row[None], sums.shape)
-
-
-def update_kernel(cells, period, gathered, base, rt, out, pgrad, weight):
-    @pl.when(pl.program_id(0) == 0)
-    def _():
-        row = jnp.sum(gathered[...], axis=0)
-        s1, s2, s3 = row[0, 0], row[0, 1], row[0, 2]
-        ratio = jnp.full((1, LANES), step_size * s3, jnp.float32) / jnp.full((1, LANES), s2, jnp.float32)
-        weight[...] = jnp.broadcast_to(ratio, weight.shape)
-        pgrad[...] = jnp.full((1, LANES), -s1, jnp.float32) / jnp.full((1, LANES), period[0] * cells, jnp.float32)
-
-    factor = weight[...]
-    levels = base.shape[2]
-    for c in range(3):
-        for j in range(NJ):
-            for row in range(0, levels, 8):
-                rows = pl.ds(row, 8)
-                out[c, 0, rows, cols(j)] = base[c, 0, rows, cols(j)] + factor * rt[c, 0, rows, cols(j)]
+                total = total + extra * rt[c, x, :, cols(j)]
+                base[c, x, :, cols(j)] = base[c, x, :, cols(j)] - (sign * step_size) * extra
+        return sign * total
+
+    outer = edge(1.0, left, 0) + edge(-1.0, right, slabs - 1)
+    lane = lax.broadcasted_iota(jnp.int32, (1, LANES), 1)
+    row = jnp.zeros((1, LANES), jnp.float32)
+    for k in range(3):
+        value = jnp.sum(partial[k]) if k < 2 else jnp.sum(partial[k] + outer) + jnp.sum(inner)
+        row = jnp.where(lane == k, value, row)
+    sums[...] = jnp.broadcast_to(row[None], sums.shape)
+
+
+def update_kernel(cells, period, gathered, base, rt, out, pgrad, buffer, sem):
+    slabs, levels = base.shape[1], base.shape[2]
+    row = jnp.sum(gathered[...], axis=0)
+    s1, s2, s3 = row[0, 0], row[0, 1], row[0, 2]
+    ratio = jnp.full((1, LANES), step_size * s3, jnp.float32) / jnp.full((1, LANES), s2, jnp.float32)
+    factor = jnp.broadcast_to(ratio, (levels, LANES))
+    pgrad[...] = jnp.full((1, LANES), -s1, jnp.float32) / jnp.full((1, LANES), period[0] * cells, jnp.float32)
+
+    def slab(x, carry):
+        for c in range(3):
+            for j in range(NJ):
+                buffer[c, x, :, cols(j)] = base[c, x, :, cols(j)] + factor * rt[c, x, :, cols(j)]
+        pltpu.make_async_copy(buffer.at[:, x], out.at[:, x], sem).start()
+        return carry
+
+    lax.fori_loop(0, slabs, slab, 0)
+    pltpu.make_async_copy(buffer, out, sem).wait()
 
 
 def ring(axis):
@@ -387,29 +401,34 @@
 
     vmem = pl.BlockSpec(memory_space=pltpu.VMEM)
     smem = pl.BlockSpec(memory_space=pltpu.SMEM)
-    slab1 = pl.BlockSpec((1, 1, levels, NC), lambda i: (0, i, 0, 0))
+    hbm = pl.BlockSpec(memory_space=pl.ANY)
     slab3 = pl.BlockSpec((3, 1, levels, NC), lambda i: (0, i, 0, 0))
     slab9 = pl.BlockSpec((9, 1, levels, NC), lambda i: (0, i, 0, 0))
     four3 = pl.BlockSpec((3, 1, 4, NC), lambda i: (0, i, 0, 0))
-    edge3 = pl.BlockSpec((3, levels, NC), lambda i: (0, 0, 0))
     sums3 = pl.BlockSpec((3, levels, LANES), lambda i: (0, 0, 0))
 
     def shape(*dims):
         return jax.ShapeDtypeStruct(dims, jnp.float32)
+
+    def params(mib):
+        return pltpu.CompilerParams(vmem_limit_bytes=mib << 20)
 
     field = shape(3, slabs, levels, NC)
     four = shape(3, slabs, 4, NC)
     edge = shape(3, levels, NC)
+    four_buffer = pltpu.VMEM((3, slabs, 4, NC), jnp.float32)
+    edge_buffer = pltpu.VMEM((3, levels, NC), jnp.float32)
     padded = pltpu.VMEM((3, slabs + 2, NJ, ROWS, LANES), jnp.float32)
     work = pl.CostEstimate(flops=30_000_000, bytes_accessed=40_000_000, transcendentals=0)
     little = pl.CostEstimate(flops=3_000_000, bytes_accessed=6_000_000, transcendentals=0)
 
     first, last, down, up = pl.pallas_call(
         pack_kernel,
-        grid=(slabs,),
-        in_specs=[slab3],
-        out_specs=[four3, four3, edge3, edge3],
+        in_specs=[vmem],
+        out_specs=[hbm] * 4,
         out_shape=[four, four, edge, edge],
+        scratch_shapes=[four_buffer, four_buffer, pltpu.SemaphoreType.DMA((4,))],
+        compiler_params=params(8),
         cost_estimate=little,
         name="pack",
     )(u)
@@ -421,16 +440,18 @@
         out_specs=[slab3, slab3, slab9],
         out_shape=[field, field, shape(9, slabs, levels, NC)],
         scratch_shapes=[padded],
+        compiler_params=params(20),
         cost_estimate=work,
         name="residual",
     )(scale, u, forcing)
 
     res, first, last, down, up = pl.pallas_call(
         lambda *refs: joined_kernel(spacing, *refs),
-        grid=(slabs,),
-        in_specs=[smem, slab3, slab1, four3, four3, vmem, vmem],
-        out_specs=[slab3, four3, four3, edge3, edge3],
+        in_specs=[smem] + [vmem] * 6,
+        out_specs=[vmem] + [hbm] * 4,
         out_shape=[field, four, four, edge, edge],
+        scratch_shapes=[four_buffer, four_buffer, edge_buffer, edge_buffer, pltpu.SemaphoreType.DMA((4,))],
+        compiler_params=params(18),
         cost_estimate=little,
         name="joined",
     )(scale, res_part, u, low, high, left, right)
@@ -446,16 +467,16 @@
             pltpu.VMEM((slabs + 2, levels, NC), jnp.float32),
             pltpu.VMEM((3, levels, LANES), jnp.float32),
         ],
+        compiler_params=params(26),
         cost_estimate=work,
         name="descent",
     )(scale, u, res, left, right, rt_part, grad, low, high)
     base, sums = pl.pallas_call(
         closing_kernel,
-        grid=(slabs,),
-        in_specs=[smem, slab3, slab3, four3, four3, vmem, vmem, vmem],
-        out_specs=[slab3, pl.BlockSpec((devices, 1, LANES), lambda i: (0, 0, 0))],
+        in_specs=[smem] + [vmem] * 7,
+        out_specs=[vmem, vmem],
         out_shape=[field, shape(devices, 1, LANES)],
-        scratch_shapes=[pltpu.VMEM((8, LANES), jnp.float32)],
+        compiler_params=params(16),
         cost_estimate=little,
         name="closing",
     )(scale, base_part, rt, res_low, res_high, res_left, res_right, partial)
@@ -464,11 +485,11 @@
     cells = 3.0 * total_levels * grid_first * NY * NZ
     updated, pgrad = pl.pallas_call(
         lambda *refs: update_kernel(cells, *refs),
-        grid=(slabs,),
-        in_specs=[smem, vmem, slab3, slab3],
-        out_specs=[slab3, pl.BlockSpec((1, LANES), lambda i: (0, 0))],
+        in_specs=[smem, vmem, vmem, vmem],
+        out_specs=[hbm, vmem],
         out_shape=[field, shape(1, LANES)],
-        scratch_shapes=[pltpu.VMEM((8, LANES), jnp.float32)],
+        scratch_shapes=[pltpu.VMEM((3, slabs, levels, NC), jnp.float32), pltpu.SemaphoreType.DMA],
+        compiler_params=params(14),
         cost_estimate=little,
         name="update",
     )(period, gathered, base, rt)

time: 92.7 us -> 76 us (0.82)
  Pallas kernels: 47.7 us -> 25.5 us
  starting transfers between devices: 17.3 us -> 19.7 us
  waiting for transfers between devices: 0.02 us -> 1.85 us
  blocking collectives: 21.5 us -> 22.9 us
    pallas_call x4, Pallas kernels: 24.7 us -> 9.82 us  [the longest x1 4.8 us: on_device(): pl.pallas_call(lambda *refs: joined_kernel(spacing, *refs), in_specs=[sme...]
    pallas_call x1, Pallas kernels: 13.5 us -> 9.81 us  [on_device(): pl.pallas_call(lambda *refs: descent_kernel(spacing, *refs), grid=(slabs,...]
    pallas_call x1, Pallas kernels: 9.47 us -> 5.86 us  [on_device(): pl.pallas_call(lambda *refs: residual_kernel(spacing, *refs), grid=(slabs...]
    ppermute x2, waiting for transfers between devices: 0.01 us -> 1.84 us  [exchange(): right = lax.ppermute(down, SPACE, space_down)]
    ppermute x2, starting transfers between devices: 5.36 us -> 6.82 us  [exchange(): low = lax.ppermute(last, TM, tm_up)]
    all_to_all x1, blocking collectives: 21.5 us -> 22.9 us  [on_device(): gathered = lax.all_to_all(sums, ALL, 0, 0)]
    ppermute x2, starting transfers between devices: 4.67 us -> 5.67 us  [exchange(): high = lax.ppermute(first, TM, tm_down)]
    unnamed x16 -> x6, local copies, waits for them, and re-layouts: 2.58 us -> 3.5 us
  transfers between devices with their start and end apart: 8 -> 8, of which waited for: 0 -> 1; matrix products, arithmetic and copies ran while one was open for 1% -> 0% of each run, Pallas kernels for 25% -> 21%
where the time goes in v3:
time: 76 us; the launch traced here: 75.8 us
  Pallas kernels  25.5 us (34%)
  blocking collectives  22.9 us (30%)
  starting transfers between devices  19.7 us (26%)
  local copies, waits for them, and re-layouts  3.66 us (5%)
  between operations  2.09 us (3%)
  waiting for transfers between devices  1.85 us (2%)
    all_to_all x1, blocking collectives, on_device(): gathered = lax.all_to_all(sums, ALL, 0, 0)  22.9 us
    pallas_call x1, Pallas kernels, on_device(): pl.pallas_call(lambda *refs: descent_kernel(spacing, *refs), grid=(slabs,...  9.81 us
    ppermute x2, starting transfers between devices, exchange(): low = lax.ppermute(last, TM, tm_up)  6.82 us
    ppermute x2, starting transfers between devices, exchange(): right = lax.ppermute(down, SPACE, space_down)  5.94 us
    pallas_call x1, Pallas kernels, on_device(): pl.pallas_call(lambda *refs: residual_kernel(spacing, *refs), grid=(slabs...  5.86 us
    ppermute x2, starting transfers between devices, exchange(): high = lax.ppermute(first, TM, tm_down)  5.67 us
    pallas_call x1, Pallas kernels, on_device(): pl.pallas_call(lambda *refs: joined_kernel(spacing, *refs), in_specs=[sme...  4.8 us
    unnamed x6, local copies, waits for them, and re-layouts  3.5 us
  transfers between devices with their start and end apart: 8, of which 1 were waited for; matrix products, arithmetic and copies ran while one was open for 0% of the time, Pallas kernels for 21%

profile of v3, /device:TPU:1, one launch (start us, length us, event | category | flops | bytes accessed | tf_op | source)
XLA Modules:
  0.0 75.8 jit_solution(15263091295912339273)
XLA Ops:
  0.6 1.7 %copy-done = f32[16,3,6,2304]{3,0,2,1:T(8,128)S(1)} copy-done((f32[16,3,6,2304]{3,0,2,1:T(8,128)S(1)}, f32[16,3,6,2304]{3,0,2,1:T(8,128)}, u32[]{:S(2)}) %copy-start) | copy-done | bytes 2654232
  2.4 1.4 %pack.1 = (f32[3,6,4,2304]{3,2,1,0:T(4,128)}, f32[3,6,4,2304]{3,2,1,0:T(4,128)}, f32[3,16,2304]{2,1,0:T(8,128)}, f32[3,16,2304]{2,1,0:T(8,128)}) custom-call(f32[3,6,16,2304]{3,2,1,0:T(8,128)S(1)} %bitcast.6), custom_call_target="tpu_custom_call" | custom-call | flops 3000000 | bytes 6000000 | tf_op jit(solution)/shard_map/pack/pallas_call | solution.py:425
  3.8 3.1 %collective-permute-start = (f32[3,6,4,2304]{3,2,1,0:T(4,128)}, f32[3,6,4,2304]{3,2,1,0:T(4,128)S(1)}, u32[]{:S(2)}, u32[]{:S(2)}) collective-permute-start(f32[3,6,4,2304]{3,2,1,0:T(4,128)} %get-tuple-element.23), channel_id=1, source_target_pairs={{0,8},{8,16},{16,24},{24,32},{32,40},{40,48},{48,56},{56,64},{64,7... | collective-permute-start | bytes 1990664 | tf_op jit(solution)/shard_map/ppermute | solution.py:385
  6.9 0.0 collective-permute-start.1
  6.9 1.3 %collective-permute-start.2 = (f32[3,16,2304]{2,1,0:T(8,128)}, f32[3,16,2304]{2,1,0:T(8,128)}, u32[]{:S(2)}, u32[]{:S(2)}) collective-permute-start(f32[3,16,2304]{2,1,0:T(8,128)} %get-tuple-element.25), channel_id=1, source_target_pairs={{0,1},{1,2},{2,3},{3,4},{4,5},{5,6},{6,7},{7,0},{8,9},{9,10},{10,1... | collective-permute-start | bytes 1327112 | tf_op jit(solution)/shard_map/ppermute | solution.py:383
  8.2 2.4 %collective-permute-start.3 = (f32[3,16,2304]{2,1,0:T(8,128)}, f32[3,16,2304]{2,1,0:T(8,128)}, u32[]{:S(2)}, u32[]{:S(2)}) collective-permute-start(f32[3,16,2304]{2,1,0:T(8,128)} %get-tuple-element.26), channel_id=1, source_target_pairs={{1,0},{2,1},{3,2},{4,3},{5,4},{6,5},{7,6},{0,7},{9,8},{10,9},{11,1... | collective-permute-start | bytes 1327112 | tf_op jit(solution)/shard_map/ppermute | solution.py:384
  11.9 0.1 broadcast_in_dim.3
  11.9 0.1 reshape_reshape.3.refs_2_
  12.1 5.9 %residual.1 = (f32[3,6,16,2304]{3,2,1,0:T(8,128)S(1)}, f32[3,6,16,2304]{3,2,1,0:T(8,128)S(1)}, f32[9,6,16,2304]{3,2,1,0:T(8,128)S(1)}) custom-call(f32[1]{0:T(128)S(6)} %div.3.refs_0_.scale, f32[3,6,16,2304]{3,2,1,0:T(8,128)S(1)} %bitcast.7, f32[1,2304]{1,0:T(1,128)S(1)} %reshape_reshape.3.refs_2_), custom_call_target="tpu_custom_call" | custom-call | flops 30000000 | bytes 40000000 | tf_op jit(solution)/shard_map/residual/pallas_call | solution.py:436
  18.0 0.0 collective-permute-done.2.refs_5_.refs_3_
  18.0 1.8 %collective-permute-done.3.refs_6_.refs_4_ = f32[3,16,2304]{2,1,0:T(8,128)} collective-permute-done((f32[3,16,2304]{2,1,0:T(8,128)}, f32[3,16,2304]{2,1,0:T(8,128)}, u32[]{:S(2)}, u32[]{:S(2)}) %collective-permute-start.3) | collective-permute-done | bytes 442400 | tf_op jit(solution)/shard_map/ppermute | solution.py:384
  19.8 0.0 collective-permute-done.refs_3_.refs_7_
  19.8 0.0 collective-permute-done.1.refs_4_.refs_8_
  19.8 4.8 %joined.1 = (f32[3,6,16,2304]{3,2,1,0:T(8,128)}, f32[3,6,4,2304]{3,2,1,0:T(4,128)S(1)}, f32[3,6,4,2304]{3,2,1,0:T(4,128)S(1)}, f32[3,16,2304]{2,1,0:T(8,128)S(1)}, f32[3,16,2304]{2,1,0:T(8,128)S(1)}) custom-call(f32[1]{0:T(128)S(6)} %div.3.refs_0_.scale, f32[3,6,16,2304]{3,2,1,0:T(8,128)S(1)} %get-tuple-element.22.refs_1_, f32[3,6,16,2304]{3,2,1,0:T(8,128)S(1)} %bitcast.8, ...), custom_call_target="tpu_custom_call" | custom-call | flops 3000000 | bytes 6000000 | tf_op jit(solution)/shard_map/joined/pallas_call | solution.py:448
  24.6 3.7 %collective-permute-start.4 = (f32[3,6,4,2304]{3,2,1,0:T(4,128)S(1)}, f32[3,6,4,2304]{3,2,1,0:T(4,128)S(1)}, u32[]{:S(2)}, u32[]{:S(2)}) collective-permute-start(f32[3,6,4,2304]{3,2,1,0:T(4,128)S(1)} %get-tuple-element.32), channel_id=1, source_target_pairs={{0,8},{8,16},{16,24},{24,32},{32,40},{40,48},{48,56},{56,64},{64,7... | collective-permute-start | bytes 1990664 | tf_op jit(solution)/shard_map/ppermute | solution.py:385
  28.4 5.7 %collective-permute-start.5 = (f32[3,6,4,2304]{3,2,1,0:T(4,128)S(1)}, f32[3,6,4,2304]{3,2,1,0:T(4,128)S(1)}, u32[]{:S(2)}, u32[]{:S(2)}) collective-permute-start(f32[3,6,4,2304]{3,2,1,0:T(4,128)S(1)} %get-tuple-element.33), channel_id=1, source_target_pairs={{8,0},{16,8},{24,16},{32,24},{40,32},{48,40},{56,48},{64,56},{72,6... | collective-permute-start | bytes 1990664 | tf_op jit(solution)/shard_map/ppermute | solution.py:386
  34.0 0.0 collective-permute-start.6
  34.0 3.6 %collective-permute-start.7 = (f32[3,16,2304]{2,1,0:T(8,128)S(1)}, f32[3,16,2304]{2,1,0:T(8,128)S(1)}, u32[]{:S(2)}, u32[]{:S(2)}) collective-permute-start(f32[3,16,2304]{2,1,0:T(8,128)S(1)} %get-tuple-element.35), channel_id=1, source_target_pairs={{1,0},{2,1},{3,2},{4,3},{5,4},{6,5},{7,6},{0,7},{9,8},{10,9},{11,1... | collective-permute-start | bytes 1327112 | tf_op jit(solution)/shard_map/ppermute | solution.py:384
  37.6 1.7 %copy-done.2 = f32[3,6,16,2304]{3,2,1,0:T(8,128)S(1)} copy-done((f32[3,6,16,2304]{3,2,1,0:T(8,128)S(1)}, f32[3,6,16,2304]{3,2,1,0:T(8,128)}, u32[]{:S(2)}) %copy-start.2) | copy-done | bytes 2654232
  39.4 9.8 %descent.1 = (f32[3,6,16,2304]{3,2,1,0:T(8,128)S(1)}, f32[3,6,16,2304]{3,2,1,0:T(8,128)S(1)}, f32[3,16,128]{2,1,0:T(8,128)S(1)}) custom-call(f32[1]{0:T(128)S(6)} %div.3.refs_0_.scale, f32[3,6,16,2304]{3,2,1,0:T(8,128)S(1)} %bitcast.9, f32[3,6,16,2304]{3,2,1,0:T(8,128)S(1)} %copy-done.2, f32[3,16,2304]{2,1,0:T(8,128)} %collective-permute-done.2.refs_5_.refs_3_, ...), custom_call_target="tpu_custom_call" | custom-call | flops 30000000 | bytes 40000000 | tf_op jit(solution)/shard_map/descent/pallas_call | solution.py:459
  49.2 0.0 collective-permute-done.6.left
  49.2 1.3 %closing.1 = (f32[3,6,16,2304]{3,2,1,0:T(8,128)S(1)}, f32[128,1,128]{2,1,0:T(1,128)S(1)}) custom-call(f32[1]{0:T(128)S(6)} %div.3.refs_0_.scale, f32[3,6,16,2304]{3,2,1,0:T(8,128)S(1)} %get-tuple-element.30.part, f32[3,6,16,2304]{3,2,1,0:T(8,128)S(1)} %get-tuple-element.31.rt.refs_3_, f32[3,6,4,2304]{3,2,1,0:T(4,128)S(1)} %collective-permute-done.4.low, ...), custom_call_target="tpu_custom_call" | custom-call | flops 3000000 | bytes 6000000 | tf_op jit(solution)/shard_map/closing/pallas_call | solution.py:474
  50.6 22.9 %all_to_all.5.refs_1_ = f32[128,1,128]{2,1,0:T(1,128)S(1)} all-to-all(f32[128,1,128]{2,1,0:T(1,128)S(1)} %get-tuple-element.37), channel_id=1, replica_groups=mesh['tm_0'=2,'tm_1'=4,'tm_2'=2,'space_0'=2,'space_1'=4] {'tm_0','tm_1',..., dimensions={0} | all-to-all | bytes 131072 | tf_op jit(solution)/shard_map/all_to_all | solution.py:484
  73.5 2.3 %update.1 = (f32[3,6,16,2304]{3,2,1,0:T(8,128)}, f32[1,128]{1,0:T(1,128)}) custom-call(f32[1]{0:T(128)S(6)} %copy.6.refs_0_, f32[128,1,128]{2,1,0:T(1,128)S(1)} %all_to_all.5.refs_1_, f32[3,6,16,2304]{3,2,1,0:T(8,128)S(1)} %get-tuple-element.38.refs_2_, f32[3,6,16,2304]{3,2,1,0:T(8,128)S(1)} %get-tuple-element.31.rt.refs_3_), custom_call_target="tpu_custom_call" | custom-call | flops 3000000 | bytes 6000000 | tf_op jit(solution)/shard_map/update/pallas_call | solution.py:486
  (8 shorter events, 0.1 us)
Async XLA Ops:
  0.6 1.8 %copy-start = (f32[16,3,6,2304]{3,0,2,1:T(8,128)S(1)}, f32[16,3,6,2304]{3,0,2,1:T(8,128)}, u32[]{:S(2)}) copy-start(f32[16,3,6,2304]{3,0,2,1:T(8,128)} %param.3) | copy-start | bytes 7962628
  2.4 9.7 %copy-start.1 = (f32[16,3,6,2304]{3,0,2,1:T(8,128)S(1)}, f32[16,3,6,2304]{3,0,2,1:T(8,128)}, u32[]{:S(2)}) copy-start(f32[16,3,6,2304]{3,0,2,1:T(8,128)} %param.3) | copy-start | bytes 7962628
  3.8 16.1 %collective-permute-start = (f32[3,6,4,2304]{3,2,1,0:T(4,128)}, f32[3,6,4,2304]{3,2,1,0:T(4,128)S(1)}, u32[]{:S(2)}, u32[]{:S(2)}) collective-permute-start(f32[3,6,4,2304]{3,2,1,0:T(4,128)} %get-tuple-element.23), channel_id=1, source_target_pairs={{0,8},{8,16},{16,24},{24,32},{32,40},{40,48},{48,56},{56,64},{64,7... | collective-permute-start | bytes 1990664 | tf_op jit(solution)/shard_map/ppermute | solution.py:385
  6.9 13.0 %collective-permute-start.1 = (f32[3,6,4,2304]{3,2,1,0:T(4,128)}, f32[3,6,4,2304]{3,2,1,0:T(4,128)}, u32[]{:S(2)}, u32[]{:S(2)}) collective-permute-start(f32[3,6,4,2304]{3,2,1,0:T(4,128)} %get-tuple-element.24), channel_id=1, source_target_pairs={{8,0},{16,8},{24,16},{32,24},{40,32},{48,40},{56,48},{64,56},{72,6... | collective-permute-start | bytes 1990664 | tf_op jit(solution)/shard_map/ppermute | solution.py:386
  6.9 11.1 %collective-permute-start.2 = (f32[3,16,2304]{2,1,0:T(8,128)}, f32[3,16,2304]{2,1,0:T(8,128)}, u32[]{:S(2)}, u32[]{:S(2)}) collective-permute-start(f32[3,16,2304]{2,1,0:T(8,128)} %get-tuple-element.25), channel_id=1, source_target_pairs={{0,1},{1,2},{2,3},{3,4},{4,5},{5,6},{6,7},{7,0},{8,9},{9,10},{10,1... | collective-permute-start | bytes 1327112 | tf_op jit(solution)/shard_map/ppermute | solution.py:383
  8.2 11.7 %collective-permute-start.3 = (f32[3,16,2304]{2,1,0:T(8,128)}, f32[3,16,2304]{2,1,0:T(8,128)}, u32[]{:S(2)}, u32[]{:S(2)}) collective-permute-start(f32[3,16,2304]{2,1,0:T(8,128)} %get-tuple-element.26), channel_id=1, source_target_pairs={{1,0},{2,1},{3,2},{4,3},{5,4},{6,5},{7,6},{0,7},{9,8},{10,9},{11,1... | collective-permute-start | bytes 1327112 | tf_op jit(solution)/shard_map/ppermute | solution.py:384
  24.6 24.6 %collective-permute-start.4 = (f32[3,6,4,2304]{3,2,1,0:T(4,128)S(1)}, f32[3,6,4,2304]{3,2,1,0:T(4,128)S(1)}, u32[]{:S(2)}, u32[]{:S(2)}) collective-permute-start(f32[3,6,4,2304]{3,2,1,0:T(4,128)S(1)} %get-tuple-element.32), channel_id=1, source_target_pairs={{0,8},{8,16},{16,24},{24,32},{32,40},{40,48},{48,56},{56,64},{64,7... | collective-permute-start | bytes 1990664 | tf_op jit(solution)/shard_map/ppermute | solution.py:385
  28.4 20.8 %collective-permute-start.5 = (f32[3,6,4,2304]{3,2,1,0:T(4,128)S(1)}, f32[3,6,4,2304]{3,2,1,0:T(4,128)S(1)}, u32[]{:S(2)}, u32[]{:S(2)}) collective-permute-start(f32[3,6,4,2304]{3,2,1,0:T(4,128)S(1)} %get-tuple-element.33), channel_id=1, source_target_pairs={{8,0},{16,8},{24,16},{32,24},{40,32},{48,40},{56,48},{64,56},{72,6... | collective-permute-start | bytes 1990664 | tf_op jit(solution)/shard_map/ppermute | solution.py:386
  34.0 15.1 %collective-permute-start.6 = (f32[3,16,2304]{2,1,0:T(8,128)S(1)}, f32[3,16,2304]{2,1,0:T(8,128)S(1)}, u32[]{:S(2)}, u32[]{:S(2)}) collective-permute-start(f32[3,16,2304]{2,1,0:T(8,128)S(1)} %get-tuple-element.34), channel_id=1, source_target_pairs={{0,1},{1,2},{2,3},{3,4},{4,5},{5,6},{6,7},{7,0},{8,9},{9,10},{10,1... | collective-permute-start | bytes 1327112 | tf_op jit(solution)/shard_map/ppermute | solution.py:383
  34.0 15.2 %collective-permute-start.7 = (f32[3,16,2304]{2,1,0:T(8,128)S(1)}, f32[3,16,2304]{2,1,0:T(8,128)S(1)}, u32[]{:S(2)}, u32[]{:S(2)}) collective-permute-start(f32[3,16,2304]{2,1,0:T(8,128)S(1)} %get-tuple-element.35), channel_id=1, source_target_pairs={{1,0},{2,1},{3,2},{4,3},{5,4},{6,5},{7,6},{0,7},{9,8},{10,9},{11,1... | collective-permute-start | bytes 1327112 | tf_op jit(solution)/shard_map/ppermute | solution.py:384
  37.6 1.7 %copy-start.2 = (f32[3,6,16,2304]{3,2,1,0:T(8,128)S(1)}, f32[3,6,16,2304]{3,2,1,0:T(8,128)}, u32[]{:S(2)}) copy-start(f32[3,6,16,2304]{3,2,1,0:T(8,128)} %get-tuple-element.27.refs_2_) | copy-start | bytes 7962628

commit v4 on v3

--- a/solution.py
+++ b/solution.py
@@ -7,6 +7,7 @@
 from jax.experimental.pallas import tpu as pltpu
 from jax.sharding import Mesh
 from jax.sharding import PartitionSpec as P
+
 
 NY = 48
 NZ = 48
@@ -126,24 +127,22 @@
             ref[c, x, pl.ds(levels - 4, 4), cols(j + k)] += above[k]
 
 
-def pack_kernel(own, first, last, down, up, first_buffer, last_buffer, sems):
-    slabs, levels = own.shape[1], own.shape[2]
+def edges_kernel(own, down, up, sems):
+    slabs = own.shape[1]
     copies = [
-        pltpu.make_async_copy(own.at[:, 0], down, sems.at[0]),
-        pltpu.make_async_copy(own.at[:, slabs - 1], up, sems.at[1]),
+        pltpu.make_async_copy(own.at[:, slabs - 1], up, sems.at[0]),
+        pltpu.make_async_copy(own.at[:, 0], down, sems.at[1]),
     ]
     for copy in copies:
         copy.start()
-    first_buffer[...] = own[:, :, pl.ds(0, 4), :]
-    last_buffer[...] = own[:, :, pl.ds(levels - 4, 4), :]
-    copies += [
-        pltpu.make_async_copy(first_buffer, first, sems.at[2]),
-        pltpu.make_async_copy(last_buffer, last, sems.at[3]),
-    ]
-    for copy in copies[2:]:
-        copy.start()
     for copy in copies:
         copy.wait()
+
+
+def ends_kernel(own, first, last):
+    levels = own.shape[2]
+    first[...] = own[:, :, pl.ds(0, 4), :]
+    last[...] = own[:, :, pl.ds(levels - 4, 4), :]
 
 
 def residual_kernel(spacing, scale, own, forcing, res, rt, grad, scratch):
@@ -187,55 +186,34 @@
             rt[c, 0, :, cols(j)] = q
 
 
-def joined_kernel(spacing, scale, part, own, low, high, left, right, res, first, last, down, up, first_buffer, last_buffer, down_buffer, up_buffer, sems):
+def joined_kernel(spacing, scale, part, own, low, high, left, right, res, first, last, down, up):
     slabs, levels = own.shape[1], own.shape[2]
     alpha = 1.0 / (2.0 * spacing)
     beta = viscosity / spacing**2
     border = Borders([w * scale[0] for w in weights])
 
-    def slab(x):
+    def slab(x, carry):
         for c in range(3):
             res[c, x] = part[c, x]
             add_borders(border, res, low, high, c, x, levels)
-
-    slab(0)
+        return carry
+
+    lax.fori_loop(0, slabs, slab, 0)
     for c in range(3):
         for j in range(NJ):
             plus = alpha * own[0, 0, :, cols(j)] + beta
             value = res[c, 0, :, cols(j)] - plus * left[c, :, cols(j)]
             res[c, 0, :, cols(j)] = value
-            down_buffer[c, :, cols(j)] = plus * value
-    copies = [pltpu.make_async_copy(down_buffer, down, sems.at[0])]
-    copies[0].start()
-
-    slab(slabs - 1)
-    for c in range(3):
-        for j in range(NJ):
+            down[c, :, cols(j)] = plus * value
             minus = alpha * own[0, slabs - 1, :, cols(j)] - beta
             value = res[c, slabs - 1, :, cols(j)] + minus * right[c, :, cols(j)]
             res[c, slabs - 1, :, cols(j)] = value
-            up_buffer[c, :, cols(j)] = minus * value
-    copies += [pltpu.make_async_copy(up_buffer, up, sems.at[1])]
-    copies[1].start()
-
-    def inner(x, carry):
-        slab(x)
-        return carry
-
-    lax.fori_loop(1, slabs - 1, inner, 0)
-    first_buffer[...] = res[:, :, pl.ds(0, 4), :]
-    last_buffer[...] = res[:, :, pl.ds(levels - 4, 4), :]
-    copies += [
-        pltpu.make_async_copy(first_buffer, first, sems.at[2]),
-        pltpu.make_async_copy(last_buffer, last, sems.at[3]),
-    ]
-    for copy in copies[2:]:
-        copy.start()
-    for copy in copies:
-        copy.wait()
-
-
-def descent_kernel(spacing, scale, own, res, left, right, part, grad, low, high, base, rt, sums, scratch, flow, acc):
+            up[c, :, cols(j)] = minus * value
+    first[...] = res[:, :, pl.ds(0, 4), :]
+    last[...] = res[:, :, pl.ds(levels - 4, 4), :]
+
+
+def descent_kernel(spacing, scale, own, res, left, right, part, grad, low, high, base, rt, sums, res_out, scratch, flow, acc, sem):
     levels = own.shape[2]
     slabs = own.shape[1]
     x = pl.program_id(0)
@@ -244,6 +222,7 @@
 
     @pl.when(x == 0)
     def _():
+        pltpu.make_async_copy(res, res_out, sem).start()
         fill(scratch, res)
         flow[0] = jnp.zeros_like(flow[0])
         flow[slabs + 1] = jnp.zeros_like(flow[0])
@@ -284,9 +263,9 @@
 
         for j in range(NJ):
             here = at(c, 0, j)
-            (yp0, ym0, zp0, zm0) = products(j - 1)
+            (_, ym0, zp0, zm0) = products(j - 1)
             (yp1, ym1, zp1, zm1) = products(j)
-            (yp2, ym2, zp2, zm2) = products(j + 1)
+            (yp2, _, zp2, zm2) = products(j + 1)
             total = (6.0 * beta) * here - rate(scratch, c, x + 1, j, levels, scaled)
             nxt, prv = at(c, 1, j), at(c, -1, j)
             total = total - (flow[x + 2, :, cols(j)] + beta) * nxt
@@ -314,6 +293,7 @@
     @pl.when(x == slabs - 1)
     def _():
         sums[...] = acc[...]
+        pltpu.make_async_copy(res, res_out, sem).wait()
 
 
 def closing_kernel(scale, part, rt, low, high, left, right, partial, base, sums):
@@ -387,7 +367,7 @@
     return low, high, left, right
 
 
-def on_device(velocity, period, wavenumber):
+def step(velocity, period, wavenumber):
     levels, _, slabs, _ = velocity.shape
     devices = lax.axis_size(ALL)
     total_levels = levels * lax.axis_size(TM)
@@ -416,21 +396,28 @@
     field = shape(3, slabs, levels, NC)
     four = shape(3, slabs, 4, NC)
     edge = shape(3, levels, NC)
-    four_buffer = pltpu.VMEM((3, slabs, 4, NC), jnp.float32)
-    edge_buffer = pltpu.VMEM((3, levels, NC), jnp.float32)
     padded = pltpu.VMEM((3, slabs + 2, NJ, ROWS, LANES), jnp.float32)
     work = pl.CostEstimate(flops=30_000_000, bytes_accessed=40_000_000, transcendentals=0)
     little = pl.CostEstimate(flops=3_000_000, bytes_accessed=6_000_000, transcendentals=0)
 
-    first, last, down, up = pl.pallas_call(
-        pack_kernel,
+    down, up = pl.pallas_call(
+        edges_kernel,
+        in_specs=[pl.BlockSpec(memory_space=pltpu.HBM)],
+        out_specs=[vmem] * 2,
+        out_shape=[edge, edge],
+        scratch_shapes=[pltpu.SemaphoreType.DMA((2,))],
+        compiler_params=params(60),
+        cost_estimate=little,
+        name="edges",
+    )(u)
+    first, last = pl.pallas_call(
+        ends_kernel,
         in_specs=[vmem],
-        out_specs=[hbm] * 4,
-        out_shape=[four, four, edge, edge],
-        scratch_shapes=[four_buffer, four_buffer, pltpu.SemaphoreType.DMA((4,))],
+        out_specs=[vmem] * 2,
+        out_shape=[four, four],
         compiler_params=params(8),
         cost_estimate=little,
-        name="pack",
+        name="ends",
     )(u)
     low, high, left, right = exchange(first, last, down, up)
     res_part, rt_part, grad = pl.pallas_call(
@@ -440,7 +427,7 @@
         out_specs=[slab3, slab3, slab9],
         out_shape=[field, field, shape(9, slabs, levels, NC)],
         scratch_shapes=[padded],
-        compiler_params=params(20),
+        compiler_params=params(16),
         cost_estimate=work,
         name="residual",
     )(scale, u, forcing)
@@ -448,26 +435,26 @@
     res, first, last, down, up = pl.pallas_call(
         lambda *refs: joined_kernel(spacing, *refs),
         in_specs=[smem] + [vmem] * 6,
-        out_specs=[vmem] + [hbm] * 4,
+        out_specs=[vmem] * 5,
         out_shape=[field, four, four, edge, edge],
-        scratch_shapes=[four_buffer, four_buffer, edge_buffer, edge_buffer, pltpu.SemaphoreType.DMA((4,))],
         compiler_params=params(18),
         cost_estimate=little,
         name="joined",
     )(scale, res_part, u, low, high, left, right)
     res_low, res_high, res_left, res_right = exchange(first, last, down, up)
-    base_part, rt, partial = pl.pallas_call(
+    base_part, rt, partial, res_out = pl.pallas_call(
         lambda *refs: descent_kernel(spacing, *refs),
         grid=(slabs,),
         in_specs=[smem, vmem, vmem, vmem, vmem, slab3, slab9, four3, four3],
-        out_specs=[slab3, slab3, sums3],
-        out_shape=[field, field, shape(3, levels, LANES)],
+        out_specs=[slab3, slab3, sums3, hbm],
+        out_shape=[field, field, shape(3, levels, LANES), field],
         scratch_shapes=[
             padded,
             pltpu.VMEM((slabs + 2, levels, NC), jnp.float32),
             pltpu.VMEM((3, levels, LANES), jnp.float32),
+            pltpu.SemaphoreType.DMA,
         ],
-        compiler_params=params(26),
+        compiler_params=params(22),
         cost_estimate=work,
         name="descent",
     )(scale, u, res, left, right, rt_part, grad, low, high)
@@ -494,11 +481,11 @@
         name="update",
     )(period, gathered, base, rt)
     back = (2, 0, 1, 3)
-    return jnp.transpose(updated, back), jnp.transpose(res, back), pgrad[0, :1]
+    return jnp.transpose(updated, back), jnp.transpose(res_out, back), pgrad[0, :1]
 
 
 def solution(mesh):
     split = Mesh(mesh.devices.reshape(2, 4, 2, 2, 4), ALL)
     in_specs = (P(TM, None, SPACE, None), P(), P())
     out_specs = (P(TM, None, SPACE, None), P(TM, None, SPACE, None), P())
-    return jax.shard_map(on_device, mesh=split, in_specs=in_specs, out_specs=out_specs, check_vma=False)
+    return jax.shard_map(step, mesh=split, in_specs=in_specs, out_specs=out_specs, check_vma=False)

time: 76 us -> 75.4 us (level)
  local copies, waits for them, and re-layouts: 3.66 us -> 1.92 us
  blocking collectives: 22.9 us -> 24.6 us
  waiting for transfers between devices: 1.85 us -> 2.87 us
  starting transfers between devices: 19.7 us -> 18.7 us
    unnamed x6 -> x4, local copies, waits for them, and re-layouts: 3.5 us -> 1.75 us
    all_to_all x1, blocking collectives: 22.9 us -> 24.6 us  [step(): gathered = lax.all_to_all(sums, ALL, 0, 0)]
    ppermute x2, waiting for transfers between devices: 0.01 us -> 1.37 us  [exchange(): left = lax.ppermute(up, SPACE, space_up)]
    ppermute x2, starting transfers between devices: 6.82 us -> 5.67 us  [exchange(): low = lax.ppermute(last, TM, tm_up)]
    pallas_call x6 -> x7, Pallas kernels: 25.5 us -> 24.9 us  [the longest x1 9.83 us: step(): pl.pallas_call(lambda *refs: descent_kernel(spacing, *refs), grid=(slabs,...]
  transfers between devices with their start and end apart: 8 -> 8, of which waited for: 1 -> 2; matrix products, arithmetic and copies ran while one was open for 0% -> 0% of each run, Pallas kernels for 21% -> 24%
where the time goes in v4:
time: 75.4 us; the launch traced here: 75.2 us
  Pallas kernels  24.9 us (33%)
  blocking collectives  24.6 us (33%)
  starting transfers between devices  18.7 us (25%)
  waiting for transfers between devices  2.87 us (4%)
  between operations  2.08 us (3%)
  local copies, waits for them, and re-layouts  1.92 us (3%)
    all_to_all x1, blocking collectives, step(): gathered = lax.all_to_all(sums, ALL, 0, 0)  24.6 us
    pallas_call x1, Pallas kernels, step(): pl.pallas_call(lambda *refs: descent_kernel(spacing, *refs), grid=(slabs,...  9.83 us
    ppermute x2, starting transfers between devices, exchange(): right = lax.ppermute(down, SPACE, space_down)  6.02 us
    pallas_call x1, Pallas kernels, step(): pl.pallas_call(lambda *refs: residual_kernel(spacing, *refs), grid=(slabs...  5.86 us
    ppermute x2, starting transfers between devices, exchange(): high = lax.ppermute(first, TM, tm_down)  5.67 us
    ppermute x2, starting transfers between devices, exchange(): low = lax.ppermute(last, TM, tm_up)  5.67 us
    pallas_call x1, Pallas kernels, step(): pl.pallas_call(lambda *refs: joined_kernel(spacing, *refs), in_specs=[sme...  2.38 us
    pallas_call x1, Pallas kernels, step(): pl.pallas_call(lambda *refs: update_kernel(cells, *refs), in_specs=[smem,...  2.31 us
  transfers between devices with their start and end apart: 8, of which 2 were waited for; matrix products, arithmetic and copies ran while one was open for 0% of the time, Pallas kernels for 24%

profile of v4, /device:TPU:1, one launch (start us, length us, event | category | flops | bytes accessed | tf_op | source)
XLA Modules:
  0.0 75.2 jit_solution(1006930490216667434)
XLA Ops:
  0.6 0.0 copy-start
  0.6 1.7 %copy-done = f32[16,3,6,2304]{3,0,2,1:T(8,128)S(1)} copy-done((f32[16,3,6,2304]{3,0,2,1:T(8,128)S(1)}, f32[16,3,6,2304]{3,0,2,1:T(8,128)}, u32[]{:S(2)}) %copy-start) | copy-done | bytes 2654232
  2.4 1.1 %ends.1 = (f32[3,6,4,2304]{3,2,1,0:T(4,128)}, f32[3,6,4,2304]{3,2,1,0:T(4,128)}) custom-call(f32[3,6,16,2304]{3,2,1,0:T(8,128)S(1)} %bitcast.7), custom_call_target="tpu_custom_call" | custom-call | flops 3000000 | bytes 6000000 | tf_op jit(solution)/shard_map/ends/pallas_call | solution.py:413
  3.5 3.0 %collective-permute-start = (f32[3,6,4,2304]{3,2,1,0:T(4,128)}, f32[3,6,4,2304]{3,2,1,0:T(4,128)S(1)}, u32[]{:S(2)}, u32[]{:S(2)}) collective-permute-start(f32[3,6,4,2304]{3,2,1,0:T(4,128)} %get-tuple-element.24), channel_id=1, source_target_pairs={{0,8},{8,16},{16,24},{24,32},{32,40},{40,48},{48,56},{56,64},{64,7... | collective-permute-start | bytes 1990664 | tf_op jit(solution)/shard_map/ppermute | solution.py:365
  6.6 2.1 %edges.1 = (f32[3,16,2304]{2,1,0:T(8,128)}, f32[3,16,2304]{2,1,0:T(8,128)}) custom-call(f32[3,6,16,2304]{3,2,1,0:T(8,128)} %bitcast.6), custom_call_target="tpu_custom_call" | custom-call | flops 3000000 | bytes 6000000 | tf_op jit(solution)/shard_map/edges/pallas_call | solution.py:403
  8.6 1.4 %collective-permute-start.2 = (f32[3,16,2304]{2,1,0:T(8,128)}, f32[3,16,2304]{2,1,0:T(8,128)}, u32[]{:S(2)}, u32[]{:S(2)}) collective-permute-start(f32[3,16,2304]{2,1,0:T(8,128)} %get-tuple-element.26), channel_id=1, source_target_pairs={{0,1},{1,2},{2,3},{3,4},{4,5},{5,6},{6,7},{7,0},{8,9},{9,10},{10,1... | collective-permute-start | bytes 1327112 | tf_op jit(solution)/shard_map/ppermute | solution.py:363
  10.0 2.4 %collective-permute-start.3 = (f32[3,16,2304]{2,1,0:T(8,128)}, f32[3,16,2304]{2,1,0:T(8,128)}, u32[]{:S(2)}, u32[]{:S(2)}) collective-permute-start(f32[3,16,2304]{2,1,0:T(8,128)} %get-tuple-element.27), channel_id=1, source_target_pairs={{1,0},{2,1},{3,2},{4,3},{5,4},{6,5},{7,6},{0,7},{9,8},{10,9},{11,1... | collective-permute-start | bytes 1327112 | tf_op jit(solution)/shard_map/ppermute | solution.py:364
  13.8 0.1 broadcast_in_dim.3
  13.9 0.1 reshape_reshape.3.refs_2_
  14.0 5.9 %residual.1 = (f32[3,6,16,2304]{3,2,1,0:T(8,128)S(1)}, f32[3,6,16,2304]{3,2,1,0:T(8,128)S(1)}, f32[9,6,16,2304]{3,2,1,0:T(8,128)S(1)}) custom-call(f32[1]{0:T(128)S(6)} %div.3.refs_0_.scale, f32[3,6,16,2304]{3,2,1,0:T(8,128)S(1)} %bitcast.8, f32[1,2304]{1,0:T(1,128)S(1)} %reshape_reshape.3.refs_2_), custom_call_target="tpu_custom_call" | custom-call | flops 30000000 | bytes 40000000 | tf_op jit(solution)/shard_map/residual/pallas_call | solution.py:423
  19.9 1.4 %collective-permute-done.2.refs_5_.refs_3_ = f32[3,16,2304]{2,1,0:T(8,128)} collective-permute-done((f32[3,16,2304]{2,1,0:T(8,128)}, f32[3,16,2304]{2,1,0:T(8,128)}, u32[]{:S(2)}, u32[]{:S(2)}) %collective-permute-start.2) | collective-permute-done | bytes 442400 | tf_op jit(solution)/shard_map/ppermute | solution.py:363
  21.3 1.5 %collective-permute-done.3.refs_6_.refs_4_ = f32[3,16,2304]{2,1,0:T(8,128)} collective-permute-done((f32[3,16,2304]{2,1,0:T(8,128)}, f32[3,16,2304]{2,1,0:T(8,128)}, u32[]{:S(2)}, u32[]{:S(2)}) %collective-permute-start.3) | collective-permute-done | bytes 442400 | tf_op jit(solution)/shard_map/ppermute | solution.py:364
  22.8 0.0 collective-permute-done.refs_3_.refs_7_
  22.8 0.0 collective-permute-done.1.refs_4_.refs_8_
  22.8 2.4 %joined.1 = (f32[3,6,16,2304]{3,2,1,0:T(8,128)S(1)}, f32[3,6,4,2304]{3,2,1,0:T(4,128)S(1)}, f32[3,6,4,2304]{3,2,1,0:T(4,128)S(1)}, f32[3,16,2304]{2,1,0:T(8,128)S(1)}, f32[3,16,2304]{2,1,0:T(8,128)S(1)}) custom-call(f32[1]{0:T(128)S(6)} %div.3.refs_0_.scale, f32[3,6,16,2304]{3,2,1,0:T(8,128)S(1)} %get-tuple-element.23.refs_1_, ...), custom_call_target="tpu_custom_call" | custom-call | flops 3000000 | bytes 6000000 | tf_op jit(solution)/shard_map/joined/pallas_call | solution.py:435
  25.1 2.7 %collective-permute-start.4 = (f32[3,6,4,2304]{3,2,1,0:T(4,128)S(1)}, f32[3,6,4,2304]{3,2,1,0:T(4,128)S(1)}, u32[]{:S(2)}, u32[]{:S(2)}) collective-permute-start(f32[3,6,4,2304]{3,2,1,0:T(4,128)S(1)} %get-tuple-element.33), channel_id=1, source_target_pairs={{0,8},{8,16},{16,24},{24,32},{32,40},{40,48},{48,56},{56,64},{64,7... | collective-permute-start | bytes 1990664 | tf_op jit(solution)/shard_map/ppermute | solution.py:365
  27.8 5.7 %collective-permute-start.5 = (f32[3,6,4,2304]{3,2,1,0:T(4,128)S(1)}, f32[3,6,4,2304]{3,2,1,0:T(4,128)S(1)}, u32[]{:S(2)}, u32[]{:S(2)}) collective-permute-start(f32[3,6,4,2304]{3,2,1,0:T(4,128)S(1)} %get-tuple-element.34), channel_id=1, source_target_pairs={{8,0},{16,8},{24,16},{32,24},{40,32},{48,40},{56,48},{64,56},{72,6... | collective-permute-start | bytes 1990664 | tf_op jit(solution)/shard_map/ppermute | solution.py:366
  33.5 0.0 collective-permute-start.6
  33.5 3.6 %collective-permute-start.7 = (f32[3,16,2304]{2,1,0:T(8,128)S(1)}, f32[3,16,2304]{2,1,0:T(8,128)S(1)}, u32[]{:S(2)}, u32[]{:S(2)}) collective-permute-start(f32[3,16,2304]{2,1,0:T(8,128)S(1)} %get-tuple-element.36), channel_id=1, source_target_pairs={{1,0},{2,1},{3,2},{4,3},{5,4},{6,5},{7,6},{0,7},{9,8},{10,9},{11,1... | collective-permute-start | bytes 1327112 | tf_op jit(solution)/shard_map/ppermute | solution.py:364
  37.0 9.8 %descent.1 = (f32[3,6,16,2304]{3,2,1,0:T(8,128)S(1)}, f32[3,6,16,2304]{3,2,1,0:T(8,128)S(1)}, f32[3,16,128]{2,1,0:T(8,128)S(1)}, f32[3,6,16,2304]{3,2,1,0:T(8,128)}) custom-call(f32[1]{0:T(128)S(6)} %div.3.refs_0_.scale, f32[3,6,16,2304]{3,2,1,0:T(8,128)S(1)} %bitcast.10, f32[3,6,16,2304]{3,2,1,0:T(8,128)S(1)} %get-tuple-element.28.refs_2_, ...), custom_call_target="tpu_custom_call" | custom-call | flops 30000000 | bytes 40000000 | tf_op jit(solution)/shard_map/descent/pallas_call | solution.py:445
  46.9 0.0 collective-permute-done.6.left
  46.9 1.3 %closing.1 = (f32[3,6,16,2304]{3,2,1,0:T(8,128)S(1)}, f32[128,1,128]{2,1,0:T(1,128)S(1)}) custom-call(f32[1]{0:T(128)S(6)} %div.3.refs_0_.scale, f32[3,6,16,2304]{3,2,1,0:T(8,128)S(1)} %get-tuple-element.31.part, f32[3,6,16,2304]{3,2,1,0:T(8,128)S(1)} %get-tuple-element.32.rt.refs_3_, f32[3,6,4,2304]{3,2,1,0:T(4,128)S(1)} %collective-permute-done.4.low, ...), custom_call_target="tpu_custom_call" | custom-call | flops 3000000 | bytes 6000000 | tf_op jit(solution)/shard_map/closing/pallas_call | solution.py:461
  48.3 24.6 %all_to_all.5.refs_1_ = f32[128,1,128]{2,1,0:T(1,128)S(1)} all-to-all(f32[128,1,128]{2,1,0:T(1,128)S(1)} %get-tuple-element.38), channel_id=1, replica_groups=mesh['tm_0'=2,'tm_1'=4,'tm_2'=2,'space_0'=2,'space_1'=4] {'tm_0','tm_1',..., dimensions={0} | all-to-all | bytes 131072 | tf_op jit(solution)/shard_map/all_to_all | solution.py:471
  72.9 2.3 %update.1 = (f32[3,6,16,2304]{3,2,1,0:T(8,128)}, f32[1,128]{1,0:T(1,128)}) custom-call(f32[1]{0:T(128)S(6)} %copy.6.refs_0_, f32[128,1,128]{2,1,0:T(1,128)S(1)} %all_to_all.5.refs_1_, f32[3,6,16,2304]{3,2,1,0:T(8,128)S(1)} %get-tuple-element.39.refs_2_, f32[3,6,16,2304]{3,2,1,0:T(8,128)S(1)} %get-tuple-element.32.rt.refs_3_), custom_call_target="tpu_custom_call" | custom-call | flops 3000000 | bytes 6000000 | tf_op jit(solution)/shard_map/update/pallas_call | solution.py:473
  (7 shorter events, 0.1 us)
Async XLA Ops:
  0.6 1.8 %copy-start = (f32[16,3,6,2304]{3,0,2,1:T(8,128)S(1)}, f32[16,3,6,2304]{3,0,2,1:T(8,128)}, u32[]{:S(2)}) copy-start(f32[16,3,6,2304]{3,0,2,1:T(8,128)} %param.3) | copy-start | bytes 7962628
  2.4 11.6 %copy-start.1 = (f32[16,3,6,2304]{3,0,2,1:T(8,128)S(1)}, f32[16,3,6,2304]{3,0,2,1:T(8,128)}, u32[]{:S(2)}) copy-start(f32[16,3,6,2304]{3,0,2,1:T(8,128)} %param.3) | copy-start | bytes 7962628
  3.5 19.2 %collective-permute-start = (f32[3,6,4,2304]{3,2,1,0:T(4,128)}, f32[3,6,4,2304]{3,2,1,0:T(4,128)S(1)}, u32[]{:S(2)}, u32[]{:S(2)}) collective-permute-start(f32[3,6,4,2304]{3,2,1,0:T(4,128)} %get-tuple-element.24), channel_id=1, source_target_pairs={{0,8},{8,16},{16,24},{24,32},{32,40},{40,48},{48,56},{56,64},{64,7... | collective-permute-start | bytes 1990664 | tf_op jit(solution)/shard_map/ppermute | solution.py:365
  6.5 16.2 %collective-permute-start.1 = (f32[3,6,4,2304]{3,2,1,0:T(4,128)}, f32[3,6,4,2304]{3,2,1,0:T(4,128)}, u32[]{:S(2)}, u32[]{:S(2)}) collective-permute-start(f32[3,6,4,2304]{3,2,1,0:T(4,128)} %get-tuple-element.25), channel_id=1, source_target_pairs={{8,0},{16,8},{24,16},{32,24},{40,32},{48,40},{56,48},{64,56},{72,6... | collective-permute-start | bytes 1990664 | tf_op jit(solution)/shard_map/ppermute | solution.py:366
  8.6 12.6 %collective-permute-start.2 = (f32[3,16,2304]{2,1,0:T(8,128)}, f32[3,16,2304]{2,1,0:T(8,128)}, u32[]{:S(2)}, u32[]{:S(2)}) collective-permute-start(f32[3,16,2304]{2,1,0:T(8,128)} %get-tuple-element.26), channel_id=1, source_target_pairs={{0,1},{1,2},{2,3},{3,4},{4,5},{5,6},{6,7},{7,0},{8,9},{9,10},{10,1... | collective-permute-start | bytes 1327112 | tf_op jit(solution)/shard_map/ppermute | solution.py:363
  10.0 12.8 %collective-permute-start.3 = (f32[3,16,2304]{2,1,0:T(8,128)}, f32[3,16,2304]{2,1,0:T(8,128)}, u32[]{:S(2)}, u32[]{:S(2)}) collective-permute-start(f32[3,16,2304]{2,1,0:T(8,128)} %get-tuple-element.27), channel_id=1, source_target_pairs={{1,0},{2,1},{3,2},{4,3},{5,4},{6,5},{7,6},{0,7},{9,8},{10,9},{11,1... | collective-permute-start | bytes 1327112 | tf_op jit(solution)/shard_map/ppermute | solution.py:364
  25.1 21.8 %collective-permute-start.4 = (f32[3,6,4,2304]{3,2,1,0:T(4,128)S(1)}, f32[3,6,4,2304]{3,2,1,0:T(4,128)S(1)}, u32[]{:S(2)}, u32[]{:S(2)}) collective-permute-start(f32[3,6,4,2304]{3,2,1,0:T(4,128)S(1)} %get-tuple-element.33), channel_id=1, source_target_pairs={{0,8},{8,16},{16,24},{24,32},{32,40},{40,48},{48,56},{56,64},{64,7... | collective-permute-start | bytes 1990664 | tf_op jit(solution)/shard_map/ppermute | solution.py:365
  27.8 19.1 %collective-permute-start.5 = (f32[3,6,4,2304]{3,2,1,0:T(4,128)S(1)}, f32[3,6,4,2304]{3,2,1,0:T(4,128)S(1)}, u32[]{:S(2)}, u32[]{:S(2)}) collective-permute-start(f32[3,6,4,2304]{3,2,1,0:T(4,128)S(1)} %get-tuple-element.34), channel_id=1, source_target_pairs={{8,0},{16,8},{24,16},{32,24},{40,32},{48,40},{56,48},{64,56},{72,6... | collective-permute-start | bytes 1990664 | tf_op jit(solution)/shard_map/ppermute | solution.py:366
  33.5 13.4 %collective-permute-start.6 = (f32[3,16,2304]{2,1,0:T(8,128)S(1)}, f32[3,16,2304]{2,1,0:T(8,128)S(1)}, u32[]{:S(2)}, u32[]{:S(2)}) collective-permute-start(f32[3,16,2304]{2,1,0:T(8,128)S(1)} %get-tuple-element.35), channel_id=1, source_target_pairs={{0,1},{1,2},{2,3},{3,4},{4,5},{5,6},{6,7},{7,0},{8,9},{9,10},{10,1... | collective-permute-start | bytes 1327112 | tf_op jit(solution)/shard_map/ppermute | solution.py:363
  33.5 13.4 %collective-permute-start.7 = (f32[3,16,2304]{2,1,0:T(8,128)S(1)}, f32[3,16,2304]{2,1,0:T(8,128)S(1)}, u32[]{:S(2)}, u32[]{:S(2)}) collective-permute-start(f32[3,16,2304]{2,1,0:T(8,128)S(1)} %get-tuple-element.36), channel_id=1, source_target_pairs={{1,0},{2,1},{3,2},{4,3},{5,4},{6,5},{7,6},{0,7},{9,8},{10,9},{11,1... | collective-permute-start | bytes 1327112 | tf_op jit(solution)/shard_map/ppermute | solution.py:364

commit v5 on v4

--- a/solution.py
+++ b/solution.py
@@ -127,11 +127,30 @@
             ref[c, x, pl.ds(levels - 4, 4), cols(j + k)] += above[k]
 
 
-def edges_kernel(own, down, up, sems):
+def level_parity():
+    return lax.axis_index(TM[-1])
+
+
+def slab_parity():
+    return lax.rem(lax.axis_index(SPACE[-1]), 2)
+
+
+def by_parity(parity, body, odd, even):
+    @pl.when(parity == 1)
+    def _():
+        body(even, odd)
+
+    @pl.when(parity == 0)
+    def _():
+        body(odd, even)
+
+
+def edges_kernel(own, odd, even, sems):
     slabs = own.shape[1]
+    upper = slab_parity() * (slabs - 1)
     copies = [
-        pltpu.make_async_copy(own.at[:, slabs - 1], up, sems.at[0]),
-        pltpu.make_async_copy(own.at[:, 0], down, sems.at[1]),
+        pltpu.make_async_copy(own.at[:, upper], odd, sems.at[0]),
+        pltpu.make_async_copy(own.at[:, slabs - 1 - upper], even, sems.at[1]),
     ]
     for copy in copies:
         copy.start()
@@ -139,21 +158,32 @@
         copy.wait()
 
 
-def ends_kernel(own, first, last):
+def ends_kernel(own, odd, even):
     levels = own.shape[2]
-    first[...] = own[:, :, pl.ds(0, 4), :]
-    last[...] = own[:, :, pl.ds(levels - 4, 4), :]
-
-
-def residual_kernel(spacing, scale, own, forcing, res, rt, grad, scratch):
+
+    def body(first, last):
+        first[...] = own[:, :, pl.ds(0, 4), :]
+        last[...] = own[:, :, pl.ds(levels - 4, 4), :]
+
+    by_parity(level_parity(), body, odd, even)
+
+
+def residual_kernel(spacing, total_levels, period, wavenumber, own, res, rt, grad, scratch, forcing, factors):
     levels = own.shape[2]
     x = pl.program_id(0)
 
     @pl.when(x == 0)
     def _():
         fill(scratch, own)
-
-    scaled = [w * scale[0] for w in weights]
+        inverse_step = (total_levels / jnp.broadcast_to(period[...], (1, LANES)))[0, 0]
+        for m in range(4):
+            factors[m] = weights[m] * inverse_step
+        turn = jnp.broadcast_to(wavenumber[...], (1, LANES)).astype(jnp.float32) * (2.0 * math.pi / NY)
+        lane = lax.broadcasted_iota(jnp.int32, (1, LANES), 1).astype(jnp.float32)
+        for j in range(NJ):
+            forcing[:, cols(j)] = jnp.sin(turn * jnp.floor((lane + (j * LANES + 0.5)) * (1.0 / NZ)))
+
+    scaled = [factors[m] for m in range(4)]
     alpha = 1.0 / (2.0 * spacing)
     beta = viscosity / spacing**2
     sh = Shifts((levels, LANES))
@@ -186,34 +216,46 @@
             rt[c, 0, :, cols(j)] = q
 
 
-def joined_kernel(spacing, scale, part, own, low, high, left, right, res, first, last, down, up):
+def joined_kernel(spacing, scale, part, own, tm_odd, tm_even, space_odd, space_even, res, out_tm_odd, out_tm_even, out_space_odd, out_space_even):
     slabs, levels = own.shape[1], own.shape[2]
     alpha = 1.0 / (2.0 * spacing)
     beta = viscosity / spacing**2
     border = Borders([w * scale[0] for w in weights])
 
-    def slab(x, carry):
+    def inner(low, high):
+        def slab(x, carry):
+            for c in range(3):
+                res[c, x] = part[c, x]
+                add_borders(border, res, low, high, c, x, levels)
+            return carry
+
+        lax.fori_loop(0, slabs, slab, 0)
+
+    by_parity(level_parity(), inner, tm_odd, tm_even)
+
+    def outer(lower, upper):
+        (left, down), (right, up) = lower, upper
         for c in range(3):
-            res[c, x] = part[c, x]
-            add_borders(border, res, low, high, c, x, levels)
-        return carry
-
-    lax.fori_loop(0, slabs, slab, 0)
-    for c in range(3):
-        for j in range(NJ):
-            plus = alpha * own[0, 0, :, cols(j)] + beta
-            value = res[c, 0, :, cols(j)] - plus * left[c, :, cols(j)]
-            res[c, 0, :, cols(j)] = value
-            down[c, :, cols(j)] = plus * value
-            minus = alpha * own[0, slabs - 1, :, cols(j)] - beta
-            value = res[c, slabs - 1, :, cols(j)] + minus * right[c, :, cols(j)]
-            res[c, slabs - 1, :, cols(j)] = value
-            up[c, :, cols(j)] = minus * value
-    first[...] = res[:, :, pl.ds(0, 4), :]
-    last[...] = res[:, :, pl.ds(levels - 4, 4), :]
-
-
-def descent_kernel(spacing, scale, own, res, left, right, part, grad, low, high, base, rt, sums, res_out, scratch, flow, acc, sem):
+            for j in range(NJ):
+                plus = alpha * own[0, 0, :, cols(j)] + beta
+                value = res[c, 0, :, cols(j)] - plus * left[c, :, cols(j)]
+                res[c, 0, :, cols(j)] = value
+                down[c, :, cols(j)] = plus * value
+                minus = alpha * own[0, slabs - 1, :, cols(j)] - beta
+                value = res[c, slabs - 1, :, cols(j)] + minus * right[c, :, cols(j)]
+                res[c, slabs - 1, :, cols(j)] = value
+                up[c, :, cols(j)] = minus * value
+
+    by_parity(slab_parity(), outer, (space_odd, out_space_odd), (space_even, out_space_even))
+
+    def ends(first, last):
+        first[...] = res[:, :, pl.ds(0, 4), :]
+        last[...] = res[:, :, pl.ds(levels - 4, 4), :]
+
+    by_parity(level_parity(), ends, out_tm_odd, out_tm_even)
+
+
+def descent_kernel(spacing, scale, own, res, space_odd, space_even, part, grad, tm_odd, tm_even, base, rt, sums, res_out, scratch, flow, acc, sem):
     levels = own.shape[2]
     slabs = own.shape[1]
     x = pl.program_id(0)
@@ -237,12 +279,17 @@
     scaled = [w * scale[0] for w in weights]
     border = Borders(scaled)
     rt[...] = part[...]
-    for c in range(3):
-        add_borders(border, rt, low, high, c, 0, levels)
-
+
+    def borders(low, high):
+        for c in range(3):
+            add_borders(border, rt, low, high, c, 0, levels)
+
+    by_parity(level_parity(), borders, tm_odd, tm_even)
     sh = Shifts((levels, LANES))
-    is_first = jnp.where(x == 0, 1.0, 0.0).astype(jnp.float32)
-    is_last = jnp.where(x == slabs - 1, 1.0, 0.0).astype(jnp.float32)
+    odd = slab_parity() == 1
+    lower = jnp.where(x == 0, -1.0, 0.0).astype(jnp.float32)
+    upper = jnp.where(x == slabs - 1, 1.0, 0.0).astype(jnp.float32)
+    from_odd, from_even = jnp.where(odd, upper, lower), jnp.where(odd, lower, upper)
 
     def at(c, dx, j):
         return scratch[c, x + 1 + dx, j % NJ, pl.ds(OWN, levels), :]
@@ -276,7 +323,7 @@
             for k in range(3):
                 diff = grad[c * 3 + k, 0, :, cols(j)]
                 if c == 0:
-                    diff = diff + (is_last * right[k, :, cols(j)] - is_first * left[k, :, cols(j)])
+                    diff = diff + (from_odd * space_odd[k, :, cols(j)] + from_even * space_even[k, :, cols(j)])
                 term = at(k, 0, j) * diff
                 dots = term if dots is None else dots + term
             total = total + alpha * dots
@@ -296,38 +343,42 @@
         pltpu.make_async_copy(res, res_out, sem).wait()
 
 
-def closing_kernel(scale, part, rt, low, high, left, right, partial, base, sums):
+def closing_kernel(scale, part, rt, tm_odd, tm_even, space_odd, space_even, partial, base, sums, inner, outer):
     slabs, levels = part.shape[1], part.shape[2]
     border = Borders([w * scale[0] for w in weights])
 
-    def slab(x, total):
-        for c in range(3):
-            base[c, x] = part[c, x]
-            for j in range(0, NJ, 2):
-                below, above = border.from_low(low, c, x, j), border.from_high(high, c, x, j)
-                for k in range(2):
-                    for row, take in ((0, below[k]), (levels - 4, above[k])):
-                        rows = pl.ds(row, 4)
-                        total = total - take * rt[c, x, rows, cols(j + k)]
-                        base[c, x, rows, cols(j + k)] += step_size * take
-        return total
-
-    inner = lax.fori_loop(0, slabs, slab, jnp.zeros((4, LANES), jnp.float32))
-
-    def edge(sign, message, x):
+    def middle(low, high):
+        def slab(x, total):
+            for c in range(3):
+                base[c, x] = part[c, x]
+                for j in range(0, NJ, 2):
+                    below, above = border.from_low(low, c, x, j), border.from_high(high, c, x, j)
+                    for k in range(2):
+                        for row, take in ((0, below[k]), (levels - 4, above[k])):
+                            rows = pl.ds(row, 4)
+                            total = total - take * rt[c, x, rows, cols(j + k)]
+                            base[c, x, rows, cols(j + k)] += step_size * take
+            return total
+
+        inner[...] = lax.fori_loop(0, slabs, slab, jnp.zeros((4, LANES), jnp.float32))
+
+    by_parity(level_parity(), middle, tm_odd, tm_even)
+
+    def edges(left, right):
         total = jnp.zeros((levels, LANES), jnp.float32)
-        for c in range(3):
-            for j in range(NJ):
-                extra = message[c, :, cols(j)]
-                total = total + extra * rt[c, x, :, cols(j)]
-                base[c, x, :, cols(j)] = base[c, x, :, cols(j)] - (sign * step_size) * extra
-        return sign * total
-
-    outer = edge(1.0, left, 0) + edge(-1.0, right, slabs - 1)
+        for sign, message, x in ((1.0, left, 0), (-1.0, right, slabs - 1)):
+            for c in range(3):
+                for j in range(NJ):
+                    extra = sign * message[c, :, cols(j)]
+                    total = total + extra * rt[c, x, :, cols(j)]
+                    base[c, x, :, cols(j)] = base[c, x, :, cols(j)] - step_size * extra
+        outer[...] = total
+
+    by_parity(slab_parity(), edges, space_odd, space_even)
     lane = lax.broadcasted_iota(jnp.int32, (1, LANES), 1)
     row = jnp.zeros((1, LANES), jnp.float32)
     for k in range(3):
-        value = jnp.sum(partial[k]) if k < 2 else jnp.sum(partial[k] + outer) + jnp.sum(inner)
+        value = jnp.sum(partial[k]) if k < 2 else jnp.sum(partial[k] + outer[...]) + jnp.sum(inner[...])
         row = jnp.where(lane == k, value, row)
     sums[...] = jnp.broadcast_to(row[None], sums.shape)
 
@@ -351,20 +402,21 @@
     pltpu.make_async_copy(buffer, out, sem).wait()
 
 
-def ring(axis):
+def pairing(axis, odd):
     count = lax.axis_size(axis)
-    up = [(i, (i + 1) % count) for i in range(count)]
-    return up, [(j, i) for i, j in up]
-
-
-def exchange(first, last, down, up):
-    tm_up, tm_down = ring(TM)
-    space_up, space_down = ring(SPACE)
-    left = lax.ppermute(up, SPACE, space_up)
-    right = lax.ppermute(down, SPACE, space_down)
-    low = lax.ppermute(last, TM, tm_up)
-    high = lax.ppermute(first, TM, tm_down)
-    return low, high, left, right
+    pairs = []
+    for i in range(odd, count, 2):
+        other = (i + 1) % count
+        pairs += [(i, other), (other, i)]
+    return pairs
+
+
+def send(array, axis, odd):
+    return lax.ppermute(array, axis, pairing(axis, odd))
+
+
+def exchange(tm_odd, tm_even, space_odd, space_even):
+    return (send(tm_odd, TM, 1), send(tm_even, TM, 0), send(space_odd, SPACE, 1), send(space_even, SPACE, 0))
 
 
 def step(velocity, period, wavenumber):
@@ -375,10 +427,6 @@
     spacing = 2.0 * math.pi / NY
     u = jnp.transpose(velocity, (1, 2, 0, 3))
     scale = total_levels / period
-    row_index = jnp.arange(NY, dtype=jnp.float32)
-    profile = jnp.sin(wavenumber[0].astype(jnp.float32) * (2.0 * math.pi / NY) * row_index)
-    forcing = jnp.repeat(profile, NZ).reshape(1, NC)
-
     vmem = pl.BlockSpec(memory_space=pltpu.VMEM)
     smem = pl.BlockSpec(memory_space=pltpu.SMEM)
     hbm = pl.BlockSpec(memory_space=pl.ANY)
@@ -400,7 +448,7 @@
     work = pl.CostEstimate(flops=30_000_000, bytes_accessed=40_000_000, transcendentals=0)
     little = pl.CostEstimate(flops=3_000_000, bytes_accessed=6_000_000, transcendentals=0)
 
-    down, up = pl.pallas_call(
+    space_odd, space_even = pl.pallas_call(
         edges_kernel,
         in_specs=[pl.BlockSpec(memory_space=pltpu.HBM)],
         out_specs=[vmem] * 2,
@@ -410,7 +458,7 @@
         cost_estimate=little,
         name="edges",
     )(u)
-    first, last = pl.pallas_call(
+    tm_odd, tm_even = pl.pallas_call(
         ends_kernel,
         in_specs=[vmem],
         out_specs=[vmem] * 2,
@@ -419,20 +467,20 @@
         cost_estimate=little,
         name="ends",
     )(u)
-    low, high, left, right = exchange(first, last, down, up)
+    halo = exchange(tm_odd, tm_even, space_odd, space_even)
     res_part, rt_part, grad = pl.pallas_call(
-        lambda *refs: residual_kernel(spacing, *refs),
+        lambda *refs: residual_kernel(spacing, total_levels, *refs),
         grid=(slabs,),
-        in_specs=[smem, vmem, vmem],
+        in_specs=[vmem, vmem, vmem],
         out_specs=[slab3, slab3, slab9],
         out_shape=[field, field, shape(9, slabs, levels, NC)],
-        scratch_shapes=[padded],
+        scratch_shapes=[padded, pltpu.VMEM((1, NC), jnp.float32), pltpu.SMEM((4,), jnp.float32)],
         compiler_params=params(16),
         cost_estimate=work,
         name="residual",
-    )(scale, u, forcing)
-
-    res, first, last, down, up = pl.pallas_call(
+    )(period.reshape(1, 1), wavenumber.reshape(1, 1), u)
+
+    res, *messages = pl.pallas_call(
         lambda *refs: joined_kernel(spacing, *refs),
         in_specs=[smem] + [vmem] * 6,
         out_specs=[vmem] * 5,
@@ -440,8 +488,8 @@
         compiler_params=params(18),
         cost_estimate=little,
         name="joined",
-    )(scale, res_part, u, low, high, left, right)
-    res_low, res_high, res_left, res_right = exchange(first, last, down, up)
+    )(scale, res_part, u, *halo)
+    res_halo = exchange(*messages)
     base_part, rt, partial, res_out = pl.pallas_call(
         lambda *refs: descent_kernel(spacing, *refs),
         grid=(slabs,),
@@ -457,16 +505,17 @@
         compiler_params=params(22),
         cost_estimate=work,
         name="descent",
-    )(scale, u, res, left, right, rt_part, grad, low, high)
+    )(scale, u, res, *halo[2:], rt_part, grad, *halo[:2])
     base, sums = pl.pallas_call(
         closing_kernel,
         in_specs=[smem] + [vmem] * 7,
         out_specs=[vmem, vmem],
         out_shape=[field, shape(devices, 1, LANES)],
+        scratch_shapes=[pltpu.VMEM((4, LANES), jnp.float32), pltpu.VMEM((levels, LANES), jnp.float32)],
         compiler_params=params(16),
         cost_estimate=little,
         name="closing",
-    )(scale, base_part, rt, res_low, res_high, res_left, res_right, partial)
+    )(scale, base_part, rt, *res_halo, partial)
 
     gathered = lax.all_to_all(sums, ALL, 0, 0)
     cells = 3.0 * total_levels * grid_first * NY * NZ

time: 75.4 us -> 74.4 us (0.987)
  waiting for transfers between devices: 2.87 us -> 9.53 us
  Pallas kernels: 24.9 us -> 22.2 us
  starting transfers between devices: 18.7 us -> 16 us
  blocking collectives: 24.6 us -> 22.7 us
    ppermute x8, waiting for transfers between devices: 2.87 us -> 9.53 us  [send(): return lax.ppermute(array, axis, pairing(axis, odd))]
    ppermute x8, starting transfers between devices: 18.7 us -> 16 us  [send(): return lax.ppermute(array, axis, pairing(axis, odd))]
    all_to_all x1, blocking collectives: 24.6 us -> 22.7 us  [step(): gathered = lax.all_to_all(sums, ALL, 0, 0)]
    pallas_call x1, Pallas kernels: 9.83 us -> 8.22 us  [step(): pl.pallas_call(lambda *refs: descent_kernel(spacing, *refs), grid=(slabs,...]
    pallas_call x1, Pallas kernels: 2.38 us -> 1.02 us  [step(): pl.pallas_call(lambda *refs: joined_kernel(spacing, *refs), in_specs=[sme...]
  transfers between devices with their start and end apart: 8 -> 8, of which waited for: 2 -> 2; matrix products, arithmetic and copies ran while one was open for 0% -> 0% of each run, Pallas kernels for 24% -> 22%
where the time goes in v5:
time: 74.4 us; the launch traced here: 74.2 us
  blocking collectives  22.7 us (31%)
  Pallas kernels  22.2 us (30%)
  starting transfers between devices  16 us (22%)
  waiting for transfers between devices  9.53 us (13%)
  between operations  2.05 us (3%)
  local copies, waits for them, and re-layouts  1.75 us (2%)
    all_to_all x1, blocking collectives, step(): gathered = lax.all_to_all(sums, ALL, 0, 0)  22.7 us
    ppermute x8, starting transfers between devices, send(): return lax.ppermute(array, axis, pairing(axis, odd))  16 us
    ppermute x8, waiting for transfers between devices, send(): return lax.ppermute(array, axis, pairing(axis, odd))  9.53 us
    pallas_call x1, Pallas kernels, step(): pl.pallas_call(lambda *refs: descent_kernel(spacing, *refs), grid=(slabs,...  8.22 us
    pallas_call x1, Pallas kernels, step(): pl.pallas_call(lambda *refs: residual_kernel(spacing, total_levels, *refs...  6.11 us
    pallas_call x1, Pallas kernels, step(): pl.pallas_call(lambda *refs: update_kernel(cells, *refs), in_specs=[smem,...  2.29 us
    pallas_call x1, Pallas kernels, step(): pl.pallas_call(edges_kernel, in_specs=[pl.BlockSpec(memory_space=pltpu.HB...  2.08 us
    unnamed x4, local copies, waits for them, and re-layouts  1.75 us
  transfers between devices with their start and end apart: 8, of which 2 were waited for; matrix products, arithmetic and copies ran while one was open for 0% of the time, Pallas kernels for 22%

profile of v5, /device:TPU:1, one launch (start us, length us, event | category | flops | bytes accessed | tf_op | source)
XLA Modules:
  0.0 74.2 jit_solution(1621613948448129443)
XLA Ops:
  0.6 0.0 copy-start
  0.6 1.7 %copy-done = f32[16,3,6,2304]{3,0,2,1:T(8,128)S(1)} copy-done((f32[16,3,6,2304]{3,0,2,1:T(8,128)S(1)}, f32[16,3,6,2304]{3,0,2,1:T(8,128)}, u32[]{:S(2)}) %copy-start) | copy-done | bytes 2654232
  2.4 1.1 %ends.1 = (f32[3,6,4,2304]{3,2,1,0:T(4,128)}, f32[3,6,4,2304]{3,2,1,0:T(4,128)}) custom-call(f32[3,6,16,2304]{3,2,1,0:T(8,128)S(1)} %bitcast.10), custom_call_target="tpu_custom_call" | custom-call | flops 3000000 | bytes 6000000 | tf_op jit(solution)/shard_map/ends/pallas_call | solution.py:461
  3.5 3.0 %collective-permute-start = (f32[3,6,4,2304]{3,2,1,0:T(4,128)}, f32[3,6,4,2304]{3,2,1,0:T(4,128)S(1)}, u32[]{:S(2)}, u32[]{:S(2)}) collective-permute-start(f32[3,6,4,2304]{3,2,1,0:T(4,128)} %get-tuple-element.24), channel_id=1, source_target_pairs={{8,16},{16,8},{24,32},{32,24},{40,48},{48,40},{56,64},{64,56},{72,... | collective-permute-start | bytes 1990664 | tf_op jit(solution)/shard_map/ppermute | solution.py:415
  6.5 4.4 %collective-permute-start.1 = (f32[3,6,4,2304]{3,2,1,0:T(4,128)}, f32[3,6,4,2304]{3,2,1,0:T(4,128)S(1)}, u32[]{:S(2)}, u32[]{:S(2)}) collective-permute-start(f32[3,6,4,2304]{3,2,1,0:T(4,128)} %get-tuple-element.25), channel_id=1, source_target_pairs={{0,8},{8,0},{16,24},{24,16},{32,40},{40,32},{48,56},{56,48},{64,72... | collective-permute-start | bytes 1990664 | tf_op jit(solution)/shard_map/ppermute | solution.py:415
  11.0 2.1 %edges.1 = (f32[3,16,2304]{2,1,0:T(8,128)}, f32[3,16,2304]{2,1,0:T(8,128)}) custom-call(f32[3,6,16,2304]{3,2,1,0:T(8,128)} %bitcast.9), custom_call_target="tpu_custom_call" | custom-call | flops 3000000 | bytes 6000000 | tf_op jit(solution)/shard_map/edges/pallas_call | solution.py:451
  13.1 2.8 %collective-permute-start.2 = (f32[3,16,2304]{2,1,0:T(8,128)}, f32[3,16,2304]{2,1,0:T(8,128)S(1)}, u32[]{:S(2)}, u32[]{:S(2)}) collective-permute-start(f32[3,16,2304]{2,1,0:T(8,128)} %get-tuple-element.26), channel_id=1, source_target_pairs={{1,2},{2,1},{3,4},{4,3},{5,6},{6,5},{7,0},{0,7},{9,10},{10,9},{11,... | collective-permute-start | bytes 1327112 | tf_op jit(solution)/shard_map/ppermute | solution.py:415
  17.3 6.1 %residual.1 = (f32[3,6,16,2304]{3,2,1,0:T(8,128)S(1)}, f32[3,6,16,2304]{3,2,1,0:T(8,128)S(1)}, f32[9,6,16,2304]{3,2,1,0:T(8,128)S(1)}) custom-call(f32[1,1]{1,0:T(1,128)} %bitcast.7.refs_0_, s32[1,1]{1,0:T(1,128)} %bitcast.8.refs_1_, f32[3,6,16,2304]{3,2,1,0:T(8,128)S(1)} %bitcast.11), custom_call_target="tpu_custom_call" | custom-call | flops 30000000 | bytes 40000000 | tf_op jit(solution)/shard_map/residual/pallas_call | solution.py:471
  23.4 4.3 %collective-permute-done.2.refs_5_.refs_3_ = f32[3,16,2304]{2,1,0:T(8,128)S(1)} collective-permute-done((f32[3,16,2304]{2,1,0:T(8,128)}, f32[3,16,2304]{2,1,0:T(8,128)S(1)}, u32[]{:S(2)}, u32[]{:S(2)}) %collective-permute-start.2) | collective-permute-done | bytes 442400 | tf_op jit(solution)/shard_map/ppermute | solution.py:415
  27.6 0.0 collective-permute-done.3.refs_6_.refs_4_
  27.6 0.0 collective-permute-done.refs_3_.refs_7_
  27.7 0.0 collective-permute-done.1.refs_4_.refs_8_
  27.7 1.0 %joined.1 = (f32[3,6,16,2304]{3,2,1,0:T(8,128)S(1)}, f32[3,6,4,2304]{3,2,1,0:T(4,128)S(1)}, f32[3,6,4,2304]{3,2,1,0:T(4,128)S(1)}, f32[3,16,2304]{2,1,0:T(8,128)S(1)}, f32[3,16,2304]{2,1,0:T(8,128)S(1)}) custom-call(f32[1]{0:T(128)S(6)} %div.3.refs_0_.scale, f32[3,6,16,2304]{3,2,1,0:T(8,128)S(1)} %get-tuple-element.23.refs_1_, ...), custom_call_target="tpu_custom_call" | custom-call | flops 3000000 | bytes 6000000 | tf_op jit(solution)/shard_map/joined/pallas_call | solution.py:483
  28.7 0.1 collective-permute-start.4
  28.8 4.8 %collective-permute-start.5 = (f32[3,6,4,2304]{3,2,1,0:T(4,128)S(1)}, f32[3,6,4,2304]{3,2,1,0:T(4,128)S(1)}, u32[]{:S(2)}, u32[]{:S(2)}) collective-permute-start(f32[3,6,4,2304]{3,2,1,0:T(4,128)S(1)} %get-tuple-element.34), channel_id=1, source_target_pairs={{0,8},{8,0},{16,24},{24,16},{32,40},{40,32},{48,56},{56,48},{64,72... | collective-permute-start | bytes 1990664 | tf_op jit(solution)/shard_map/ppermute | solution.py:415
  33.6 0.8 %collective-permute-start.6 = (f32[3,16,2304]{2,1,0:T(8,128)S(1)}, f32[3,16,2304]{2,1,0:T(8,128)S(1)}, u32[]{:S(2)}, u32[]{:S(2)}) collective-permute-start(f32[3,16,2304]{2,1,0:T(8,128)S(1)} %get-tuple-element.35), channel_id=1, source_target_pairs={{1,2},{2,1},{3,4},{4,3},{5,6},{6,5},{7,0},{0,7},{9,10},{10,9},{11,... | collective-permute-start | bytes 1327112 | tf_op jit(solution)/shard_map/ppermute | solution.py:415
  34.4 0.0 collective-permute-start.7
  34.4 8.2 %descent.1 = (f32[3,6,16,2304]{3,2,1,0:T(8,128)S(1)}, f32[3,6,16,2304]{3,2,1,0:T(8,128)S(1)}, f32[3,16,128]{2,1,0:T(8,128)S(1)}, f32[3,6,16,2304]{3,2,1,0:T(8,128)}) custom-call(f32[1]{0:T(128)S(6)} %div.3.refs_0_.scale, f32[3,6,16,2304]{3,2,1,0:T(8,128)S(1)} %bitcast.13, f32[3,6,16,2304]{3,2,1,0:T(8,128)S(1)} %get-tuple-element.28.refs_2_, ...), custom_call_target="tpu_custom_call" | custom-call | flops 30000000 | bytes 40000000 | tf_op jit(solution)/shard_map/descent/pallas_call | solution.py:493
  42.6 5.2 %collective-permute-done.6.space_odd = f32[3,16,2304]{2,1,0:T(8,128)S(1)} collective-permute-done((f32[3,16,2304]{2,1,0:T(8,128)S(1)}, f32[3,16,2304]{2,1,0:T(8,128)S(1)}, u32[]{:S(2)}, u32[]{:S(2)}) %collective-permute-start.6) | collective-permute-done | bytes 442400 | tf_op jit(solution)/shard_map/ppermute | solution.py:415
  47.9 0.0 collective-permute-done.4.tm_odd
  47.9 0.0 collective-permute-done.5.tm_even
  47.9 1.3 %closing.1 = (f32[3,6,16,2304]{3,2,1,0:T(8,128)S(1)}, f32[128,1,128]{2,1,0:T(1,128)S(1)}) custom-call(f32[1]{0:T(128)S(6)} %div.3.refs_0_.scale, f32[3,6,16,2304]{3,2,1,0:T(8,128)S(1)} %get-tuple-element.31.part, f32[3,6,16,2304]{3,2,1,0:T(8,128)S(1)} %get-tuple-element.32.rt.refs_3_, f32[3,6,4,2304]{3,2,1,0:T(4,128)S(1)} %collective-permute-done.4.tm_odd, ...), custom_call_target="tpu_custom_call" | custom-call | flops 3000000 | bytes 6000000 | tf_op jit(solution)/shard_map/closing/pallas_call | solution.py:509
  49.2 22.7 %all_to_all.5.refs_1_ = f32[128,1,128]{2,1,0:T(1,128)S(1)} all-to-all(f32[128,1,128]{2,1,0:T(1,128)S(1)} %get-tuple-element.38), channel_id=1, replica_groups=mesh['tm_0'=2,'tm_1'=4,'tm_2'=2,'space_0'=2,'space_1'=4] {'tm_0','tm_1',..., dimensions={0} | all-to-all | bytes 131072 | tf_op jit(solution)/shard_map/all_to_all | solution.py:520
  71.9 2.3 %update.1 = (f32[3,6,16,2304]{3,2,1,0:T(8,128)}, f32[1,128]{1,0:T(1,128)}) custom-call(f32[1]{0:T(128)} %copy.6.refs_0_, f32[128,1,128]{2,1,0:T(1,128)S(1)} %all_to_all.5.refs_1_, f32[3,6,16,2304]{3,2,1,0:T(8,128)S(1)} %get-tuple-element.39.refs_2_, f32[3,6,16,2304]{3,2,1,0:T(8,128)S(1)} %get-tuple-element.32.rt.refs_3_), custom_call_target="tpu_custom_call" | custom-call | flops 3000000 | bytes 6000000 | tf_op jit(solution)/shard_map/update/pallas_call | solution.py:522
  (4 shorter events, 0.0 us)
Async XLA Ops:
  0.6 1.8 %copy-start = (f32[16,3,6,2304]{3,0,2,1:T(8,128)S(1)}, f32[16,3,6,2304]{3,0,2,1:T(8,128)}, u32[]{:S(2)}) copy-start(f32[16,3,6,2304]{3,0,2,1:T(8,128)} %param.3) | copy-start | bytes 7962628
  2.4 14.9 %copy-start.1 = (f32[16,3,6,2304]{3,0,2,1:T(8,128)S(1)}, f32[16,3,6,2304]{3,0,2,1:T(8,128)}, u32[]{:S(2)}) copy-start(f32[16,3,6,2304]{3,0,2,1:T(8,128)} %param.3) | copy-start | bytes 7962628
  3.5 24.1 %collective-permute-start = (f32[3,6,4,2304]{3,2,1,0:T(4,128)}, f32[3,6,4,2304]{3,2,1,0:T(4,128)S(1)}, u32[]{:S(2)}, u32[]{:S(2)}) collective-permute-start(f32[3,6,4,2304]{3,2,1,0:T(4,128)} %get-tuple-element.24), channel_id=1, source_target_pairs={{8,16},{16,8},{24,32},{32,24},{40,48},{48,40},{56,64},{64,56},{72,... | collective-permute-start | bytes 1990664 | tf_op jit(solution)/shard_map/ppermute | solution.py:415
  6.5 21.1 %collective-permute-start.1 = (f32[3,6,4,2304]{3,2,1,0:T(4,128)}, f32[3,6,4,2304]{3,2,1,0:T(4,128)S(1)}, u32[]{:S(2)}, u32[]{:S(2)}) collective-permute-start(f32[3,6,4,2304]{3,2,1,0:T(4,128)} %get-tuple-element.25), channel_id=1, source_target_pairs={{0,8},{8,0},{16,24},{24,16},{32,40},{40,32},{48,56},{56,48},{64,72... | collective-permute-start | bytes 1990664 | tf_op jit(solution)/shard_map/ppermute | solution.py:415
  13.1 14.6 %collective-permute-start.2 = (f32[3,16,2304]{2,1,0:T(8,128)}, f32[3,16,2304]{2,1,0:T(8,128)S(1)}, u32[]{:S(2)}, u32[]{:S(2)}) collective-permute-start(f32[3,16,2304]{2,1,0:T(8,128)} %get-tuple-element.26), channel_id=1, source_target_pairs={{1,2},{2,1},{3,4},{4,3},{5,6},{6,5},{7,0},{0,7},{9,10},{10,9},{11,... | collective-permute-start | bytes 1327112 | tf_op jit(solution)/shard_map/ppermute | solution.py:415
  15.9 11.7 %collective-permute-start.3 = (f32[3,16,2304]{2,1,0:T(8,128)}, f32[3,16,2304]{2,1,0:T(8,128)S(1)}, u32[]{:S(2)}, u32[]{:S(2)}) collective-permute-start(f32[3,16,2304]{2,1,0:T(8,128)} %get-tuple-element.27), channel_id=1, source_target_pairs={{0,1},{1,0},{2,3},{3,2},{4,5},{5,4},{6,7},{7,6},{8,9},{9,8},{10,11... | collective-permute-start | bytes 1327112 | tf_op jit(solution)/shard_map/ppermute | solution.py:415
  28.7 19.2 %collective-permute-start.4 = (f32[3,6,4,2304]{3,2,1,0:T(4,128)S(1)}, f32[3,6,4,2304]{3,2,1,0:T(4,128)S(1)}, u32[]{:S(2)}, u32[]{:S(2)}) collective-permute-start(f32[3,6,4,2304]{3,2,1,0:T(4,128)S(1)} %get-tuple-element.33), channel_id=1, source_target_pairs={{8,16},{16,8},{24,32},{32,24},{40,48},{48,40},{56,64},{64,56},{72,... | collective-permute-start | bytes 1990664 | tf_op jit(solution)/shard_map/ppermute | solution.py:415
  28.8 19.1 %collective-permute-start.5 = (f32[3,6,4,2304]{3,2,1,0:T(4,128)S(1)}, f32[3,6,4,2304]{3,2,1,0:T(4,128)S(1)}, u32[]{:S(2)}, u32[]{:S(2)}) collective-permute-start(f32[3,6,4,2304]{3,2,1,0:T(4,128)S(1)} %get-tuple-element.34), channel_id=1, source_target_pairs={{0,8},{8,0},{16,24},{24,16},{32,40},{40,32},{48,56},{56,48},{64,72... | collective-permute-start | bytes 1990664 | tf_op jit(solution)/shard_map/ppermute | solution.py:415
  33.6 14.3 %collective-permute-start.6 = (f32[3,16,2304]{2,1,0:T(8,128)S(1)}, f32[3,16,2304]{2,1,0:T(8,128)S(1)}, u32[]{:S(2)}, u32[]{:S(2)}) collective-permute-start(f32[3,16,2304]{2,1,0:T(8,128)S(1)} %get-tuple-element.35), channel_id=1, source_target_pairs={{1,2},{2,1},{3,4},{4,3},{5,6},{6,5},{7,0},{0,7},{9,10},{10,9},{11,... | collective-permute-start | bytes 1327112 | tf_op jit(solution)/shard_map/ppermute | solution.py:415
  34.4 13.5 %collective-permute-start.7 = (f32[3,16,2304]{2,1,0:T(8,128)S(1)}, f32[3,16,2304]{2,1,0:T(8,128)S(1)}, u32[]{:S(2)}, u32[]{:S(2)}) collective-permute-start(f32[3,16,2304]{2,1,0:T(8,128)S(1)} %get-tuple-element.36), channel_id=1, source_target_pairs={{0,1},{1,0},{2,3},{3,2},{4,5},{5,4},{6,7},{7,6},{8,9},{9,8},{10,11... | collective-permute-start | bytes 1327112 | tf_op jit(solution)/shard_map/ppermute | solution.py:415
